TPU v7x, 32 devices: a whole 2x2x4 slice. The times are simulated.
32 devices in a mesh: dp: 8 (over z, y), fsdp: 4 (over x, core).
Axes of the slice: x: 2, y: 2, z: 4, core: 2. Of those that a mesh axis runs over, the one named last changes fastest.
Arguments:
- inputs: bfloat16 [28928, 768], P(('dp', 'fsdp')), may hold values from -6 to 6
- skip_input: bfloat16 [28928, 768], P(('dp', 'fsdp')), may hold values from -6 to 6
- cotangent: bfloat16 [28928, 768], P(('dp', 'fsdp')), may hold values from -6 to 6
- row_item: int32 [28928], P(('dp', 'fsdp')), may hold values from 0 to 2, as said below
- row_live: int32 [28928], P(('dp', 'fsdp')), may hold values from 0 to 1, as said below
- skip_weight: bfloat16 [768, 1536], P('fsdp'), may hold values from -0.15625 to 0.15625
- skip_bias: bfloat16 [768], P('fsdp'), may hold values from -1.5 to 1.5
- attn_gain: bfloat16 [768], P('fsdp'), may hold values from 0.099609375 to 1.8984375
- attn_shift: bfloat16 [768], P('fsdp'), may hold values from -1.5 to 1.5
- qkv_weight: bfloat16 [2304, 768], P('fsdp'), may hold values from -0.21875 to 0.21875
- proj_weight: bfloat16 [768, 768], P('fsdp'), may hold values from -3 to 3
- proj_bias: bfloat16 [768], P('fsdp'), may hold values from -1.5 to 1.5
- mlp_gain: bfloat16 [768], P('fsdp'), may hold values from 0.099609375 to 1.8984375
- mlp_shift: bfloat16 [768], P('fsdp'), may hold values from -1.5 to 1.5
- hidden_weight: bfloat16 [3072, 768], P('fsdp'), may hold values from -0.21875 to 0.21875
- hidden_bias: bfloat16 [3072], P('fsdp'), may hold values from -2.5 to 2.5
- output_weight: bfloat16 [768, 3072], P('fsdp'), may hold values from -0.109375 to 0.109375
- output_bias: bfloat16 [768], P('fsdp'), may hold values from -1.5 to 1.5
Outputs:
- output: bfloat16 [28928, 768], P(('dp', 'fsdp'))
- grad_input: bfloat16 [28928, 768], P(('dp', 'fsdp'))
- grad_skip: bfloat16 [28928, 768], P(('dp', 'fsdp'))
- grad_skip_weight: float32 [768, 1536], P('fsdp')
- grad_skip_bias: float32 [768], P('fsdp')
- grad_attn_gain: float32 [768], P('fsdp')
- grad_attn_shift: float32 [768], P('fsdp')
- grad_qkv_weight: float32 [2304, 768], P('fsdp')
- grad_proj_weight: float32 [768, 768], P('fsdp')
- grad_proj_bias: float32 [768], P('fsdp')
- grad_mlp_gain: float32 [768], P('fsdp')
- grad_mlp_shift: float32 [768], P('fsdp')
- grad_hidden_weight: float32 [3072, 768], P('fsdp')
- grad_hidden_bias: float32 [3072], P('fsdp')
- grad_output_weight: float32 [768, 3072], P('fsdp')
- grad_output_bias: float32 [768], P('fsdp')
Inputs may be any that keep to these rules, and one draw needn't show every extreme that they name: `row_item`: each device's 904 rows hold, from its first row, either one item of 901 rows numbered 0, or 3 items of 257 rows numbered 0 to 2 in order; rows after the last item carry the last item's number. About a third of the devices hold one long item. `row_live`: 1 on the rows of items, 0 on the rows after them.
All inputs are finite; a program needn't handle non-finite values.
Results may differ from a plain program's by a relative error of at most 0.015.
Values may be sent and summed in bfloat16 or wider, within the bound.
No kernel may reach another device: no remote copies, remote signals or barrier semaphores. Data moves between devices by JAX's collectives and lax.ppermute only.
A program may use at most 192 MiB of HBM per device.

v0:
```python
import jax
import jax.numpy as jnp
from jax import lax
from jax.sharding import PartitionSpec as P

H = 12


epsilon = 1e-05
masked_score = -1e30


def layer_norm(stream, norm_gain, norm_shift):
    row_mean = jnp.mean(stream, axis=1, keepdims=True)
    centred = stream - row_mean
    row_var = jnp.mean(centred * centred, axis=1, keepdims=True)
    return centred * lax.rsqrt(row_var + epsilon) * norm_gain + norm_shift


def times_t(left, weight):
    return lax.dot_general(
        left, weight, (((1,), (1,)), ((), ())), preferred_element_type=jnp.float32
    )


def times_n(left, weight):
    return jnp.dot(left, weight, preferred_element_type=jnp.float32)


def rows_outer(grad_rows, left):
    return lax.dot_general(
        grad_rows, left, (((0,), (0,)), ((), ())), preferred_element_type=jnp.float32
    )


def column_sums(grad_rows):
    return jnp.sum(grad_rows.astype(jnp.float32), axis=0)


def shards(
    inputs,
    skip_input,
    cotangent,
    row_item,
    row_live,
    skip_weight,
    skip_bias,
    attn_gain,
    attn_shift,
    qkv_weight,
    proj_weight,
    proj_bias,
    mlp_gain,
    mlp_shift,
    hidden_weight,
    hidden_bias,
    output_weight,
    output_bias,
):
    row_count, model_width = inputs.shape
    head_size = model_width // H
    score_scale = head_size ** (-0.5)
    gathered = (
        lax.all_gather(skip_weight, "fsdp", axis=0, tiled=True),
        lax.all_gather(qkv_weight, "fsdp", axis=0, tiled=True),
        lax.all_gather(proj_weight, "fsdp", axis=0, tiled=True),
        lax.all_gather(skip_bias, "fsdp", axis=0, tiled=True),
        lax.all_gather(attn_gain, "fsdp", axis=0, tiled=True),
        lax.all_gather(attn_shift, "fsdp", axis=0, tiled=True),
        lax.all_gather(proj_bias, "fsdp", axis=0, tiled=True),
        lax.all_gather(mlp_gain, "fsdp", axis=0, tiled=True),
        lax.all_gather(mlp_shift, "fsdp", axis=0, tiled=True),
        lax.all_gather(hidden_bias, "fsdp", axis=0, tiled=True),
        lax.all_gather(output_bias, "fsdp", axis=0, tiled=True),
    )
    skip_full, qkv_full, proj_full = (gathered[0], gathered[1], gathered[2])
    (
        skip_vec,
        gain_first,
        shift_first,
        proj_vec,
        gain_second,
        shift_second,
        hidden_vec,
        output_vec,
    ) = [member.astype(jnp.float32) for member in gathered[3:]]
    joined = jnp.concatenate([inputs, skip_input], axis=1)
    stream_a = times_t(joined, skip_full) + skip_vec
    normed_a = layer_norm(stream_a, gain_first, shift_first).astype(jnp.bfloat16)
    packed = times_t(normed_a, qkv_full).astype(jnp.bfloat16)
    allowed = (row_item[:, None] == row_item[None, :]) & (row_live[None, :] == 1)

    def head_slices(head_index):
        query_head = lax.dynamic_slice_in_dim(packed, head_index * head_size, head_size, 1)
        key_head = lax.dynamic_slice_in_dim(
            packed, model_width + head_index * head_size, head_size, 1
        )
        value_head = lax.dynamic_slice_in_dim(
            packed, 2 * model_width + head_index * head_size, head_size, 1
        )
        scores = jnp.where(allowed, times_t(query_head, key_head) * score_scale, masked_score)
        return (query_head, key_head, value_head, scores)

    def head_forward(head_index, state):
        merged, log_totals = state
        query_head, key_head, value_head, scores = head_slices(head_index)
        row_max = jnp.max(scores, axis=1, keepdims=True)
        exp_scores = jnp.exp(scores - row_max)
        row_total = jnp.sum(exp_scores, axis=1, keepdims=True)
        attn_probs = (exp_scores / row_total).astype(jnp.bfloat16)
        head_out = times_n(attn_probs, value_head)
        merged = lax.dynamic_update_slice_in_dim(merged, head_out, head_index * head_size, 1)
        log_totals = lax.dynamic_update_slice_in_dim(
            log_totals, row_max + jnp.log(row_total), head_index, 1
        )
        return (merged, log_totals)

    merged, log_totals = lax.fori_loop(
        0,
        H,
        head_forward,
        (jnp.zeros((row_count, model_width), jnp.float32), jnp.zeros((row_count, H), jnp.float32)),
    )
    attended = merged.astype(jnp.bfloat16)
    stream_b = stream_a + times_t(attended, proj_full) + proj_vec
    normed_b = layer_norm(stream_b, gain_second, shift_second).astype(jnp.bfloat16)
    hidden_full, output_full = (
        lax.all_gather(hidden_weight, "fsdp", axis=0, tiled=True),
        lax.all_gather(output_weight, "fsdp", axis=0, tiled=True),
    )
    pre_act = times_t(normed_b, hidden_full) + hidden_vec
    activation = jax.nn.gelu(pre_act, approximate=False).astype(jnp.bfloat16)
    output = (stream_b + times_t(activation, output_full) + output_vec).astype(jnp.bfloat16)
    hidden_back, output_back = (hidden_full, output_full)
    grad_out = cotangent * row_live[:, None].astype(jnp.bfloat16)
    grad_output_weight = rows_outer(grad_out, activation)
    grad_output_bias = column_sums(grad_out)
    grad_act = times_n(grad_out, output_back)
    gelu_value, gelu_back = jax.vjp(lambda value: jax.nn.gelu(value, approximate=False), pre_act)
    grad_pre = gelu_back(grad_act)[0].astype(jnp.bfloat16)
    grad_hidden_weight = rows_outer(grad_pre, normed_b)
    grad_hidden_bias = column_sums(grad_pre)
    grad_normed_b = times_n(grad_pre, hidden_back)
    norm_value, norm_back = jax.vjp(layer_norm, stream_b, gain_second, shift_second)
    grad_part_b, grad_mlp_gain, grad_mlp_shift = norm_back(grad_normed_b)
    grad_stream_b = grad_out.astype(jnp.float32) + grad_part_b
    mlp_shards = (
        lax.psum_scatter(
            grad_hidden_weight.astype(jnp.bfloat16), "fsdp", scatter_dimension=0, tiled=True
        ).astype(jnp.float32),
        lax.psum_scatter(
            grad_hidden_bias.astype(jnp.bfloat16), "fsdp", scatter_dimension=0, tiled=True
        ).astype(jnp.float32),
        lax.psum_scatter(
            grad_output_weight.astype(jnp.bfloat16), "fsdp", scatter_dimension=0, tiled=True
        ).astype(jnp.float32),
        lax.psum_scatter(
            grad_output_bias.astype(jnp.bfloat16), "fsdp", scatter_dimension=0, tiled=True
        ).astype(jnp.float32),
        lax.psum_scatter(
            grad_mlp_gain.astype(jnp.bfloat16), "fsdp", scatter_dimension=0, tiled=True
        ).astype(jnp.float32),
        lax.psum_scatter(
            grad_mlp_shift.astype(jnp.bfloat16), "fsdp", scatter_dimension=0, tiled=True
        ).astype(jnp.float32),
    )
    skip_back, qkv_back, proj_back = (skip_full, qkv_full, proj_full)
    grad_branch = grad_stream_b.astype(jnp.bfloat16)
    grad_proj_weight = rows_outer(grad_branch, attended)
    grad_proj_bias = column_sums(grad_branch)
    grad_attended = times_n(grad_branch, proj_back).astype(jnp.bfloat16)

    def head_backward(head_index, grad_packed):
        query_head, key_head, value_head, scores = head_slices(head_index)
        log_head = lax.dynamic_slice_in_dim(log_totals, head_index, 1, 1)
        grad_head = lax.dynamic_slice_in_dim(grad_attended, head_index * head_size, head_size, 1)
        probs_full = jnp.exp(scores - log_head)
        grad_value = rows_outer(probs_full.astype(jnp.bfloat16), grad_head)
        grad_probs = times_t(grad_head, value_head)
        row_delta = jnp.sum(probs_full * grad_probs, axis=1, keepdims=True)
        grad_scores = (probs_full * (grad_probs - row_delta)).astype(jnp.bfloat16)
        grad_query = times_n(grad_scores, key_head) * score_scale
        grad_key = rows_outer(grad_scores, query_head) * score_scale
        grad_packed = lax.dynamic_update_slice_in_dim(
            grad_packed, grad_query, head_index * head_size, 1
        )
        grad_packed = lax.dynamic_update_slice_in_dim(
            grad_packed, grad_key, model_width + head_index * head_size, 1
        )
        grad_packed = lax.dynamic_update_slice_in_dim(
            grad_packed, grad_value, 2 * model_width + head_index * head_size, 1
        )
        return grad_packed

    grad_qkv = lax.fori_loop(
        0, H, head_backward, jnp.zeros((row_count, 3 * model_width), jnp.float32)
    ).astype(jnp.bfloat16)
    grad_qkv_weight = rows_outer(grad_qkv, normed_a)
    grad_normed_a = times_n(grad_qkv, qkv_back)
    first_value, first_back = jax.vjp(layer_norm, stream_a, gain_first, shift_first)
    grad_part_a, grad_attn_gain, grad_attn_shift = first_back(grad_normed_a)
    grad_rounded = (grad_stream_b + grad_part_a).astype(jnp.bfloat16)
    grad_skip_weight = rows_outer(grad_rounded, joined)
    grad_skip_bias = column_sums(grad_rounded)
    grad_joined = times_n(grad_rounded, skip_back)
    grad_input = grad_joined[:, :model_width].astype(jnp.bfloat16)
    grad_skip = grad_joined[:, model_width:].astype(jnp.bfloat16)
    attn_shards = (
        lax.psum_scatter(
            grad_skip_weight.astype(jnp.bfloat16), "fsdp", scatter_dimension=0, tiled=True
        ).astype(jnp.float32),
        lax.psum_scatter(
            grad_skip_bias.astype(jnp.bfloat16), "fsdp", scatter_dimension=0, tiled=True
        ).astype(jnp.float32),
        lax.psum_scatter(
            grad_attn_gain.astype(jnp.bfloat16), "fsdp", scatter_dimension=0, tiled=True
        ).astype(jnp.float32),
        lax.psum_scatter(
            grad_attn_shift.astype(jnp.bfloat16), "fsdp", scatter_dimension=0, tiled=True
        ).astype(jnp.float32),
        lax.psum_scatter(
            grad_qkv_weight.astype(jnp.bfloat16), "fsdp", scatter_dimension=0, tiled=True
        ).astype(jnp.float32),
        lax.psum_scatter(
            grad_proj_weight.astype(jnp.bfloat16), "fsdp", scatter_dimension=0, tiled=True
        ).astype(jnp.float32),
        lax.psum_scatter(
            grad_proj_bias.astype(jnp.bfloat16), "fsdp", scatter_dimension=0, tiled=True
        ).astype(jnp.float32),
    )
    summed = lax.psum(
        (
            mlp_shards[0],
            mlp_shards[1],
            mlp_shards[2],
            mlp_shards[3],
            mlp_shards[4],
            mlp_shards[5],
            attn_shards[0],
            attn_shards[1],
            attn_shards[2],
            attn_shards[3],
            attn_shards[4],
            attn_shards[5],
            attn_shards[6],
        ),
        "dp",
    )
    mlp_shards = summed[:6]
    attn_shards = summed[6:]
    device_total = lax.axis_size("dp") * lax.axis_size("fsdp")
    mlp_final = [member / device_total for member in mlp_shards]
    attn_final = [member / device_total for member in attn_shards]
    return (
        output,
        grad_input,
        grad_skip,
        attn_final[0],
        attn_final[1],
        attn_final[2],
        attn_final[3],
        attn_final[4],
        attn_final[5],
        attn_final[6],
        mlp_final[4],
        mlp_final[5],
        mlp_final[0],
        mlp_final[1],
        mlp_final[2],
        mlp_final[3],
    )


def solution(mesh):
    in_specs = (
        P(("dp", "fsdp"), None),
        P(("dp", "fsdp"), None),
        P(("dp", "fsdp"), None),
        P(("dp", "fsdp")),
        P(("dp", "fsdp")),
        P("fsdp", None),
        P("fsdp"),
        P("fsdp"),
        P("fsdp"),
        P("fsdp", None),
        P("fsdp", None),
        P("fsdp"),
        P("fsdp"),
        P("fsdp"),
        P("fsdp", None),
        P("fsdp"),
        P("fsdp", None),
        P("fsdp"),
    )
    out_specs = (
        P(("dp", "fsdp"), None),
        P(("dp", "fsdp"), None),
        P(("dp", "fsdp"), None),
        P("fsdp", None),
        P("fsdp"),
        P("fsdp"),
        P("fsdp"),
        P("fsdp", None),
        P("fsdp", None),
        P("fsdp"),
        P("fsdp"),
        P("fsdp"),
        P("fsdp", None),
        P("fsdp"),
        P("fsdp", None),
        P("fsdp"),
    )
    return jax.shard_map(shards, mesh=mesh, in_specs=in_specs, out_specs=out_specs, check_vma=False)
```

profile of v0, /device:TPU:0, one launch (start us, length us, event | category | flops | bytes accessed | tf_op | source)
XLA Modules:
  0.0 987.2 jit_solution(3834545871091344442)
XLA Ops:
  13.5 13.5 %all-reduce.17 = (bf16[768]{0:T(1024)(128)(2,1)S(1)}, bf16[768]{0:T(1024)(128)(2,1)S(1)}, bf16[768]{0:T(1024)(128)(2,1)S(1)}, bf16[768]{0:T(1024)(128)(2,1)S(1)}...) all-reduce(bf16[768]{0:T(1024)(128)(2,1)S(1)} %dynamic-update-slice, ...), channel_id=1, replica_groups=mesh['dp'=8,'fsdp'=4] {'fsdp'}, use_global_device_ids=true, to_apply=%add.3 | all-reduce | flops 4608 | bytes 18432
  28.2 5.4 all-gather
  36.6 5.0 add_reduce_fusion
  43.2 25.8 %all-gather.9.cloned.1.call-done = bf16[2304,768]{1,0:T(8,128)(2,1)} async-done(((bf16[576,768]{1,0:T(8,128)(2,1)}), bf16[2304,768]{1,0:T(8,128)(2,1)}) %all-gather.9.cloned.1.call-update) | async-done | bytes 3538960 | tf_op jit(solution)/shard_map/all_gather | solution.py:65
  69.0 7.9 convolution_convert_fusion
  78.3 100.2 %while.34 = (s32[]{:T(128)}, bf16[904,768]{0,1:T(8,128)(2,1)}, f32[904,12]{0,1:T(8,128)S(1)}, bf16[904,2304]{1,0:T(8,128)(2,1)}, s32[904]{0:T(1024)S(1)}, /*inde...) while((s32[]{:T(128)}, bf16[904,768]{0,1:T(8,128)(2,1)}, ...), condition=%wide.region_5.6_spmd.clone, body=%wide.region_2.5_spmd.clone.sunk | while | flops 217378560 | bytes 24318088 | solution.py:118
  133.0 3.9 fusion.110
  178.4 4.2 fusion.63
  183.1 33.1 %multiply_convert_fusion.1 = (bf16[904,3072]{1,0:T(8,128)(2,1)}, f32[904,3072]{1,0:T(8,128)}, f32[904,3072]{1,0:T(8,128)}) fusion(f32[3072]{0:T(1024)S(1)} %bitcast.41, bf16[3072,768]{1,0:T(8,128)(2,1)} %all-gather.13.cloned.1.call-done, f32[904,768]{1,0:T(8,128)S(1)} %get-tuple-element.424, f32[768]{0:T(1024)S(1)} %convert_element_type.178, ...), kind=kOutput, calls=%fused_computation.41 | convolution fusion | flops 4452366336 | bytes 35292224 | tf_op jit(solution)/shard_map/dot_general | solution.py:21
  216.2 14.6 %fusion.64 = (bf16[3072]{0:T(1024)(128)(2,1)S(1)}, bf16[904,3072]{1,0:T(8,128)(2,1)S(1)}) fusion(f32[904,3072]{1,0:T(8,128)} %get-tuple-element.411, bf16[768,3072]{1,0:T(8,128)(2,1)} %all-gather.15.cloned.1.call-done, bf16[904,768]{1,0:T(8,128)(2,1)} %param.24, bf16[904]{0:T(1024)(128)(2,1)S(1)} %convert_element_type.184, ...), kind=kOutput, calls=%fused_computation.134 | convolution fusion | flops 4310731776 | bytes 33898256 | tf_op jit(solution)/shard_map/dot_general | solution.py:27
  230.9 4.9 multiply_reduce_fusion.1
  242.9 4.0 convolution_convert_fusion.6
  249.8 187.8 %while.35 = (s32[]{:T(128)}, bf16[904,2304]{0,1:T(8,128)(2,1)}, bf16[904,2304]{1,0:T(8,128)(2,1)}, f32[904,12]{0,1:T(8,128)S(1)}, bf16[904,768]{1,0:T(8,128)(2,1...) while((s32[]{:T(128)}, bf16[904,2304]{0,1:T(8,128)(2,1)}, ...), condition=%wide.region_12.13_spmd.clone, body=%wide.region_10.0_spmd.clone.sunk | while | flops 532122432 | bytes 40460396 | solution.py:195
  250.0 3.7 fusion.119
  253.7 4.1 multiply_reduce_fusion.9
  265.7 3.7 fusion.119
  269.3 4.1 multiply_reduce_fusion.9
  281.3 3.6 fusion.119
  285.0 4.1 multiply_reduce_fusion.9
  296.9 3.7 fusion.119
  300.6 4.1 multiply_reduce_fusion.9
  312.5 3.7 fusion.119
  316.2 4.1 multiply_reduce_fusion.9
  328.2 3.7 fusion.119
  331.8 4.1 multiply_reduce_fusion.9
  343.8 3.6 fusion.119
  347.4 4.1 multiply_reduce_fusion.9
  359.4 3.6 fusion.119
  363.1 4.1 multiply_reduce_fusion.9
  375.1 3.7 fusion.119
  378.7 4.1 multiply_reduce_fusion.9
  390.7 3.6 fusion.119
  394.3 4.1 multiply_reduce_fusion.9
  406.3 3.6 fusion.119
  409.9 4.1 multiply_reduce_fusion.9
  425.6 4.1 multiply_reduce_fusion.9
  437.7 8.7 multiply_reduce_fusion.2
  450.0 5.8 convolution_convert_fusion.5
  455.9 8.7 convolution_convert_fusion.3
  466.3 10.6 %convolution_convert_fusion.2 = bf16[3072,768]{1,0:T(8,128)(2,1)} fusion(bf16[904,3072]{1,0:T(8,128)(2,1)} %copy-done.47, f32[904,768]{1,0:T(8,128)S(1)} %copy-done.3, f32[768]{0:T(1024)S(1)} %convert_element_type.178, f32[768]{0:T(1024)S(1)} %convert_element_type.177, f32[904]{0:T(1024)S(1)} %fusion.52, f32[904]{0:T(1024)S(1)} %broadcast_multiply_fusion.6), kind=kOutput, calls=%fused_computation.57 | convolution fusion | flops 4271437824 | bytes 13063232 | tf_op jit(solution)/shard_map/dot_general | solution.py:31
  477.0 9.8 convolution_convert_fusion.1
  488.4 11.1 %all-reduce.16 = (bf16[768]{0:T(1024)(128)(2,1)S(1)}, bf16[768]{0:T(1024)(128)(2,1)S(1)}, bf16[768]{0:T(1024)(128)(2,1)S(1)}, bf16[768]{0:T(1024)(128)(2,1)S(1)}...) all-reduce(bf16[768]{0:T(1024)(128)(2,1)S(1)} %dynamic-update-slice, ...), channel_id=1, replica_groups=mesh['dp'=8,'fsdp'=4] {'fsdp'}, use_global_device_ids=true, to_apply=%add.6 | all-reduce | flops 9216 | bytes 36864
  501.6 4.4 convolution_convert_fusion.4
  507.8 10.7 %add_convert_fusion.2 = bf16[904,768]{1,0:T(8,128)(2,1)} fusion(f32[904,768]{1,0:T(8,128)S(1)} %copy-done.3, bf16[904,3072]{1,0:T(8,128)(2,1)} %get-tuple-element.410, bf16[768,3072]{1,0:T(8,128)(2,1)} %all-gather.15.cloned.1.call-done, f32[768]{0:T(1024)S(1)} %convert_element_type.182), kind=kOutput, calls=%fused_computation.69 | convolution fusion | flops 4267689984 | bytes 14441472 | tf_op jit(solution)/shard_map/dot_general | solution.py:21
  518.5 23.7 %reduce-scatter.8.cloned.1.call-done = bf16[576,768]{1,0:T(8,128)(2,1)} async-done(((bf16[2304,768]{1,0:T(8,128)(2,1)}), bf16[576,768]{1,0:T(8,128)(2,1)}) %reduce-scatter.8.cloned.1.call-update) | async-done | bytes 884752 | tf_op jit(solution)/shard_map/reduce_scatter | solution.py:221
  542.1 50.5 %reduce-scatter.12.cloned.1.call-done = bf16[768,768]{1,0:T(8,128)(2,1)} async-done(((bf16[3072,768]{1,0:T(8,128)(2,1)}), bf16[768,768]{1,0:T(8,128)(2,1)}) %reduce-scatter.12.cloned.1.call-update) | async-done | bytes 1179664 | tf_op jit(solution)/shard_map/reduce_scatter | solution.py:148
  592.7 50.4 %reduce-scatter.14.cloned.1.call-done = bf16[192,3072]{1,0:T(8,128)(2,1)} async-done(((bf16[768,3072]{1,0:T(8,128)(2,1)}), bf16[192,3072]{1,0:T(8,128)(2,1)}) %reduce-scatter.14.cloned.1.call-update) | async-done | bytes 1179664 | tf_op jit(solution)/shard_map/reduce_scatter | solution.py:154
  643.0 323.5 %all-reduce.19 = (f32[192,1536]{1,0:T(8,128)S(1)}, f32[192]{0:T(256)}, f32[192]{0:T(256)}, f32[192]{0:T(256)}, f32[576,768]{1,0:T(8,128)}, /*index=5*/f32[192,76...) all-reduce(bf16[192,1536]{1,0:T(8,128)(2,1)} %reduce-scatter.6.clon, ...), channel_id=1, replica_groups=mesh['dp'=8,'fsdp'=4] {'dp'}, use_global_device_ids=true, to_apply=%region_16.17 | all-reduce | flops 2066496 | bytes 12403200 | tf_op jit(solution)/shard_map/psum | solution.py:231
  (351 shorter events, 239.6 us)
Async XLA Ops:
  7.2 4.9 copy-start.40
  7.2 5.1 copy-start.41
  7.2 5.3 copy-start.42
  7.2 5.5 copy-start.43
  7.2 5.8 copy-start.44
  7.3 6.0 copy-start.45
  7.3 19.7 %copy-start.11 = (bf16[904,768]{1,0:T(8,128)(2,1)S(1)}, bf16[904,768]{1,0:T(8,128)(2,1)}, u32[]{:S(2)}) copy-start(bf16[904,768]{1,0:T(8,128)(2,1)} %param.22) | copy-start | bytes 4165636
  7.3 29.4 %all-gather.7.cloned.1.call-start = ((), (), s32[]{:S(2)}) async-start(), calls=%async_computation.5 | async-start | bytes 2949120 | tf_op jit(solution)/shard_map/all_gather | solution.py:64
  8.0 61.0 %all-gather.9.cloned.1.call-start = ((), (), s32[]{:S(2)}) async-start(), calls=%async_computation.6 | async-start | bytes 4423680 | tf_op jit(solution)/shard_map/all_gather | solution.py:65
  8.8 19.5 %copy-start.30 = (bf16[768]{0:T(1024)(128)(2,1)S(1)}, bf16[768]{0:T(1024)(128)(2,1)}, u32[]{:S(2)}) copy-start(bf16[768]{0:T(1024)(128)(2,1)} %param.37) | copy-start | bytes 4612
  8.8 24.9 %copy-start.12 = (bf16[904,768]{1,0:T(8,128)(2,1)S(1)}, bf16[904,768]{1,0:T(8,128)(2,1)}, u32[]{:S(2)}) copy-start(bf16[904,768]{1,0:T(8,128)(2,1)} %param.23) | copy-start | bytes 4165636
  8.8 169.7 %all-gather.11.cloned.1.call-start = ((), (), s32[]{:S(2)}) async-start(), calls=%async_computation.7 | async-start | bytes 1474560 | tf_op jit(solution)/shard_map/all_gather | solution.py:66
  9.5 173.6 %all-gather.13.cloned.1.call-start = ((), (), s32[]{:S(2)}) async-start(), calls=%async_computation.8 | async-start | bytes 5898240 | tf_op jit(solution)/shard_map/all_gather | solution.py:128
  10.1 206.1 %all-gather.15.cloned.1.call-start = ((), (), s32[]{:S(2)}) async-start(), calls=%async_computation.9 | async-start | bytes 5898240 | tf_op jit(solution)/shard_map/all_gather | solution.py:129
  10.7 507.8 %reduce-scatter.10.cloned.1.call-start = ((), (), s32[]{:S(2)}) async-start(), calls=%async_computation.12 | async-start | bytes 1474560 | tf_op jit(solution)/shard_map/reduce_scatter | solution.py:224
  26.9 151.5 %copy-start.16 = (f32[768]{0:T(1024)}, f32[768]{0:T(1024)S(1)}, u32[]{:S(2)}) copy-start(f32[768]{0:T(1024)S(1)} %convert_element_type.170) | copy-start | bytes 9220
  28.2 40.8 %copy-start.22 = (f32[768]{0:T(1024)}, f32[768]{0:T(1024)S(1)}, u32[]{:S(2)}) copy-start(f32[768]{0:T(1024)S(1)} %convert_element_type.171) | copy-start | bytes 9220
  28.2 40.8 %copy-start.27 = (f32[768]{0:T(1024)}, f32[768]{0:T(1024)S(1)}, u32[]{:S(2)}) copy-start(f32[768]{0:T(1024)S(1)} %convert_element_type.172) | copy-start | bytes 9220
  41.7 35.2 %copy-start.4 = (f32[904,768]{1,0:T(8,128)}, f32[904,768]{1,0:T(8,128)S(1)}, u32[]{:S(2)}) copy-start(f32[904,768]{1,0:T(8,128)S(1)} %get-tuple-element.422) | copy-start | bytes 8331268
  41.7 35.2 %copy-start.18 = (f32[904]{0:T(1024)}, f32[904]{0:T(1024)S(1)}, u32[]{:S(2)}) copy-start(f32[904]{0:T(1024)S(1)} %broadcast_multiply_fusion.7) | copy-start | bytes 10852
  43.2 33.7 %copy-start.24 = (f32[904]{0:T(1024)}, f32[904]{0:T(1024)S(1)}, u32[]{:S(2)}) copy-start(f32[904]{0:T(1024)S(1)} %fusion.51) | copy-start | bytes 10852
  43.2 35.1 %copy-start.39 = (s32[904]{0:T(1024)S(1)}, s32[904]{0:T(1024)}, u32[]{:S(2)}) copy-start(s32[904]{0:T(1024)} %param.25) | copy-start | bytes 10852
  182.6 48.2 %copy-start.2 = (f32[904,768]{1,0:T(8,128)}, f32[904,768]{1,0:T(8,128)S(1)}, u32[]{:S(2)}) copy-start(f32[904,768]{1,0:T(8,128)S(1)} %get-tuple-element.424) | copy-start | bytes 8331268
  216.2 14.7 %copy-start.38 = (bf16[3072,768]{1,0:T(8,128)(2,1)S(1)}, bf16[3072,768]{1,0:T(8,128)(2,1)}, u32[]{:S(2)}) copy-start(bf16[3072,768]{1,0:T(8,128)(2,1)} %all-gather.13.cloned.1.call-done) | copy-start | bytes 14155780
  230.8 5.0 copy-start.47
  249.7 187.9 %copy-start.17 = (f32[768]{0:T(1024)S(1)}, f32[768]{0:T(1024)}, u32[]{:S(2)}) copy-start(f32[768]{0:T(1024)} %copy-done.16) | copy-start | bytes 9220
  249.7 187.9 %copy-start.19 = (f32[904]{0:T(1024)S(1)}, f32[904]{0:T(1024)}, u32[]{:S(2)}) copy-start(f32[904]{0:T(1024)} %copy-done.18) | copy-start | bytes 10852
  249.8 187.9 %copy-start.23 = (f32[768]{0:T(1024)S(1)}, f32[768]{0:T(1024)}, u32[]{:S(2)}) copy-start(f32[768]{0:T(1024)} %copy-done.22) | copy-start | bytes 9220
  249.8 187.9 %copy-start.25 = (f32[904]{0:T(1024)S(1)}, f32[904]{0:T(1024)}, u32[]{:S(2)}) copy-start(f32[904]{0:T(1024)} %copy-done.24) | copy-start | bytes 10852
  253.7 4.1 copy-start
  269.3 4.1 copy-start
  300.6 4.1 copy-start
  331.8 4.1 copy-start
  363.1 4.1 copy-start
  437.5 80.9 %reduce-scatter.6.cloned.1.call-start = ((), (), s32[]{:S(2)}) async-start(), calls=%async_computation.10 | async-start | bytes 2949120 | tf_op jit(solution)/shard_map/reduce_scatter | solution.py:209
  437.6 8.7 copy-start.21
  437.6 8.8 copy-start.5
  449.9 5.9 copy-start.6
  450.0 5.9 copy-start.28
  455.8 86.4 %reduce-scatter.8.cloned.1.call-start = ((), (), s32[]{:S(2)}) async-start(), calls=%async_computation.11 | async-start | bytes 4423680 | tf_op jit(solution)/shard_map/reduce_scatter | solution.py:221
  464.6 128.1 %reduce-scatter.12.cloned.1.call-start = ((), (), s32[]{:S(2)}) async-start(), calls=%async_computation.13 | async-start | bytes 5898240 | tf_op jit(solution)/shard_map/reduce_scatter | solution.py:148
  477.0 166.1 %reduce-scatter.14.cloned.1.call-start = ((), (), s32[]{:S(2)}) async-start(), calls=%async_computation.14 | async-start | bytes 5898240 | tf_op jit(solution)/shard_map/reduce_scatter | solution.py:154
  972.2 4.5 copy-start.36
  972.2 5.1 copy-start.35
  972.3 5.6 copy-start.34
  972.3 6.2 copy-start.33
  972.3 6.7 copy-start.32
  972.3 7.3 copy-start.31
  (32 other events, 78.6 us)
Sparse Core Ops, SparseCore 0:
  9.6 26.9 all-gather.6
  38.2 30.7 all-gather.8
  70.5 17.4 all-gather.10
  89.4 37.4 all-gather.12
  128.3 37.4 all-gather.14
  437.7 25.1 reduce-scatter.9
  465.9 33.1 reduce-scatter.5
  501.7 40.3 reduce-scatter.7
  544.7 47.9 reduce-scatter.11
  595.0 47.9 reduce-scatter.13
where the time goes:
time: 993 us; the launch traced here: 987 us
  matrix products  380 us (38%)
  blocking collectives  354 us (36%)
  waiting for transfers between devices  155 us (16%)
  other arithmetic  40.4 us (4%)
  local copies, waits for them, and re-layouts  39.4 us (4%)
  between operations  16.9 us (2%)
    psum x1, blocking collectives, shards(): lax.psum((mlp_shards[0], mlp_shards[1], mlp_shards[2], mlp_shards[3], mlp...  324 us
    dot_general x41, matrix products, times_t(): lax.dot_general(left, weight, (((1,), (1,)), ((), ())), preferred_element...  181 us
    dot_general x29, matrix products, times_n(): return jnp.dot(left, weight, preferred_element_type=jnp.float32)  106 us
    dot_general x29, matrix products, rows_outer(): lax.dot_general(grad_rows, left, (((0,), (0,)), ((), ())), preferred_elem...  93.6 us
    reduce_scatter x1, waiting for transfers between devices, shards(): lax.psum_scatter(grad_hidden_weight.astype(jnp.bfloat16), 'fsdp', scatter...  50.5 us
    reduce_scatter x1, waiting for transfers between devices, shards(): lax.psum_scatter(grad_output_weight.astype(jnp.bfloat16), 'fsdp', scatter...  50.4 us
    all_gather x1, waiting for transfers between devices, shards(): lax.all_gather(qkv_weight, 'fsdp', axis=0, tiled=True)  25.8 us
    unnamed x2, blocking collectives  24.6 us
  transfers between devices with their start and end apart: 10, of which 5 were waited for; matrix products, arithmetic and copies ran while one was open for 20% of the time, Pallas kernels for 0%

commit v1 on v0

--- a/solution.py
+++ b/solution.py
@@ -35,6 +35,41 @@
 
 def column_sums(grad_rows):
     return jnp.sum(grad_rows.astype(jnp.float32), axis=0)
+
+
+def bit_pairs(count, bit):
+    return [(place, place ^ (1 << bit)) for place in range(count)]
+
+
+def add_low(first, second):
+    return (first.astype(jnp.float32) + second.astype(jnp.float32)).astype(jnp.bfloat16)
+
+
+def half_swap(stack, axis_name, bit):
+    mine = (lax.axis_index(axis_name) >> bit) & 1
+    keep = lax.dynamic_index_in_dim(stack, mine, 1, keepdims=False)
+    send = lax.dynamic_index_in_dim(stack, 1 - mine, 1, keepdims=False)
+    return add_low(keep, lax.ppermute(send, axis_name, bit_pairs(lax.axis_size(axis_name), bit)))
+
+
+def reduce_shard(grad):
+    n_group, n_data = lax.axis_size("fsdp"), lax.axis_size("dp")
+    rows, columns = grad.shape[0] // n_group, grad.shape[1]
+    part = grad.reshape(n_group, rows, columns)
+    for bit in range(n_group.bit_length() - 1):
+        part = half_swap(part.reshape(-1, 2, rows, columns), "fsdp", bit)
+    part = part.reshape(rows, columns)
+    bits = n_data.bit_length() - 1
+    for bit in range(bits - 1):
+        part = half_swap(part.reshape(1, 2, -1, columns), "dp", bit)[0]
+    part = add_low(part, lax.ppermute(part, "dp", bit_pairs(n_data, bits - 1)))
+    for bit in reversed(range(bits - 1)):
+        other = lax.ppermute(part, "dp", bit_pairs(n_data, bit))
+        low = ((lax.axis_index("dp") >> bit) & 1) == 0
+        part = jnp.where(
+            low, jnp.concatenate([part, other], 0), jnp.concatenate([other, part], 0)
+        )
+    return part.astype(jnp.float32) / (n_group * n_data)
 
 
 def shards(
@@ -144,26 +179,9 @@
     norm_value, norm_back = jax.vjp(layer_norm, stream_b, gain_second, shift_second)
     grad_part_b, grad_mlp_gain, grad_mlp_shift = norm_back(grad_normed_b)
     grad_stream_b = grad_out.astype(jnp.float32) + grad_part_b
-    mlp_shards = (
-        lax.psum_scatter(
-            grad_hidden_weight.astype(jnp.bfloat16), "fsdp", scatter_dimension=0, tiled=True
-        ).astype(jnp.float32),
-        lax.psum_scatter(
-            grad_hidden_bias.astype(jnp.bfloat16), "fsdp", scatter_dimension=0, tiled=True
-        ).astype(jnp.float32),
-        lax.psum_scatter(
-            grad_output_weight.astype(jnp.bfloat16), "fsdp", scatter_dimension=0, tiled=True
-        ).astype(jnp.float32),
-        lax.psum_scatter(
-            grad_output_bias.astype(jnp.bfloat16), "fsdp", scatter_dimension=0, tiled=True
-        ).astype(jnp.float32),
-        lax.psum_scatter(
-            grad_mlp_gain.astype(jnp.bfloat16), "fsdp", scatter_dimension=0, tiled=True
-        ).astype(jnp.float32),
-        lax.psum_scatter(
-            grad_mlp_shift.astype(jnp.bfloat16), "fsdp", scatter_dimension=0, tiled=True
-        ).astype(jnp.float32),
-    )
+    vec_grads = [grad_hidden_bias, grad_output_bias, grad_mlp_gain, grad_mlp_shift]
+    final_hidden = reduce_shard(grad_hidden_weight.astype(jnp.bfloat16))
+    final_output = reduce_shard(grad_output_weight.astype(jnp.bfloat16))
     skip_back, qkv_back, proj_back = (skip_full, qkv_full, proj_full)
     grad_branch = grad_stream_b.astype(jnp.bfloat16)
     grad_proj_weight = rows_outer(grad_branch, attended)
@@ -205,69 +223,48 @@
     grad_joined = times_n(grad_rounded, skip_back)
     grad_input = grad_joined[:, :model_width].astype(jnp.bfloat16)
     grad_skip = grad_joined[:, model_width:].astype(jnp.bfloat16)
-    attn_shards = (
-        lax.psum_scatter(
-            grad_skip_weight.astype(jnp.bfloat16), "fsdp", scatter_dimension=0, tiled=True
-        ).astype(jnp.float32),
-        lax.psum_scatter(
-            grad_skip_bias.astype(jnp.bfloat16), "fsdp", scatter_dimension=0, tiled=True
-        ).astype(jnp.float32),
-        lax.psum_scatter(
-            grad_attn_gain.astype(jnp.bfloat16), "fsdp", scatter_dimension=0, tiled=True
-        ).astype(jnp.float32),
-        lax.psum_scatter(
-            grad_attn_shift.astype(jnp.bfloat16), "fsdp", scatter_dimension=0, tiled=True
-        ).astype(jnp.float32),
-        lax.psum_scatter(
-            grad_qkv_weight.astype(jnp.bfloat16), "fsdp", scatter_dimension=0, tiled=True
-        ).astype(jnp.float32),
-        lax.psum_scatter(
-            grad_proj_weight.astype(jnp.bfloat16), "fsdp", scatter_dimension=0, tiled=True
-        ).astype(jnp.float32),
-        lax.psum_scatter(
-            grad_proj_bias.astype(jnp.bfloat16), "fsdp", scatter_dimension=0, tiled=True
-        ).astype(jnp.float32),
-    )
-    summed = lax.psum(
-        (
-            mlp_shards[0],
-            mlp_shards[1],
-            mlp_shards[2],
-            mlp_shards[3],
-            mlp_shards[4],
-            mlp_shards[5],
-            attn_shards[0],
-            attn_shards[1],
-            attn_shards[2],
-            attn_shards[3],
-            attn_shards[4],
-            attn_shards[5],
-            attn_shards[6],
-        ),
-        "dp",
-    )
-    mlp_shards = summed[:6]
-    attn_shards = summed[6:]
-    device_total = lax.axis_size("dp") * lax.axis_size("fsdp")
-    mlp_final = [member / device_total for member in mlp_shards]
-    attn_final = [member / device_total for member in attn_shards]
+    final_proj = reduce_shard(grad_proj_weight.astype(jnp.bfloat16))
+    final_qkv = reduce_shard(grad_qkv_weight.astype(jnp.bfloat16))
+    n_group = lax.axis_size("fsdp")
+    rows = model_width // n_group
+    vectors = jnp.stack(
+        [
+            grad_skip_bias,
+            grad_attn_gain,
+            grad_attn_shift,
+            grad_proj_bias,
+            grad_mlp_gain,
+            grad_mlp_shift,
+            grad_output_bias,
+        ]
+    )
+    wide = grad_hidden_bias.reshape(n_group, -1, rows)
+    wide_count = wide.shape[1]
+    wide = jnp.swapaxes(wide, 0, 1).reshape(wide_count, model_width)
+    vectors = jnp.concatenate([vectors, wide], 0)
+    vectors = jnp.pad(vectors, ((0, 128 - vectors.shape[0]), (0, 0))).T
+    last = jnp.concatenate([grad_skip_weight, vectors], 1).astype(jnp.bfloat16)
+    last = reduce_shard(last)
+    final_skip = last[:, : 2 * model_width]
+    final_vec = last[:, 2 * model_width :].T
+    final_wide = final_vec[7 : 7 + wide_count].reshape(-1)
     return (
         output,
         grad_input,
         grad_skip,
-        attn_final[0],
-        attn_final[1],
-        attn_final[2],
-        attn_final[3],
-        attn_final[4],
-        attn_final[5],
-        attn_final[6],
-        mlp_final[4],
-        mlp_final[5],
-        mlp_final[0],
-        mlp_final[1],
-        mlp_final[2],
-        mlp_final[3],
+        final_skip,
+        final_vec[0],
+        final_vec[1],
+        final_vec[2],
+        final_qkv,
+        final_proj,
+        final_vec[3],
+        final_vec[4],
+        final_vec[5],
+        final_hidden,
+        final_wide,
+        final_output,
+        final_vec[6],
     )
 
 

time: 993 us -> 707 us (0.71)
  blocking collectives: 354 us -> 18.9 us
  local copies, waits for them, and re-layouts: 39.4 us -> 74.3 us
  starting transfers between devices: 0.39 us -> 33.5 us
  matrix products: 380 us -> 362 us
    psum x1 -> x0, blocking collectives: 324 us -> none  [shards(): lax.psum((mlp_shards[0], mlp_shards[1], mlp_shards[2], mlp_shards[3], mlp...]
    reduce_scatter x5 -> x0, waiting for transfers between devices: 125 us -> none  [the longest x1 50.5 us: shards(): lax.psum_scatter(grad_hidden_weight.astype(jnp.bfloat16), 'fsdp', scatter...]
    ppermute x0 -> x35, waiting for transfers between devices: none -> 118 us  [the longest x20 71.5 us: half_swap(): lax.ppermute(send, axis_name, bit_pairs(lax.axis_size(axis_name), bit))]
    ppermute x0 -> x35, starting transfers between devices: none -> 33.4 us  [the longest x20 20.7 us: half_swap(): lax.ppermute(send, axis_name, bit_pairs(lax.axis_size(axis_name), bit))]
    dynamic_update_slice x12, local copies, waits for them, and re-layouts: 1.3 us -> 16.8 us  [head_forward(): lax.dynamic_update_slice_in_dim(log_totals, row_max + jnp.log(row_total),...]
    dot_general x29, matrix products: 93.6 us -> 81.5 us  [rows_outer(): lax.dot_general(grad_rows, left, (((0,), (0,)), ((), ())), preferred_elem...]
    unnamed x2 -> x1, blocking collectives: 24.6 us -> 13.5 us
  transfers between devices with their start and end apart: 10 -> 40, of which waited for: 5 -> 21; matrix products, arithmetic and copies ran while one was open for 20% -> 65% of each run, Pallas kernels for 0% -> 0%
where the time goes in v1:
time: 707 us; the launch traced here: 699 us
  matrix products  362 us (51%)
  waiting for transfers between devices  147 us (21%)
  local copies, waits for them, and re-layouts  74.3 us (11%)
  other arithmetic  45.7 us (6%)
  starting transfers between devices  33.5 us (5%)
  blocking collectives  18.9 us (3%)
  between operations  15.8 us (2%)
    dot_general x41, matrix products, times_t(): lax.dot_general(left, weight, (((1,), (1,)), ((), ())), preferred_element...  178 us
    dot_general x29, matrix products, times_n(): return jnp.dot(left, weight, preferred_element_type=jnp.float32)  102 us
    dot_general x29, matrix products, rows_outer(): lax.dot_general(grad_rows, left, (((0,), (0,)), ((), ())), preferred_elem...  81.5 us
    ppermute x20, waiting for transfers between devices, half_swap(): lax.ppermute(send, axis_name, bit_pairs(lax.axis_size(axis_name), bit))  71.5 us
    ppermute x10, waiting for transfers between devices, reduce_shard(): other = lax.ppermute(part, 'dp', bit_pairs(n_data, bit))  35.1 us
    all_gather x1, waiting for transfers between devices, shards(): lax.all_gather(qkv_weight, 'fsdp', axis=0, tiled=True)  25.8 us
    while x48, local copies, waits for them, and re-layouts  21.4 us
    ppermute x20, starting transfers between devices, half_swap(): lax.ppermute(send, axis_name, bit_pairs(lax.axis_size(axis_name), bit))  20.7 us
  transfers between devices with their start and end apart: 40, of which 21 were waited for; matrix products, arithmetic and copies ran while one was open for 65% of the time, Pallas kernels for 0%

profile of v1, /device:TPU:0, one launch (start us, length us, event | category | flops | bytes accessed | tf_op | source)
XLA Modules:
  0.0 698.9 jit_solution(112456032396676453)
XLA Ops:
  13.7 13.5 %all-reduce.8 = (bf16[768]{0:T(1024)(128)(2,1)S(1)}, bf16[768]{0:T(1024)(128)(2,1)S(1)}, bf16[768]{0:T(1024)(128)(2,1)S(1)}, bf16[768]{0:T(1024)(128)(2,1)S(1)},...) all-reduce(bf16[768]{0:T(1024)(128)(2,1)S(1)} %dynamic-update-slice, ...), channel_id=1, replica_groups=mesh['dp'=8,'fsdp'=4] {'fsdp'}, use_global_device_ids=true, to_apply=%add.4 | all-reduce | flops 5376 | bytes 21504
  28.5 5.4 all-gather
  36.7 5.0 add_reduce_fusion
  43.2 25.8 %all-gather.9.cloned.1.call-done = bf16[2304,768]{1,0:T(8,128)(2,1)} async-done(((bf16[576,768]{1,0:T(8,128)(2,1)}), bf16[2304,768]{1,0:T(8,128)(2,1)}) %all-gather.9.cloned.1.call-update) | async-done | bytes 3538960 | tf_op jit(solution)/shard_map/all_gather | solution.py:100
  69.0 8.0 %convolution_convert_fusion = bf16[904,2304]{1,0:T(8,128)(2,1)} fusion(bf16[2304,768]{1,0:T(8,128)(2,1)} %all-gather.9.cloned.1.call-done, f32[904,768]{1,0:T(8,128)S(1)} %get-tuple-element.406, f32[768]{0:T(1024)S(1)} %convert_element_type.499, f32[768]{0:T(1024)S(1)} %convert_element_type.498, f32[904]{0:T(1024)S(1)} %fusion.75, ...), kind=kOutput, calls=%fused_computation.55 | convolution fusion | flops 3205453824 | bytes 10498112 | tf_op jit(solution)/shard_map/dot_general | solution.py:21
  78.4 115.1 %while.34 = (s32[]{:T(128)}, bf16[904,768]{0,1:T(8,128)(2,1)}, f32[904,12]{0,1:T(8,128)}, bf16[904,2304]{1,0:T(8,128)(2,1)}, s32[904]{0:T(1024)S(1)}, /*index=5*...) while((s32[]{:T(128)}, bf16[904,768]{0,1:T(8,128)(2,1)}, ...), condition=%wide.region_5.6_spmd.clone, body=%wide.region_2.5_spmd.clone.sunk | while | flops 217378560 | bytes 24318088 | solution.py:153
  93.9 3.8 fusion.133
  132.4 3.6 fusion.133
  193.5 4.2 fusion.86
  198.2 32.6 %multiply_convert_fusion.1 = (bf16[904,3072]{1,0:T(8,128)(2,1)S(1)}, f32[904,3072]{1,0:T(8,128)}, f32[904,3072]{1,0:T(8,128)}) fusion(f32[3072]{0:T(1024)S(1)} %bitcast.185, bf16[3072,768]{1,0:T(8,128)(2,1)} %all-gather.13.cloned.1.call-done, f32[904,768]{1,0:T(8,128)S(1)} %get-tuple-element.408, f32[768]{0:T(1024)S(1)} %convert_element_type.505, ...), kind=kOutput, calls=%fused_computation.41 | convolution fusion | flops 4452366336 | bytes 35292224 | tf_op jit(solution)/shard_map/dot_general | solution.py:21
  230.8 5.8 convolution_convert_fusion.1
  240.5 14.3 %fusion.87 = (bf16[3072]{0:T(1024)(128)(2,1)S(1)}, bf16[904,3072]{1,0:T(8,128)(2,1)S(1)}) fusion(f32[904,3072]{1,0:T(8,128)} %get-tuple-element.397, bf16[768,3072]{1,0:T(8,128)(2,1)} %all-gather.15.cloned.1.call-done, bf16[904,768]{1,0:T(8,128)(2,1)} %param.24, bf16[904]{0:T(1024)(128)(2,1)S(1)} %convert_element_type.511, ...), kind=kOutput, calls=%fused_computation.208 | convolution fusion | flops 4310731776 | bytes 33898256 | tf_op jit(solution)/shard_map/dot_general | solution.py:27
  254.8 6.6 convolution_convert_fusion.2
  263.6 7.4 %multiply_reduce_fusion.1 = (bf16[768]{0:T(1024)(128)(2,1)S(1)}, f32[904]{0:T(1024)S(1)}, bf16[768]{0:T(1024)(128)(2,1)S(1)}, f32[904,768]{1,0:T(8,128)S(1)}) fusion(f32[904,768]{1,0:T(8,128)S(1)} %get-tuple-element.408, f32[904]{0:T(1024)S(1)} %fusion.76, f32[904]{0:T(1024)S(1)} %broadcast_multiply_fusion, f32[768]{0:T(1024)S(1)} %convert_element_type.504, ...), kind=kOutput, calls=%fused_computation.71 | convolution fusion | flops 4271158784 | bytes 15843936 | tf_op jit(solution)/shard_map/dot_general | solution.py:27
  282.7 196.1 %while.35 = (s32[]{:T(128)}, bf16[904,2304]{0,1:T(8,128)(2,1)}, bf16[904,2304]{1,0:T(8,128)(2,1)}, f32[904,12]{0,1:T(8,128)}, bf16[904,768]{1,0:T(8,128)(2,1)}, ...) while((s32[]{:T(128)}, bf16[904,2304]{0,1:T(8,128)(2,1)}, ...), condition=%wide.region_12.13_spmd.clone, body=%wide.region_10.0_spmd.clone.sunk | while | flops 532122432 | bytes 40460396 | solution.py:213
  282.7 3.6 fusion.142
  287.1 4.1 multiply_reduce_fusion.9
  303.4 4.1 multiply_reduce_fusion.9
  319.7 4.1 multiply_reduce_fusion.9
  331.6 3.6 fusion.142
  336.0 4.1 multiply_reduce_fusion.9
  348.0 3.6 fusion.142
  352.3 4.1 multiply_reduce_fusion.9
  364.3 3.6 fusion.142
  368.6 4.1 multiply_reduce_fusion.9
  384.9 4.1 multiply_reduce_fusion.9
  401.2 4.1 multiply_reduce_fusion.9
  417.5 4.1 multiply_reduce_fusion.9
  433.8 4.1 multiply_reduce_fusion.9
  445.8 3.6 fusion.142
  450.1 4.1 multiply_reduce_fusion.9
  466.4 4.1 multiply_reduce_fusion.9
  478.8 7.7 %convolution_convert_fusion.3 = bf16[2304,768]{1,0:T(8,128)(2,1)S(1)} fusion(bf16[904,2304]{0,1:T(8,128)(2,1)} %get-tuple-element.307, f32[904,768]{1,0:T(8,128)} %copy-done.4, f32[768]{0:T(1024)S(1)} %copy-done.35, f32[768]{0:T(1024)S(1)} %copy-done.29, f32[904]{0:T(1024)S(1)} %copy-done.31, f32[904]{0:T(1024)S(1)} %copy-done.25, f32[768]{0:T(1024)S(1)} %copy-done.23), kind=kOutput, calls=%fused_computation.58 | convolution fusion | flops 3205140480 | bytes 10498112 | tf_op jit(solution)/shard_map/dot_general | solution.py:31
  490.2 6.8 multiply_reduce_fusion.2
  501.1 7.6 %collective-permute-done.15 = bf16[1,192,768]{2,1,0:T(8,128)(2,1)S(1)} collective-permute-done((bf16[1,192,768]{2,1,0:T(8,128)(2,1)S(1)}, bf16[1,192,768]{2,1,0:T(8,128)(2,1)S(1)}, u32[]{:S(2)}, u32[]{:S(2)}) %collective-permute-start.15) | collective-permute-done | bytes 294944 | tf_op jit(solution)/shard_map/ppermute | solution.py:52
  510.8 3.9 convolution_convert_fusion.5
  523.5 9.6 %add_convert_fusion.2 = bf16[904,768]{1,0:T(8,128)(2,1)} fusion(f32[904,768]{1,0:T(8,128)S(1)} %copy-done.3, bf16[904,3072]{1,0:T(8,128)(2,1)} %copy-done.52, bf16[768,3072]{1,0:T(8,128)(2,1)} %all-gather.15.cloned.1.call-done, f32[768]{0:T(1024)S(1)} %copy-done.33), kind=kOutput, calls=%fused_computation.77 | convolution fusion | flops 4267689984 | bytes 14441472 | tf_op jit(solution)/shard_map/dot_general | solution.py:21
  544.1 4.9 collective-permute-done.1
  563.8 7.2 %collective-permute-done.4 = bf16[48,1664]{1,0:T(8,128)(2,1)S(1)} collective-permute-done((bf16[48,1664]{1,0:T(8,128)(2,1)S(1)}, bf16[48,1664]{1,0:T(8,128)(2,1)S(1)}, u32[]{:S(2)}, u32[]{:S(2)}) %collective-permute-start.4) | collective-permute-done | bytes 159776 | tf_op jit(solution)/shard_map/ppermute | solution.py:65
  580.1 6.6 collective-permute-done.6
  588.7 11.3 %collective-permute-done.29 = bf16[1,192,3072]{2,1,0:T(8,128)(2,1)S(1)} collective-permute-done((bf16[1,192,3072]{2,1,0:T(8,128)(2,1)S(1)}, bf16[1,192,3072]{2,1,0:T(8,128)(2,1)S(1)}, u32[]{:S(2)}, u32[]{:S(2)}) %collective-permute-start.29) | collective-permute-done | bytes 1179680 | tf_op jit(solution)/shard_map/ppermute | solution.py:52
  602.7 18.1 %collective-permute-done.22 = bf16[1,768,768]{2,1,0:T(8,128)(2,1)S(1)} collective-permute-done((bf16[1,768,768]{2,1,0:T(8,128)(2,1)S(1)}, bf16[1,768,768]{2,1,0:T(8,128)(2,1)S(1)}, u32[]{:S(2)}, u32[]{:S(2)}) %collective-permute-start.22) | collective-permute-done | bytes 1179680 | tf_op jit(solution)/shard_map/ppermute | solution.py:52
  625.2 6.9 collective-permute-done.23
  636.9 12.0 %collective-permute-done.24 = bf16[1,192,768]{2,1,0:T(8,128)(2,1)S(1)} collective-permute-done((bf16[1,192,768]{2,1,0:T(8,128)(2,1)S(1)}, bf16[1,192,768]{2,1,0:T(8,128)(2,1)S(1)}, u32[]{:S(2)}, u32[]{:S(2)}) %collective-permute-start.24) | collective-permute-done | bytes 294944 | tf_op jit(solution)/shard_map/ppermute | solution.py:52
  649.1 3.9 collective-permute-done.32
  653.1 6.5 collective-permute-done.12
  674.5 9.6 %collective-permute-done.34 = bf16[96,3072]{1,0:T(8,128)(2,1)S(1)} collective-permute-done((bf16[96,3072]{1,0:T(8,128)(2,1)S(1)}, bf16[96,3072]{1,0:T(8,128)(2,1)S(1)}, u32[]{:S(2)}, u32[]{:S(2)}) %collective-permute-start.34) | collective-permute-done | bytes 589856 | tf_op jit(solution)/shard_map/ppermute | solution.py:67
  685.8 4.6 collective-permute-done.27
  (480 shorter events, 351.9 us)
Async XLA Ops:
  7.3 29.4 %all-gather.7.cloned.1.call-start = ((), (), s32[]{:S(2)}) async-start(), calls=%async_computation | async-start | bytes 2949120 | tf_op jit(solution)/shard_map/all_gather | solution.py:99
  8.0 61.0 %all-gather.9.cloned.1.call-start = ((), (), s32[]{:S(2)}) async-start(), calls=%async_computation.1 | async-start | bytes 4423680 | tf_op jit(solution)/shard_map/all_gather | solution.py:100
  8.8 184.7 %all-gather.11.cloned.1.call-start = ((), (), s32[]{:S(2)}) async-start(), calls=%async_computation.2 | async-start | bytes 1474560 | tf_op jit(solution)/shard_map/all_gather | solution.py:101
  9.5 188.7 %all-gather.13.cloned.1.call-start = ((), (), s32[]{:S(2)}) async-start(), calls=%async_computation.3 | async-start | bytes 5898240 | tf_op jit(solution)/shard_map/all_gather | solution.py:163
  10.1 230.3 %all-gather.15.cloned.1.call-start = ((), (), s32[]{:S(2)}) async-start(), calls=%async_computation.4 | async-start | bytes 5898240 | tf_op jit(solution)/shard_map/all_gather | solution.py:164
  27.2 166.3 %copy-start.22 = (f32[768]{0:T(1024)}, f32[768]{0:T(1024)S(1)}, u32[]{:S(2)}) copy-start(f32[768]{0:T(1024)S(1)} %convert_element_type.497) | copy-start | bytes 9220
  28.4 40.6 %copy-start.28 = (f32[768]{0:T(1024)}, f32[768]{0:T(1024)S(1)}, u32[]{:S(2)}) copy-start(f32[768]{0:T(1024)S(1)} %convert_element_type.498) | copy-start | bytes 9220
  197.7 65.9 %copy-start.2 = (f32[904,768]{1,0:T(8,128)}, f32[904,768]{1,0:T(8,128)S(1)}, u32[]{:S(2)}) copy-start(f32[904,768]{1,0:T(8,128)S(1)} %get-tuple-element.408) | copy-start | bytes 8331268
  240.4 317.6 %collective-permute-start.28 = (bf16[2,192,3072]{2,1,0:T(8,128)(2,1)}, bf16[2,192,3072]{2,1,0:T(8,128)(2,1)}, u32[]{:S(2)}, u32[]{:S(2)}) collective-permute-start(bf16[2,192,3072]{2,1,0:T(8,128)(2,1)} %dynamic-slice_bitcast_fusion), channel_id=1, source_target_pairs={{0,1},{1,0},{2,3},{3,2},{4,5},{5,4},{6,7},{7,6},{8,9},{9,8},{10,11... | collective-permute-start | bytes 7077896 | tf_op jit(solution)/shard_map/ppermute | solution.py:52
  263.1 314.1 %collective-permute-start.21 = (bf16[2,768,768]{2,1,0:T(8,128)(2,1)}, bf16[2,768,768]{2,1,0:T(8,128)(2,1)}, u32[]{:S(2)}, u32[]{:S(2)}) collective-permute-start(bf16[2,768,768]{2,1,0:T(8,128)(2,1)} %dynamic-slice_bitcast_fusion.1), channel_id=1, source_target_pairs={{0,1},{1,0},{2,3},{3,2},{4,5},{5,4},{6,7},{7,6},{8,9},{9,8},{10,11... | collective-permute-start | bytes 7077896 | tf_op jit(solution)/shard_map/ppermute | solution.py:52
  276.9 221.4 %collective-permute-start.14 = (bf16[2,192,768]{2,1,0:T(8,128)(2,1)S(1)}, bf16[2,192,768]{2,1,0:T(8,128)(2,1)}, u32[]{:S(2)}, u32[]{:S(2)}) collective-permute-start(bf16[2,192,768]{2,1,0:T(8,128)(2,1)S(1)} %dynamic-slice_bitcast_fusion.5), channel_id=1, source_target_pairs={{0,1},{1,0},{2,3},{3,2},{4,5},{5,4},{6,7},{7,6},{8,9},{9,8},{10,11... | collective-permute-start | bytes 1769480 | tf_op jit(solution)/shard_map/ppermute | solution.py:52
  282.7 196.1 %copy-start.23 = (f32[768]{0:T(1024)S(1)}, f32[768]{0:T(1024)}, u32[]{:S(2)}) copy-start(f32[768]{0:T(1024)} %copy-done.22) | copy-start | bytes 9220
  282.7 196.1 %copy-start.25 = (f32[904]{0:T(1024)S(1)}, f32[904]{0:T(1024)}, u32[]{:S(2)}) copy-start(f32[904]{0:T(1024)} %copy-done.24) | copy-start | bytes 10852
  282.7 196.1 %copy-start.29 = (f32[768]{0:T(1024)S(1)}, f32[768]{0:T(1024)}, u32[]{:S(2)}) copy-start(f32[768]{0:T(1024)} %copy-done.28) | copy-start | bytes 9220
  282.7 196.1 %copy-start.31 = (f32[904]{0:T(1024)S(1)}, f32[904]{0:T(1024)}, u32[]{:S(2)}) copy-start(f32[904]{0:T(1024)} %copy-done.30) | copy-start | bytes 10852
  282.7 196.1 %copy-start.35 = (f32[768]{0:T(1024)S(1)}, f32[768]{0:T(1024)}, u32[]{:S(2)}) copy-start(f32[768]{0:T(1024)} %copy-done.34) | copy-start | bytes 9220
  487.9 62.1 %collective-permute-start.7 = (bf16[2,576,768]{2,1,0:T(8,128)(2,1)}, bf16[2,576,768]{2,1,0:T(8,128)(2,1)}, u32[]{:S(2)}, u32[]{:S(2)}) collective-permute-start(bf16[2,576,768]{2,1,0:T(8,128)(2,1)} %dynamic-slice_bitcast_fusion.2), channel_id=1, source_target_pairs={{0,1},{1,0},{2,3},{3,2},{4,5},{5,4},{6,7},{7,6},{8,9},{9,8},{10,11... | collective-permute-start | bytes 5308424 | tf_op jit(solution)/shard_map/ppermute | solution.py:52
  499.7 9.0 %collective-permute-start.15 = (bf16[1,192,768]{2,1,0:T(8,128)(2,1)S(1)}, bf16[1,192,768]{2,1,0:T(8,128)(2,1)S(1)}, u32[]{:S(2)}, u32[]{:S(2)}) collective-permute-start(bf16[1,192,768]{2,1,0:T(8,128)(2,1)S(1)} %constant_dynamic-slice_fusion.3), channel_id=1, source_target_pairs={{0,2},{1,3},{2,0},{3,1},{4,6},{5,7},{6,4},{7,5},{8,10},{9,11},{10,... | collective-permute-start | bytes 884744 | tf_op jit(solution)/shard_map/ppermute | solution.py:52
  509.5 6.1 collective-permute-start.16
  516.5 4.4 collective-permute-start.17
  519.5 15.2 %collective-permute-start = (bf16[2,192,1664]{2,1,0:T(8,128)(2,1)S(1)}, bf16[2,192,1664]{2,1,0:T(8,128)(2,1)S(1)}, u32[]{:S(2)}, u32[]{:S(2)}) collective-permute-start(bf16[2,192,1664]{2,1,0:T(8,128)(2,1)S(1)} %fusion.47), channel_id=1, source_target_pairs={{0,1},{1,0},{2,3},{3,2},{4,5},{5,4},{6,7},{7,6},{8,9},{9,8},{10,11... | collective-permute-start | bytes 3833864 | tf_op jit(solution)/shard_map/ppermute | solution.py:52
  521.0 12.0 %collective-permute-start.18 = (bf16[48,768]{1,0:T(8,128)(2,1)S(1)}, bf16[48,768]{1,0:T(8,128)(2,1)S(1)}, u32[]{:S(2)}, u32[]{:S(2)}) collective-permute-start(bf16[48,768]{1,0:T(8,128)(2,1)S(1)} %fusion.74), channel_id=1, source_target_pairs={{0,16},{4,20},{8,24},{12,28},{16,0},{20,4},{24,8},{28,12},{1,17},{... | collective-permute-start | bytes 221192 | tf_op jit(solution)/shard_map/ppermute | solution.py:65
  533.1 4.9 collective-permute-start.19
  535.0 14.0 %collective-permute-start.1 = (bf16[1,192,1664]{2,1,0:T(8,128)(2,1)S(1)}, bf16[1,192,1664]{2,1,0:T(8,128)(2,1)S(1)}, u32[]{:S(2)}, u32[]{:S(2)}) collective-permute-start(bf16[1,192,1664]{2,1,0:T(8,128)(2,1)S(1)} %constant_dynamic-slice_fusion.5), channel_id=1, source_target_pairs={{0,2},{1,3},{2,0},{3,1},{4,6},{5,7},{6,4},{7,5},{8,10},{9,11},{10,... | collective-permute-start | bytes 1916936 | tf_op jit(solution)/shard_map/ppermute | solution.py:52
  538.0 5.2 collective-permute-start.20
  549.2 7.1 %collective-permute-start.2 = (bf16[1,96,1664]{2,1,0:T(8,128)(2,1)S(1)}, bf16[1,96,1664]{2,1,0:T(8,128)(2,1)S(1)}, u32[]{:S(2)}, u32[]{:S(2)}) collective-permute-start(bf16[1,96,1664]{2,1,0:T(8,128)(2,1)S(1)} %dynamic-slice_bitcast_fusion.7), channel_id=1, source_target_pairs={{0,4},{4,0},{8,12},{12,8},{16,20},{20,16},{24,28},{28,24},{1,5},{5... | collective-permute-start | bytes 958472 | tf_op jit(solution)/shard_map/ppermute | solution.py:52
  552.1 22.6 %collective-permute-start.8 = (bf16[1,576,768]{2,1,0:T(8,128)(2,1)S(1)}, bf16[1,576,768]{2,1,0:T(8,128)(2,1)S(1)}, u32[]{:S(2)}, u32[]{:S(2)}) collective-permute-start(bf16[1,576,768]{2,1,0:T(8,128)(2,1)S(1)} %constant_dynamic-slice_fusion.4), channel_id=1, source_target_pairs={{0,2},{1,3},{2,0},{3,1},{4,6},{5,7},{6,4},{7,5},{8,10},{9,11},{10,... | collective-permute-start | bytes 2654216 | tf_op jit(solution)/shard_map/ppermute | solution.py:52
  556.4 6.6 collective-permute-start.3
  563.0 8.0 %collective-permute-start.4 = (bf16[48,1664]{1,0:T(8,128)(2,1)S(1)}, bf16[48,1664]{1,0:T(8,128)(2,1)S(1)}, u32[]{:S(2)}, u32[]{:S(2)}) collective-permute-start(bf16[48,1664]{1,0:T(8,128)(2,1)S(1)} %fusion.72), channel_id=1, source_target_pairs={{0,16},{4,20},{8,24},{12,28},{16,0},{20,4},{24,8},{28,12},{1,17},{... | collective-permute-start | bytes 479240 | tf_op jit(solution)/shard_map/ppermute | solution.py:65
  563.2 36.8 %collective-permute-start.29 = (bf16[1,192,3072]{2,1,0:T(8,128)(2,1)S(1)}, bf16[1,192,3072]{2,1,0:T(8,128)(2,1)S(1)}, u32[]{:S(2)}, u32[]{:S(2)}) collective-permute-start(bf16[1,192,3072]{2,1,0:T(8,128)(2,1)S(1)} %constant_dynamic-slice_fusion.1), channel_id=1, source_target_pairs={{0,2},{1,3},{2,0},{3,1},{4,6},{5,7},{6,4},{7,5},{8,10},{9,11},{10,... | collective-permute-start | bytes 3538952 | tf_op jit(solution)/shard_map/ppermute | solution.py:52
  571.0 5.4 collective-permute-start.5
  575.0 11.9 %collective-permute-start.9 = (bf16[1,288,768]{2,1,0:T(8,128)(2,1)S(1)}, bf16[1,288,768]{2,1,0:T(8,128)(2,1)S(1)}, u32[]{:S(2)}, u32[]{:S(2)}) collective-permute-start(bf16[1,288,768]{2,1,0:T(8,128)(2,1)S(1)} %dynamic-slice_bitcast_fusion.6), channel_id=1, source_target_pairs={{0,4},{4,0},{8,12},{12,8},{16,20},{20,16},{24,28},{28,24},{1,5},{5... | collective-permute-start | bytes 1327112 | tf_op jit(solution)/shard_map/ppermute | solution.py:52
  576.5 10.3 %collective-permute-start.6 = (bf16[96,1664]{1,0:T(8,128)(2,1)S(1)}, bf16[96,1664]{1,0:T(8,128)(2,1)S(1)}, u32[]{:S(2)}, u32[]{:S(2)}) collective-permute-start(bf16[96,1664]{1,0:T(8,128)(2,1)S(1)} %maximum_select_fusion.7), channel_id=1, source_target_pairs={{0,4},{4,0},{8,12},{12,8},{16,20},{20,16},{24,28},{28,24},{1,5},{5... | collective-permute-start | bytes 958472 | tf_op jit(solution)/shard_map/ppermute | solution.py:67
  579.5 41.2 %collective-permute-start.22 = (bf16[1,768,768]{2,1,0:T(8,128)(2,1)S(1)}, bf16[1,768,768]{2,1,0:T(8,128)(2,1)S(1)}, u32[]{:S(2)}, u32[]{:S(2)}) collective-permute-start(bf16[1,768,768]{2,1,0:T(8,128)(2,1)S(1)} %constant_dynamic-slice_fusion.2), channel_id=1, source_target_pairs={{0,2},{1,3},{2,0},{3,1},{4,6},{5,7},{6,4},{7,5},{8,10},{9,11},{10,... | collective-permute-start | bytes 3538952 | tf_op jit(solution)/shard_map/ppermute | solution.py:52
  587.1 14.8 %collective-permute-start.10 = (bf16[1,144,768]{2,1,0:T(8,128)(2,1)S(1)}, bf16[1,144,768]{2,1,0:T(8,128)(2,1)S(1)}, u32[]{:S(2)}, u32[]{:S(2)}) collective-permute-start(bf16[1,144,768]{2,1,0:T(8,128)(2,1)S(1)} %dynamic-slice_bitcast_fusion.10), channel_id=1, source_target_pairs={{0,8},{4,12},{8,0},{12,4},{16,24},{20,28},{24,16},{28,20},{1,9},{5... | collective-permute-start | bytes 663560 | tf_op jit(solution)/shard_map/ppermute | solution.py:52
  600.5 22.1 %collective-permute-start.30 = (bf16[1,96,3072]{2,1,0:T(8,128)(2,1)S(1)}, bf16[1,96,3072]{2,1,0:T(8,128)(2,1)S(1)}, u32[]{:S(2)}, u32[]{:S(2)}) collective-permute-start(bf16[1,96,3072]{2,1,0:T(8,128)(2,1)S(1)} %dynamic-slice_bitcast_fusion.3), channel_id=1, source_target_pairs={{0,4},{4,0},{8,12},{12,8},{16,20},{20,16},{24,28},{28,24},{1,5},{5... | collective-permute-start | bytes 1769480 | tf_op jit(solution)/shard_map/ppermute | solution.py:52
  602.0 34.6 %collective-permute-start.11 = (bf16[144,768]{1,0:T(8,128)(2,1)S(1)}, bf16[144,768]{1,0:T(8,128)(2,1)S(1)}, u32[]{:S(2)}, u32[]{:S(2)}) collective-permute-start(bf16[144,768]{1,0:T(8,128)(2,1)S(1)} %fusion.71), channel_id=1, source_target_pairs={{0,16},{4,20},{8,24},{12,28},{16,0},{20,4},{24,8},{28,12},{1,17},{... | collective-permute-start | bytes 663560 | tf_op jit(solution)/shard_map/ppermute | solution.py:65
  621.1 10.9 %collective-permute-start.23 = (bf16[1,384,768]{2,1,0:T(8,128)(2,1)S(1)}, bf16[1,384,768]{2,1,0:T(8,128)(2,1)S(1)}, u32[]{:S(2)}, u32[]{:S(2)}) collective-permute-start(bf16[1,384,768]{2,1,0:T(8,128)(2,1)S(1)} %dynamic-slice_bitcast_fusion.4), channel_id=1, source_target_pairs={{0,4},{4,0},{8,12},{12,8},{16,20},{20,16},{24,28},{28,24},{1,5},{5... | collective-permute-start | bytes 1769480 | tf_op jit(solution)/shard_map/ppermute | solution.py:52
  622.7 12.8 %collective-permute-start.31 = (bf16[1,48,3072]{2,1,0:T(8,128)(2,1)S(1)}, bf16[1,48,3072]{2,1,0:T(8,128)(2,1)S(1)}, u32[]{:S(2)}, u32[]{:S(2)}) collective-permute-start(bf16[1,48,3072]{2,1,0:T(8,128)(2,1)S(1)} %dynamic-slice_bitcast_fusion.8), channel_id=1, source_target_pairs={{0,8},{4,12},{8,0},{12,4},{16,24},{20,28},{24,16},{28,20},{1,9},{5... | collective-permute-start | bytes 884744 | tf_op jit(solution)/shard_map/ppermute | solution.py:52
  632.2 16.7 %collective-permute-start.24 = (bf16[1,192,768]{2,1,0:T(8,128)(2,1)S(1)}, bf16[1,192,768]{2,1,0:T(8,128)(2,1)S(1)}, u32[]{:S(2)}, u32[]{:S(2)}) collective-permute-start(bf16[1,192,768]{2,1,0:T(8,128)(2,1)S(1)} %dynamic-slice_bitcast_fusion.9), channel_id=1, source_target_pairs={{0,8},{4,12},{8,0},{12,4},{16,24},{20,28},{24,16},{28,20},{1,9},{5... | collective-permute-start | bytes 884744 | tf_op jit(solution)/shard_map/ppermute | solution.py:52
  635.6 17.3 %collective-permute-start.32 = (bf16[48,3072]{1,0:T(8,128)(2,1)S(1)}, bf16[48,3072]{1,0:T(8,128)(2,1)S(1)}, u32[]{:S(2)}, u32[]{:S(2)}) collective-permute-start(bf16[48,3072]{1,0:T(8,128)(2,1)S(1)} %fusion.69), channel_id=1, source_target_pairs={{0,16},{4,20},{8,24},{12,28},{16,0},{20,4},{24,8},{28,12},{1,17},{... | collective-permute-start | bytes 884744 | tf_op jit(solution)/shard_map/ppermute | solution.py:65
  636.6 23.0 %collective-permute-start.12 = (bf16[144,768]{1,0:T(8,128)(2,1)S(1)}, bf16[144,768]{1,0:T(8,128)(2,1)S(1)}, u32[]{:S(2)}, u32[]{:S(2)}) collective-permute-start(bf16[144,768]{1,0:T(8,128)(2,1)S(1)} %add_convert_fusion.12), channel_id=1, source_target_pairs={{0,8},{4,12},{8,0},{12,4},{16,24},{20,28},{24,16},{28,20},{1,9},{5... | collective-permute-start | bytes 663560 | tf_op jit(solution)/shard_map/ppermute | solution.py:67
  649.0 12.2 %collective-permute-start.25 = (bf16[192,768]{1,0:T(8,128)(2,1)S(1)}, bf16[192,768]{1,0:T(8,128)(2,1)S(1)}, u32[]{:S(2)}, u32[]{:S(2)}) collective-permute-start(bf16[192,768]{1,0:T(8,128)(2,1)S(1)} %fusion.68), channel_id=1, source_target_pairs={{0,16},{4,20},{8,24},{12,28},{16,0},{20,4},{24,8},{28,12},{1,17},{... | collective-permute-start | bytes 884744 | tf_op jit(solution)/shard_map/ppermute | solution.py:65
  653.0 12.2 %collective-permute-start.33 = (bf16[48,3072]{1,0:T(8,128)(2,1)S(1)}, bf16[48,3072]{1,0:T(8,128)(2,1)S(1)}, u32[]{:S(2)}, u32[]{:S(2)}) collective-permute-start(bf16[48,3072]{1,0:T(8,128)(2,1)S(1)} %add_convert_fusion.9), channel_id=1, source_target_pairs={{0,8},{4,12},{8,0},{12,4},{16,24},{20,28},{24,16},{28,20},{1,9},{5... | collective-permute-start | bytes 884744 | tf_op jit(solution)/shard_map/ppermute | solution.py:67
  659.8 13.3 %collective-permute-start.13 = (bf16[288,768]{1,0:T(8,128)(2,1)S(1)}, bf16[288,768]{1,0:T(8,128)(2,1)S(1)}, u32[]{:S(2)}, u32[]{:S(2)}) collective-permute-start(bf16[288,768]{1,0:T(8,128)(2,1)S(1)} %maximum_select_fusion.6), channel_id=1, source_target_pairs={{0,4},{4,0},{8,12},{12,8},{16,20},{20,16},{24,28},{28,24},{1,5},{5... | collective-permute-start | bytes 1327112 | tf_op jit(solution)/shard_map/ppermute | solution.py:67
  661.3 7.1 %collective-permute-start.26 = (bf16[192,768]{1,0:T(8,128)(2,1)S(1)}, bf16[192,768]{1,0:T(8,128)(2,1)S(1)}, u32[]{:S(2)}, u32[]{:S(2)}) collective-permute-start(bf16[192,768]{1,0:T(8,128)(2,1)S(1)} %add_convert_fusion.10), channel_id=1, source_target_pairs={{0,8},{4,12},{8,0},{12,4},{16,24},{20,28},{24,16},{28,20},{1,9},{5... | collective-permute-start | bytes 884744 | tf_op jit(solution)/shard_map/ppermute | solution.py:67
  665.3 18.7 %collective-permute-start.34 = (bf16[96,3072]{1,0:T(8,128)(2,1)S(1)}, bf16[96,3072]{1,0:T(8,128)(2,1)S(1)}, u32[]{:S(2)}, u32[]{:S(2)}) collective-permute-start(bf16[96,3072]{1,0:T(8,128)(2,1)S(1)} %maximum_select_fusion.5), channel_id=1, source_target_pairs={{0,4},{4,0},{8,12},{12,8},{16,20},{20,16},{24,28},{28,24},{1,5},{5... | collective-permute-start | bytes 1769480 | tf_op jit(solution)/shard_map/ppermute | solution.py:67
  668.6 21.8 %collective-permute-start.27 = (bf16[384,768]{1,0:T(8,128)(2,1)S(1)}, bf16[384,768]{1,0:T(8,128)(2,1)S(1)}, u32[]{:S(2)}, u32[]{:S(2)}) collective-permute-start(bf16[384,768]{1,0:T(8,128)(2,1)S(1)} %maximum_select_fusion.4), channel_id=1, source_target_pairs={{0,4},{4,0},{8,12},{12,8},{16,20},{20,16},{24,28},{28,24},{1,5},{5... | collective-permute-start | bytes 1769480 | tf_op jit(solution)/shard_map/ppermute | solution.py:67
  (71 other events, 615.8 us)
Sparse Core Ops, SparseCore 0:
  9.7 26.9 all-gather.6
  38.2 30.7 all-gather.8
  70.6 17.4 all-gather.10
  89.5 37.4 all-gather.12
  128.4 37.4 all-gather.14

commit v2 on v1

--- a/solution.py
+++ b/solution.py
@@ -1,6 +1,10 @@
+import functools
+
 import jax
 import jax.numpy as jnp
 from jax import lax
+from jax.experimental import pallas as pl
+from jax.experimental.pallas import tpu as pltpu
 from jax.sharding import PartitionSpec as P
 
 H = 12
@@ -70,6 +74,260 @@
             low, jnp.concatenate([part, other], 0), jnp.concatenate([other, part], 0)
         )
     return part.astype(jnp.float32) / (n_group * n_data)
+
+
+LANES = 128
+f32, bf16 = jnp.float32, jnp.bfloat16
+NT = (((1,), (1,)), ((), ()))
+NN = (((1,), (0,)), ((), ()))
+
+
+def dot_nt(left, right):
+    return lax.dot_general(left, right, NT, preferred_element_type=f32)
+
+
+def dot_nn(left, right):
+    return lax.dot_general(left, right, NN, preferred_element_type=f32)
+
+
+def lane_index(rows):
+    return lax.broadcasted_iota(jnp.int32, (rows, LANES), 1)
+
+
+def split_three(column, lane, rest):
+    high = column.astype(bf16).astype(f32)
+    middle = (column - high).astype(bf16).astype(f32)
+    low = column - high - middle
+    wide = jnp.where(lane == 3, high, jnp.where(lane == 4, middle, jnp.where(lane == 5, low, rest)))
+    return wide.astype(bf16)
+
+
+def padded(count, step):
+    return -(-count // step) * step
+
+
+def attention_forward_kernel(scale, rows, chunk, q_ref, k_ref, v_ref, qmark_ref, kmark_ref, out_ref, qaug_ref, qa, ka, va):
+    total = qa.shape[0]
+    keys = ka.shape[1]
+    head = q_ref.shape[1] // 2
+    qa[0:rows, 0:LANES] = q_ref[...] * jnp.asarray(scale, bf16)
+    qa[0:rows, LANES:] = qmark_ref[...]
+    lane_k = lane_index(rows)
+    for j in range(2):
+        own = (lane_k >= head * j) & (lane_k < head * (j + 1))
+        k_own = jnp.where(own, k_ref[...], jnp.zeros_like(k_ref))
+        ka[j, 0:rows, 0:LANES] = k_own
+        ka[j, 0:rows, LANES:] = kmark_ref[...]
+        ones = jnp.where(lane_k == head * (1 - j), jnp.ones_like(v_ref), jnp.zeros_like(v_ref))
+        va[j, 0:rows, :] = jnp.where(own, v_ref[...], ones)
+        va[j, rows:, :] = jnp.zeros((keys - rows, LANES), bf16)
+        ka[j, rows:, 0:LANES] = jnp.zeros((keys - rows, LANES), bf16)
+        lane_pad = lane_index(keys - rows)
+        ka[j, rows:, LANES:] = jnp.where(lane_pad < 3, masked_score, 0.0).astype(bf16)
+    if total > rows:
+        lane_pad = lane_index(total - rows)
+        qa[rows:, 0:LANES] = jnp.zeros((total - rows, LANES), bf16)
+        qa[rows:, LANES:] = jnp.where(lane_pad == 0, 1.0, 0.0).astype(bf16)
+    lane = lane_index(chunk)
+    for start in range(0, total, chunk):
+        q_rows = qa[start : start + chunk, :]
+        outs = []
+        size = min(chunk, rows - start)
+        for j in range(2):
+            scores = dot_nt(q_rows, ka[j])
+            row_max = jnp.max(scores, axis=1, keepdims=True)
+            probs = jnp.exp(scores - row_max).astype(bf16)
+            out = dot_nn(probs, va[j])
+            row_sum = out[:, head * (1 - j) : head * (1 - j) + 1]
+            outs.append(out / row_sum)
+            log_total = row_max + jnp.log(row_sum)
+            aug = split_three(-log_total, lane, q_rows[:, LANES:].astype(f32))
+            qaug_ref[start : start + size, j * LANES : (j + 1) * LANES] = aug[:size]
+        both = jnp.where(lane < head, outs[0], outs[1]).astype(bf16)
+        out_ref[start : start + size, :] = both[:size]
+
+
+def attention_forward(packed, qmark, kmark, chunk=304):
+    rows, width = packed.shape[0], packed.shape[1] // 3
+    pairs = width // LANES
+    total, keys = padded(rows, 16), padded(rows, 256)
+    if total % chunk:
+        chunk = total
+    kernel = functools.partial(attention_forward_kernel, (width // H) ** (-0.5), rows, chunk)
+    block = lambda offset: pl.BlockSpec((rows, LANES), lambda g: (0, g + offset))
+    fixed = pl.BlockSpec((rows, LANES), lambda g: (0, 0))
+    return pl.pallas_call(
+        kernel,
+        grid=(pairs,),
+        in_specs=[block(0), block(pairs), block(2 * pairs), fixed, fixed],
+        out_specs=[pl.BlockSpec((rows, LANES), lambda g: (0, g)), pl.BlockSpec((rows, 2 * LANES), lambda g: (0, g))],
+        out_shape=[
+            jax.ShapeDtypeStruct((rows, width), bf16),
+            jax.ShapeDtypeStruct((rows, 2 * width), bf16),
+        ],
+        scratch_shapes=[
+            pltpu.VMEM((total, 2 * LANES), bf16),
+            pltpu.VMEM((2, keys, 2 * LANES), bf16),
+            pltpu.VMEM((2, keys, LANES), bf16),
+        ],
+        name="attention_forward",
+    )(packed, packed, packed, qmark, kmark)
+
+
+def attention_backward_kernel(scale, rows, chunk, q_ref, k_ref, v_ref, go_ref, out_ref, qaug_ref, kmark_ref, dq_ref, dk_ref, dv_ref, qa, da, ka, va, kt, dqt):
+    queries = qa.shape[1]
+    total = ka.shape[0]
+    head = q_ref.shape[1] // 2
+    lane = lane_index(rows)
+    ka[0:rows, 0:LANES] = k_ref[...]
+    ka[0:rows, LANES:] = kmark_ref[...]
+    va[0:rows, 0:LANES] = v_ref[...]
+    ones = jnp.where((lane >= 3) & (lane < 6), 1.0, 0.0).astype(bf16)
+    va[0:rows, LANES:] = ones
+    if total > rows:
+        pad = total - rows
+        ka[rows:, 0:LANES] = jnp.zeros((pad, LANES), bf16)
+        ka[rows:, LANES:] = jnp.where(lane_index(pad) < 3, masked_score, 0.0).astype(bf16)
+        va[rows:, :] = jnp.zeros((pad, 2 * LANES), bf16)
+    kt[...] = ka[:, 0:LANES].astype(f32).T.astype(bf16)
+    for j in range(2):
+        own = (lane >= head * j) & (lane < head * (j + 1))
+        qa[j, 0:rows, 0:LANES] = jnp.where(own, q_ref[...] * jnp.asarray(scale, bf16), jnp.zeros_like(q_ref))
+        qa[j, 0:rows, LANES:] = qaug_ref[:, j * LANES : (j + 1) * LANES]
+        go = jnp.where(own, go_ref[...], jnp.zeros_like(go_ref))
+        delta = jnp.sum(go.astype(f32) * out_ref[...].astype(f32), axis=1, keepdims=True)
+        da[j, 0:rows, 0:LANES] = go
+        da[j, 0:rows, LANES:] = split_three(-delta, lane, 0.0)
+        qa[j, rows:, :] = jnp.zeros((queries - rows, 2 * LANES), bf16)
+        da[j, rows:, :] = jnp.zeros((queries - rows, 2 * LANES), bf16)
+    for start in range(0, total, chunk):
+        here = slice(start, start + chunk)
+        dk = dv = None
+        size = min(chunk, rows - start)
+        for j in range(2):
+            probs = jnp.exp(dot_nt(ka[here, :], qa[j]))
+            grad_probs = dot_nt(va[here, :], da[j])
+            grad_scores = (probs * grad_probs).astype(bf16)
+            dv_part = dot_nn(probs.astype(bf16), da[j, :, 0:LANES])
+            dk_part = dot_nn(grad_scores, qa[j, :, 0:LANES])
+            dq_part = dot_nn(kt[j * head : (j + 1) * head, here], grad_scores)
+            spot = slice(j * head, (j + 1) * head)
+            dqt[spot, :] = dq_part if start == 0 else dqt[spot, :] + dq_part
+            dk = dk_part if dk is None else dk + dk_part
+            dv = dv_part if dv is None else dv + dv_part
+        dk_ref[start : start + size, :] = dk.astype(bf16)[:size]
+        dv_ref[start : start + size, :] = dv.astype(bf16)[:size]
+    dq_ref[...] = (dqt[...].T * scale).astype(bf16)[:rows]
+
+
+def attention_backward(packed, grad_attended, attended, qaug, kmark, chunk=912):
+    rows, width = packed.shape[0], packed.shape[1] // 3
+    pairs = width // LANES
+    queries = padded(rows, 256)
+    total = padded(rows, 16)
+    if total % chunk:
+        chunk = total
+    kernel = functools.partial(attention_backward_kernel, (width // H) ** (-0.5), rows, chunk)
+    block = lambda offset: pl.BlockSpec((rows, LANES), lambda g: (0, g + offset))
+    fixed = pl.BlockSpec((rows, LANES), lambda g: (0, 0))
+    return pl.pallas_call(
+        kernel,
+        grid=(pairs,),
+        in_specs=[block(0), block(pairs), block(2 * pairs), block(0), block(0), pl.BlockSpec((rows, 2 * LANES), lambda g: (0, g)), fixed],
+        out_specs=[block(0)] * 3,
+        out_shape=[jax.ShapeDtypeStruct((rows, width), bf16)] * 3,
+        scratch_shapes=[
+            pltpu.VMEM((2, queries, 2 * LANES), bf16),
+            pltpu.VMEM((2, queries, 2 * LANES), bf16),
+            pltpu.VMEM((total, 2 * LANES), bf16),
+            pltpu.VMEM((total, 2 * LANES), bf16),
+            pltpu.VMEM((LANES, total), bf16),
+            pltpu.VMEM((LANES, queries), f32),
+        ],
+        name="attention_backward",
+    )(packed, packed, packed, grad_attended, attended, qaug, kmark)
+
+
+def marks(row_item, row_live):
+    rows = row_item.shape[0]
+    lane = lane_index(rows)
+    item = row_item[:, None] == lane
+    qmark = item.astype(bf16)
+    barred = (lane < 3) & ~(item & (row_live[:, None] == 1))
+    kmark = jnp.where(barred, masked_score, jnp.where((lane >= 3) & (lane < 6), 1.0, 0.0)).astype(bf16)
+    return qmark, kmark
+
+
+def place_kernel(half, place_ref, own, near, far, own_c, near_c, far_c, out_ref, sems):
+    f, low = place_ref[0], place_ref[1]
+    copies = []
+    for at, (base, piece_own, piece_near, piece_far) in enumerate(
+        ((f, own, near, far), (f ^ 1, own_c, near_c, far_c))
+    ):
+        begin = 2 * half * (base ^ 2)
+        spots = (
+            (piece_own, 2 * half * base, 2 * half),
+            (piece_near, begin + half * low, half),
+            (piece_far, begin + half * (1 - low), half),
+        )
+        for spot, (piece, start, size) in enumerate(spots):
+            rows = pl.ds(pl.multiple_of(start, half), size)
+            copies.append(
+                pltpu.make_async_copy(piece, out_ref.at[rows, :], sems.at[3 * at + spot])
+            )
+    for copy in copies:
+        copy.start()
+    for copy in copies:
+        copy.wait()
+
+
+def gather_rows(shard, name):
+    rows, columns = shard.shape
+    half = rows // 2
+    n_group, n_data = lax.axis_size("fsdp"), lax.axis_size("dp")
+    low = lax.axis_index("dp") & 1
+    send = lax.dynamic_slice_in_dim(shard, half * low, half, 0)
+    near = lax.ppermute(send, "fsdp", bit_pairs(n_group, 1))
+    own_c = lax.ppermute(shard, "fsdp", bit_pairs(n_group, 0))
+    far = lax.ppermute(near, "dp", bit_pairs(n_data, 0))
+    near_c = lax.ppermute(near, "fsdp", bit_pairs(n_group, 0))
+    far_c = lax.ppermute(far, "fsdp", bit_pairs(n_group, 0))
+    place = jnp.stack([lax.axis_index("fsdp"), low]).astype(jnp.int32)
+    anywhere = pl.BlockSpec(memory_space=pl.ANY)
+    return pl.pallas_call(
+        functools.partial(place_kernel, half),
+        in_specs=[pl.BlockSpec(memory_space=pltpu.SMEM)] + [anywhere] * 6,
+        out_specs=pl.BlockSpec(memory_space=pltpu.VMEM),
+        out_shape=jax.ShapeDtypeStruct((n_group * rows, columns), shard.dtype),
+        scratch_shapes=[pltpu.SemaphoreType.DMA((6,))],
+        name=name,
+    )(place, shard, near, far, own_c, near_c, far_c)
+
+
+def gather_vectors(members):
+    n_group = lax.axis_size("fsdp")
+    f = lax.axis_index("fsdp")
+    joined = jnp.concatenate(members)[None, :]
+    pair = lax.ppermute(joined, "fsdp", bit_pairs(n_group, 1))
+    both = jnp.concatenate([joined, pair], 0)
+    core = lax.ppermute(both, "fsdp", bit_pairs(n_group, 0))
+    every = jnp.concatenate([both, core], 0)
+    found = [every[0:1], every[2:3], every[1:2], every[3:4]]
+    ordered = jnp.concatenate(
+        [
+            sum(
+                jnp.where((f ^ at) == away, found[away], jnp.zeros_like(joined))
+                for away in range(n_group)
+            )
+            for at in range(n_group)
+        ],
+        0,
+    ).astype(jnp.float32)
+    outs, start = [], 0
+    for member in members:
+        outs.append(ordered[:, start : start + member.shape[0]].reshape(-1))
+        start += member.shape[0]
+    return outs
 
 
 def shards(
@@ -92,23 +350,8 @@
     output_weight,
     output_bias,
 ):
-    row_count, model_width = inputs.shape
-    head_size = model_width // H
-    score_scale = head_size ** (-0.5)
-    gathered = (
-        lax.all_gather(skip_weight, "fsdp", axis=0, tiled=True),
-        lax.all_gather(qkv_weight, "fsdp", axis=0, tiled=True),
-        lax.all_gather(proj_weight, "fsdp", axis=0, tiled=True),
-        lax.all_gather(skip_bias, "fsdp", axis=0, tiled=True),
-        lax.all_gather(attn_gain, "fsdp", axis=0, tiled=True),
-        lax.all_gather(attn_shift, "fsdp", axis=0, tiled=True),
-        lax.all_gather(proj_bias, "fsdp", axis=0, tiled=True),
-        lax.all_gather(mlp_gain, "fsdp", axis=0, tiled=True),
-        lax.all_gather(mlp_shift, "fsdp", axis=0, tiled=True),
-        lax.all_gather(hidden_bias, "fsdp", axis=0, tiled=True),
-        lax.all_gather(output_bias, "fsdp", axis=0, tiled=True),
-    )
-    skip_full, qkv_full, proj_full = (gathered[0], gathered[1], gathered[2])
+    model_width = inputs.shape[1]
+    skip_full = gather_rows(skip_weight, "place_skip")
     (
         skip_vec,
         gain_first,
@@ -118,51 +361,30 @@
         shift_second,
         hidden_vec,
         output_vec,
-    ) = [member.astype(jnp.float32) for member in gathered[3:]]
+    ) = gather_vectors(
+        [
+            skip_bias,
+            attn_gain,
+            attn_shift,
+            proj_bias,
+            mlp_gain,
+            mlp_shift,
+            hidden_bias,
+            output_bias,
+        ]
+    )
+    qkv_full = gather_rows(qkv_weight, "place_qkv")
+    proj_full = gather_rows(proj_weight, "place_proj")
+    hidden_full = gather_rows(hidden_weight, "place_hidden")
+    output_full = gather_rows(output_weight, "place_output")
     joined = jnp.concatenate([inputs, skip_input], axis=1)
     stream_a = times_t(joined, skip_full) + skip_vec
     normed_a = layer_norm(stream_a, gain_first, shift_first).astype(jnp.bfloat16)
     packed = times_t(normed_a, qkv_full).astype(jnp.bfloat16)
-    allowed = (row_item[:, None] == row_item[None, :]) & (row_live[None, :] == 1)
-
-    def head_slices(head_index):
-        query_head = lax.dynamic_slice_in_dim(packed, head_index * head_size, head_size, 1)
-        key_head = lax.dynamic_slice_in_dim(
-            packed, model_width + head_index * head_size, head_size, 1
-        )
-        value_head = lax.dynamic_slice_in_dim(
-            packed, 2 * model_width + head_index * head_size, head_size, 1
-        )
-        scores = jnp.where(allowed, times_t(query_head, key_head) * score_scale, masked_score)
-        return (query_head, key_head, value_head, scores)
-
-    def head_forward(head_index, state):
-        merged, log_totals = state
-        query_head, key_head, value_head, scores = head_slices(head_index)
-        row_max = jnp.max(scores, axis=1, keepdims=True)
-        exp_scores = jnp.exp(scores - row_max)
-        row_total = jnp.sum(exp_scores, axis=1, keepdims=True)
-        attn_probs = (exp_scores / row_total).astype(jnp.bfloat16)
-        head_out = times_n(attn_probs, value_head)
-        merged = lax.dynamic_update_slice_in_dim(merged, head_out, head_index * head_size, 1)
-        log_totals = lax.dynamic_update_slice_in_dim(
-            log_totals, row_max + jnp.log(row_total), head_index, 1
-        )
-        return (merged, log_totals)
-
-    merged, log_totals = lax.fori_loop(
-        0,
-        H,
-        head_forward,
-        (jnp.zeros((row_count, model_width), jnp.float32), jnp.zeros((row_count, H), jnp.float32)),
-    )
-    attended = merged.astype(jnp.bfloat16)
+    qmark, kmark = marks(row_item, row_live)
+    attended, qaug = attention_forward(packed, qmark, kmark)
     stream_b = stream_a + times_t(attended, proj_full) + proj_vec
     normed_b = layer_norm(stream_b, gain_second, shift_second).astype(jnp.bfloat16)
-    hidden_full, output_full = (
-        lax.all_gather(hidden_weight, "fsdp", axis=0, tiled=True),
-        lax.all_gather(output_weight, "fsdp", axis=0, tiled=True),
-    )
     pre_act = times_t(normed_b, hidden_full) + hidden_vec
     activation = jax.nn.gelu(pre_act, approximate=False).astype(jnp.bfloat16)
     output = (stream_b + times_t(activation, output_full) + output_vec).astype(jnp.bfloat16)
@@ -188,31 +410,9 @@
     grad_proj_bias = column_sums(grad_branch)
     grad_attended = times_n(grad_branch, proj_back).astype(jnp.bfloat16)
 
-    def head_backward(head_index, grad_packed):
-        query_head, key_head, value_head, scores = head_slices(head_index)
-        log_head = lax.dynamic_slice_in_dim(log_totals, head_index, 1, 1)
-        grad_head = lax.dynamic_slice_in_dim(grad_attended, head_index * head_size, head_size, 1)
-        probs_full = jnp.exp(scores - log_head)
-        grad_value = rows_outer(probs_full.astype(jnp.bfloat16), grad_head)
-        grad_probs = times_t(grad_head, value_head)
-        row_delta = jnp.sum(probs_full * grad_probs, axis=1, keepdims=True)
-        grad_scores = (probs_full * (grad_probs - row_delta)).astype(jnp.bfloat16)
-        grad_query = times_n(grad_scores, key_head) * score_scale
-        grad_key = rows_outer(grad_scores, query_head) * score_scale
-        grad_packed = lax.dynamic_update_slice_in_dim(
-            grad_packed, grad_query, head_index * head_size, 1
-        )
-        grad_packed = lax.dynamic_update_slice_in_dim(
-            grad_packed, grad_key, model_width + head_index * head_size, 1
-        )
-        grad_packed = lax.dynamic_update_slice_in_dim(
-            grad_packed, grad_value, 2 * model_width + head_index * head_size, 1
-        )
-        return grad_packed
-
-    grad_qkv = lax.fori_loop(
-        0, H, head_backward, jnp.zeros((row_count, 3 * model_width), jnp.float32)
-    ).astype(jnp.bfloat16)
+    grad_qkv = jnp.concatenate(
+        attention_backward(packed, grad_attended, attended, qaug, kmark), axis=1
+    )
     grad_qkv_weight = rows_outer(grad_qkv, normed_a)
     grad_normed_a = times_n(grad_qkv, qkv_back)
     first_value, first_back = jax.vjp(layer_norm, stream_a, gain_first, shift_first)

time: 707 us -> 463 us (0.65)
  matrix products: 362 us -> 116 us
  Pallas kernels: 0 us -> 76.6 us
  local copies, waits for them, and re-layouts: 74.3 us -> 32.2 us
  other arithmetic: 45.7 us -> 24.9 us
  blocking collectives: 18.9 us -> 0 us
  between operations: 15.8 us -> 2.17 us
  starting transfers between devices: 33.5 us -> 46.5 us
  waiting for transfers between devices: 147 us -> 159 us
    dot_general x41 -> x5, matrix products: 178 us -> 54.2 us  [times_t(): lax.dot_general(left, weight, (((1,), (1,)), ((), ())), preferred_element...]
    pallas_call x0 -> x7, Pallas kernels: none -> 76.6 us  [the longest x1 33.8 us: attention_backward(): pl.pallas_call(kernel, grid=(pairs,), in_specs=[block(0), block(pairs), b...]
    dot_general x29 -> x5, matrix products: 102 us -> 32.2 us  [times_n(): return jnp.dot(left, weight, preferred_element_type=jnp.float32)]
    dot_general x29 -> x5, matrix products: 81.5 us -> 29.4 us  [rows_outer(): lax.dot_general(grad_rows, left, (((0,), (0,)), ((), ())), preferred_elem...]
    ppermute x0 -> x27, waiting for transfers between devices: none -> 28.6 us  [the longest x5 24.2 us: gather_rows(): far = lax.ppermute(near, 'dp', bit_pairs(n_data, 0))]
    all_gather x5 -> x0, waiting for transfers between devices: 26.6 us -> none  [the longest x1 25.8 us: shards(): lax.all_gather(qkv_weight, 'fsdp', axis=0, tiled=True)]
    while x48 -> x0, local copies, waits for them, and re-layouts: 21.4 us -> none
    ppermute x0 -> x27, starting transfers between devices: none -> 17.4 us  [the longest x5 6.25 us: gather_rows(): far = lax.ppermute(near, 'dp', bit_pairs(n_data, 0))]
  transfers between devices with their start and end apart: 40 -> 62, of which waited for: 21 -> 28; matrix products, arithmetic and copies ran while one was open for 65% -> 21% of each run, Pallas kernels for 0% -> 8%
where the time goes in v2:
time: 463 us; the launch traced here: 457 us
  waiting for transfers between devices  159 us (34%)
  matrix products  116 us (25%)
  Pallas kernels  76.6 us (17%)
  starting transfers between devices  46.5 us (10%)
  local copies, waits for them, and re-layouts  32.2 us (7%)
  other arithmetic  24.9 us (5%)
    ppermute x20, waiting for transfers between devices, half_swap(): lax.ppermute(send, axis_name, bit_pairs(lax.axis_size(axis_name), bit))  81.5 us
    dot_general x5, matrix products, times_t(): lax.dot_general(left, weight, (((1,), (1,)), ((), ())), preferred_element...  54.2 us
    ppermute x10, waiting for transfers between devices, reduce_shard(): other = lax.ppermute(part, 'dp', bit_pairs(n_data, bit))  36.9 us
    pallas_call x1, Pallas kernels, attention_backward(): pl.pallas_call(kernel, grid=(pairs,), in_specs=[block(0), block(pairs), b...  33.8 us
    dot_general x5, matrix products, times_n(): return jnp.dot(left, weight, preferred_element_type=jnp.float32)  32.2 us
    dot_general x5, matrix products, rows_outer(): lax.dot_general(grad_rows, left, (((0,), (0,)), ((), ())), preferred_elem...  29.4 us
    ppermute x5, waiting for transfers between devices, gather_rows(): far = lax.ppermute(near, 'dp', bit_pairs(n_data, 0))  24.2 us
    pallas_call x5, Pallas kernels, gather_rows(): pl.pallas_call(functools.partial(place_kernel, half), in_specs=[pl.BlockS...  21.6 us
  transfers between devices with their start and end apart: 62, of which 28 were waited for; matrix products, arithmetic and copies ran while one was open for 21% of the time, Pallas kernels for 8%

profile of v2, /device:TPU:0, one launch (start us, length us, event | category | flops | bytes accessed | tf_op | source)
XLA Modules:
  0.0 457.2 jit_solution(17857919794799489218)
XLA Ops:
  0.7 5.5 %concatenate.144 = bf16[2112]{0:T(1024)(128)(2,1)S(1)} concatenate(bf16[192]{0:T(256)(128)(2,1)} %param.24, bf16[192]{0:T(256)(128)(2,1)} %param.25, bf16[192]{0:T(256)(128)(2,1)} %param.26, bf16[192]{0:T(256)(128)(2,1)} %param.29, bf16[192]{0:T(256)(128)(2,1)} %param.30, bf16[192]{0:T(256)(128)(2,1)} %param.31, bf16[768]{0:T(1024)(128)(2,1)} %param.33, bf16[192]{0:T(256)(128)(2,1)} %param.35), dimensions={0} | concatenate | bytes 8448 | tf_op jit(solution)/shard_map/concatenate | solution.py:310
  6.2 3.0 collective-permute-start.5
  28.5 3.6 collective-permute-done.13.far
  34.6 7.6 %collective-permute-done.1.far = bf16[96,1536]{1,0:T(8,128)(2,1)S(1)} collective-permute-done((bf16[96,1536]{1,0:T(8,128)(2,1)}, bf16[96,1536]{1,0:T(8,128)(2,1)S(1)}, u32[]{:S(2)}, u32[]{:S(2)}) %collective-permute-start.1) | collective-permute-done | bytes 294944 | tf_op jit(solution)/shard_map/ppermute | solution.py:292
  44.2 3.0 place_proj.1
  49.4 4.3 collective-permute-done.17.near
  55.9 3.7 place_skip.1
  59.6 5.0 %add_reduce_fusion = (f32[904]{0:T(1024)S(1)}, f32[904,768]{1,0:T(8,128)S(1)}) fusion(f32[768]{0:T(1024)S(1)} %add.310, bf16[904,1536]{1,0:T(8,128)(2,1)} %constant_dynamic-update-slice_fusion, bf16[768,1536]{1,0:T(8,128)(2,1)} %place_skip.1), kind=kOutput, calls=%fused_computation.48 | convolution fusion | flops 2134191232 | bytes 7920160 | tf_op jit(solution)/shard_map/dot_general | solution.py:25
  64.7 2.5 collective-permute-done.8.far
  68.9 10.5 %collective-permute-done.18.far = bf16[384,768]{1,0:T(8,128)(2,1)} collective-permute-done((bf16[384,768]{1,0:T(8,128)(2,1)}, bf16[384,768]{1,0:T(8,128)(2,1)}, u32[]{:S(2)}, u32[]{:S(2)}) %collective-permute-start.18) | collective-permute-done | bytes 589856 | tf_op jit(solution)/shard_map/ppermute | solution.py:292
  80.2 4.4 place_qkv.1
  84.6 7.8 %convolution_convert_fusion.q_ref.k_ref.v_ref = bf16[904,2304]{1,0:T(8,128)(2,1)} fusion(bf16[2304,768]{1,0:T(8,128)(2,1)} %place_qkv.1, f32[904,768]{1,0:T(8,128)S(1)} %get-tuple-element.64, f32[768]{0:T(1024)S(1)} %add.314, f32[768]{0:T(1024)S(1)} %mul.169, f32[904]{0:T(1024)S(1)} %fusion.54, f32[904]{0:T(1024)S(1)} %broadcast_multiply_fusion.1, ...), kind=kOutput, calls=%fused_computation.17 | convolution fusion | flops 3205453824 | bytes 10498112 | tf_op jit(solution)/shard_map/dot_general | solution.py:25
  92.4 21.2 %attention_forward.1 = (bf16[904,768]{1,0:T(8,128)(2,1)}, bf16[904,1536]{1,0:T(8,128)(2,1)}) custom-call(bf16[904,2304]{1,0:T(8,128)(2,1)} %convolution_convert_fusion.q_ref.k_ref.v_ref, bf16[904,2304]{1,0:T(8,128)(2,1)} %convolution_convert_fusion.q_ref.k_ref.v_ref, bf16[904,2304]{1,0:T(8,128)(2,1)} %convolution_convert_fusion.q_ref.k_ref.v_ref, ...), custom_call_target="tpu_custom_call" | custom-call | tf_op jit(solution)/shard_map/attention_forward/pallas_call | solution.py:159
  113.6 3.1 fusion.65
  119.5 5.4 %place_hidden.1 = bf16[3072,768]{1,0:T(8,128)(2,1)} custom-call(s32[2]{0:T(128)} %pad_add_fusion.place_ref, bf16[768,768]{1,0:T(8,128)(2,1)} %own.8, bf16[384,768]{1,0:T(8,128)(2,1)} %collective-permute-done.17.near, bf16[384,768]{1,0:T(8,128)(2,1)} %collective-permute-done.18.far, bf16[768,768]{1,0:T(8,128)(2,1)} %collective-permute-done.19.own_c, ...), custom_call_target="tpu_custom_call" | custom-call | tf_op jit(solution)/shard_map/place_hidden/pallas_call | solution.py:297
  124.9 32.5 %multiply_convert_fusion = (bf16[904,3072]{1,0:T(8,128)(2,1)}, f32[904,3072]{1,0:T(8,128)}, f32[904,3072]{1,0:T(8,128)}) fusion(f32[3072]{0:T(1024)S(1)} %add.327, bf16[3072,768]{1,0:T(8,128)(2,1)} %place_hidden.1, f32[904,768]{1,0:T(8,128)S(1)} %copy-done.3, f32[768]{0:T(1024)S(1)} %add.323, f32[768]{0:T(1024)S(1)} %mul.175, f32[904]{0:T(1024)S(1)} %fusion.55, ...), kind=kOutput, calls=%fused_computation.3 | convolution fusion | flops 4452366336 | bytes 35292224 | tf_op jit(solution)/shard_map/dot_general | solution.py:25
  157.4 5.1 %place_output.1 = bf16[768,3072]{1,0:T(8,128)(2,1)} custom-call(s32[2]{0:T(128)} %pad_add_fusion.place_ref, bf16[192,3072]{1,0:T(8,128)(2,1)} %own.9, bf16[96,3072]{1,0:T(8,128)(2,1)} %collective-permute-done.22.near, bf16[96,3072]{1,0:T(8,128)(2,1)} %copy-done.20, bf16[192,3072]{1,0:T(8,128)(2,1)} %collective-permute-done.24.own_c, ...), custom_call_target="tpu_custom_call" | custom-call | tf_op jit(solution)/shard_map/place_output/pallas_call | solution.py:297
  162.5 14.9 %fusion.66 = (bf16[3072]{0:T(1024)(128)(2,1)S(1)}, bf16[904,3072]{1,0:T(8,128)(2,1)S(1)}) fusion(f32[904,3072]{1,0:T(8,128)} %get-tuple-element.48, bf16[768,3072]{1,0:T(8,128)(2,1)} %place_output.1, bf16[904,768]{1,0:T(8,128)(2,1)} %param.20, bf16[904]{0:T(1024)(128)(2,1)S(1)} %convert_element_type.454, f32[904,3072]{1,0:T(8,128)} %get-tuple-element.67, ...), kind=kOutput, calls=%fused_computation.221 | convolution fusion | flops 4310731776 | bytes 33898256 | tf_op jit(solution)/shard_map/dot_general | solution.py:31
  177.4 7.3 %multiply_reduce_fusion = (bf16[768]{0:T(1024)(128)(2,1)S(1)}, f32[904]{0:T(1024)S(1)}, bf16[768]{0:T(1024)(128)(2,1)S(1)}, f32[904,768]{1,0:T(8,128)S(1)}) fusion(f32[904,768]{1,0:T(8,128)S(1)} %copy-done.3, f32[904]{0:T(1024)S(1)} %fusion.55, f32[904]{0:T(1024)S(1)} %broadcast_multiply_fusion, f32[768]{0:T(1024)S(1)} %mul.175, ...), kind=kOutput, calls=%fused_computation.33 | convolution fusion | flops 4271158784 | bytes 15843936 | tf_op jit(solution)/shard_map/dot_general | solution.py:31
  184.7 8.0 %convolution_convert_fusion.2 = bf16[3072,768]{1,0:T(8,128)(2,1)} fusion(bf16[904,3072]{1,0:T(8,128)(2,1)S(1)} %get-tuple-element.71, f32[904,768]{1,0:T(8,128)S(1)} %copy-done.3, f32[768]{0:T(1024)S(1)} %add.323, f32[768]{0:T(1024)S(1)} %mul.175, f32[904]{0:T(1024)S(1)} %fusion.55, f32[904]{0:T(1024)S(1)} %broadcast_multiply_fusion), kind=kOutput, calls=%fused_computation.19 | convolution fusion | flops 4271437824 | bytes 13063232 | tf_op jit(solution)/shard_map/dot_general | solution.py:35
  195.3 2.3 convolution_convert_fusion.6.go_ref
  197.6 2.5 convolution_convert_fusion.7
  200.1 33.8 %attention_backward.1 = (bf16[904,768]{1,0:T(8,128)(2,1)}, bf16[904,768]{1,0:T(8,128)(2,1)}, bf16[904,768]{1,0:T(8,128)(2,1)}) custom-call(bf16[904,2304]{1,0:T(8,128)(2,1)} %convolution_convert_fusion.q_ref.k_ref.v_ref, bf16[904,2304]{1,0:T(8,128)(2,1)} %convolution_convert_fusion.q_ref.k_ref.v_ref, ...), custom_call_target="tpu_custom_call" | custom-call | tf_op jit(solution)/shard_map/attention_backward/pallas_call | solution.py:233
  238.3 5.4 %multiply_reduce_fusion.1 = (bf16[768]{0:T(1024)(128)(2,1)S(1)}, f32[904]{0:T(1024)S(1)}, bf16[768]{0:T(1024)(128)(2,1)S(1)}, f32[904,768]{1,0:T(8,128)}) fusion(f32[904,768]{1,0:T(8,128)S(1)} %copy-done.1, f32[904]{0:T(1024)S(1)} %copy-done.37, f32[904]{0:T(1024)S(1)} %copy-done.31, f32[768]{0:T(1024)S(1)} %copy-done.29, f32[768]{0:T(1024)S(1)} %copy-done.35, ...), kind=kOutput, calls=%fused_computation.34 | convolution fusion | flops 3205451264 | bytes 13278816 | tf_op jit(solution)/shard_map/dot_general | solution.py:31
  243.7 6.5 %convolution_convert_fusion.3 = bf16[2304,768]{1,0:T(8,128)(2,1)} fusion(bf16[904,2304]{1,0:T(8,128)(2,1)S(1)} %constant_dynamic-update-slice_fusion.2, f32[904,768]{1,0:T(8,128)S(1)} %copy-done.1, f32[768]{0:T(1024)S(1)} %copy-done.43, f32[768]{0:T(1024)S(1)} %copy-done.35, f32[904]{0:T(1024)S(1)} %copy-done.37, f32[904]{0:T(1024)S(1)} %copy-done.31, ...), kind=kOutput, calls=%fused_computation.20 | convolution fusion | flops 3205140480 | bytes 10498112 | tf_op jit(solution)/shard_map/dot_general | solution.py:35
  250.3 7.4 %convolution_convert_fusion.1 = bf16[768,3072]{1,0:T(8,128)(2,1)} fusion(bf16[904,3072]{1,0:T(8,128)(2,1)S(1)} %bitcast.174, bf16[904,768]{1,0:T(8,128)(2,1)S(1)} %copy-done.7, bf16[904]{0:T(1024)(128)(2,1)S(1)} %convert_element_type.454), kind=kOutput, calls=%fused_computation.18 | convolution fusion | flops 4268660736 | bytes 11663120 | tf_op jit(solution)/shard_map/dot_general | solution.py:35
  257.7 5.7 %add_convert_fusion.2 = bf16[904,768]{1,0:T(8,128)(2,1)} fusion(f32[904,768]{1,0:T(8,128)S(1)} %copy-done.5, bf16[904,3072]{1,0:T(8,128)(2,1)S(1)} %bitcast.174, bf16[768,3072]{1,0:T(8,128)(2,1)S(1)} %bitcast.145, f32[768]{0:T(1024)S(1)} %copy-done.41), kind=kOutput, calls=%fused_computation.39 | convolution fusion | flops 4267689984 | bytes 14441472 | tf_op jit(solution)/shard_map/dot_general | solution.py:25
  265.2 3.9 fusion.61
  272.0 5.0 %convolution_convert_fusion.5 = bf16[768,1536]{1,0:T(8,128)(2,1)S(1)} fusion(bf16[904,768]{1,0:T(8,128)(2,1)} %get-tuple-element.42, bf16[904,1536]{1,0:T(8,128)(2,1)} %constant_dynamic-update-slice_fusion), kind=kOutput, calls=%fused_computation.32 | convolution fusion | flops 2133983232 | bytes 6524928 | tf_op jit(solution)/shard_map/dot_general | solution.py:35
  281.2 6.1 %collective-permute-done.42 = bf16[1,192,768]{2,1,0:T(8,128)(2,1)S(1)} collective-permute-done((bf16[1,192,768]{2,1,0:T(8,128)(2,1)S(1)}, bf16[1,192,768]{2,1,0:T(8,128)(2,1)S(1)}, u32[]{:S(2)}, u32[]{:S(2)}) %collective-permute-start.42) | collective-permute-done | bytes 294944 | tf_op jit(solution)/shard_map/ppermute | solution.py:56
  288.9 3.8 collective-permute-done.43
  294.6 2.6 collective-permute-done.44
  297.2 3.1 collective-permute-start.45
  313.2 5.5 %collective-permute-done.28 = bf16[1,192,1664]{2,1,0:T(8,128)(2,1)S(1)} collective-permute-done((bf16[1,192,1664]{2,1,0:T(8,128)(2,1)S(1)}, bf16[1,192,1664]{2,1,0:T(8,128)(2,1)S(1)}, u32[]{:S(2)}, u32[]{:S(2)}) %collective-permute-start.28) | collective-permute-done | bytes 639008 | tf_op jit(solution)/shard_map/ppermute | solution.py:56
  321.0 5.0 %collective-permute-done.29 = bf16[1,96,1664]{2,1,0:T(8,128)(2,1)S(1)} collective-permute-done((bf16[1,96,1664]{2,1,0:T(8,128)(2,1)S(1)}, bf16[1,96,1664]{2,1,0:T(8,128)(2,1)S(1)}, u32[]{:S(2)}, u32[]{:S(2)}) %collective-permute-start.29) | collective-permute-done | bytes 319520 | tf_op jit(solution)/shard_map/ppermute | solution.py:56
  328.0 5.1 %collective-permute-done.30 = bf16[1,48,1664]{2,1,0:T(8,128)(2,1)S(1)} collective-permute-done((bf16[1,48,1664]{2,1,0:T(8,128)(2,1)S(1)}, bf16[1,48,1664]{2,1,0:T(8,128)(2,1)S(1)}, u32[]{:S(2)}, u32[]{:S(2)}) %collective-permute-start.30) | collective-permute-done | bytes 159776 | tf_op jit(solution)/shard_map/ppermute | solution.py:56
  334.6 5.8 %collective-permute-done.31 = bf16[48,1664]{1,0:T(8,128)(2,1)S(1)} collective-permute-done((bf16[48,1664]{1,0:T(8,128)(2,1)S(1)}, bf16[48,1664]{1,0:T(8,128)(2,1)S(1)}, u32[]{:S(2)}, u32[]{:S(2)}) %collective-permute-start.31) | collective-permute-done | bytes 159776 | tf_op jit(solution)/shard_map/ppermute | solution.py:69
  340.5 2.8 collective-permute-done.35
  348.5 6.8 %collective-permute-done.33 = bf16[96,1664]{1,0:T(8,128)(2,1)S(1)} collective-permute-done((bf16[96,1664]{1,0:T(8,128)(2,1)S(1)}, bf16[96,1664]{1,0:T(8,128)(2,1)S(1)}, u32[]{:S(2)}, u32[]{:S(2)}) %collective-permute-start.33) | collective-permute-done | bytes 319520 | tf_op jit(solution)/shard_map/ppermute | solution.py:71
  356.6 11.9 %collective-permute-done.56 = bf16[1,192,3072]{2,1,0:T(8,128)(2,1)S(1)} collective-permute-done((bf16[1,192,3072]{2,1,0:T(8,128)(2,1)S(1)}, bf16[1,192,3072]{2,1,0:T(8,128)(2,1)S(1)}, u32[]{:S(2)}, u32[]{:S(2)}) %collective-permute-start.56) | collective-permute-done | bytes 1179680 | tf_op jit(solution)/shard_map/ppermute | solution.py:56
  371.4 18.0 %collective-permute-done.49 = bf16[1,768,768]{2,1,0:T(8,128)(2,1)S(1)} collective-permute-done((bf16[1,768,768]{2,1,0:T(8,128)(2,1)S(1)}, bf16[1,768,768]{2,1,0:T(8,128)(2,1)S(1)}, u32[]{:S(2)}, u32[]{:S(2)}) %collective-permute-start.49) | collective-permute-done | bytes 1179680 | tf_op jit(solution)/shard_map/ppermute | solution.py:56
  392.3 8.6 %collective-permute-done.50 = bf16[1,384,768]{2,1,0:T(8,128)(2,1)S(1)} collective-permute-done((bf16[1,384,768]{2,1,0:T(8,128)(2,1)S(1)}, bf16[1,384,768]{2,1,0:T(8,128)(2,1)S(1)}, u32[]{:S(2)}, u32[]{:S(2)}) %collective-permute-start.50) | collective-permute-done | bytes 589856 | tf_op jit(solution)/shard_map/ppermute | solution.py:56
  403.6 12.1 %collective-permute-done.51 = bf16[1,192,768]{2,1,0:T(8,128)(2,1)S(1)} collective-permute-done((bf16[1,192,768]{2,1,0:T(8,128)(2,1)S(1)}, bf16[1,192,768]{2,1,0:T(8,128)(2,1)S(1)}, u32[]{:S(2)}, u32[]{:S(2)}) %collective-permute-start.51) | collective-permute-done | bytes 294944 | tf_op jit(solution)/shard_map/ppermute | solution.py:56
  415.8 4.2 collective-permute-done.59
  420.2 6.4 %collective-permute-done.39 = bf16[144,768]{1,0:T(8,128)(2,1)S(1)} collective-permute-done((bf16[144,768]{1,0:T(8,128)(2,1)S(1)}, bf16[144,768]{1,0:T(8,128)(2,1)S(1)}, u32[]{:S(2)}, u32[]{:S(2)}) %collective-permute-start.39) | collective-permute-done | bytes 221216 | tf_op jit(solution)/shard_map/ppermute | solution.py:71
  427.8 4.2 collective-permute-done.60
  440.8 8.2 %collective-permute-done.61 = bf16[96,3072]{1,0:T(8,128)(2,1)S(1)} collective-permute-done((bf16[96,3072]{1,0:T(8,128)(2,1)S(1)}, bf16[96,3072]{1,0:T(8,128)(2,1)S(1)}, u32[]{:S(2)}, u32[]{:S(2)}) %collective-permute-start.61) | collective-permute-done | bytes 589856 | tf_op jit(solution)/shard_map/ppermute | solution.py:71
  450.7 4.6 %collective-permute-done.54 = bf16[384,768]{1,0:T(8,128)(2,1)S(1)} collective-permute-done((bf16[384,768]{1,0:T(8,128)(2,1)S(1)}, bf16[384,768]{1,0:T(8,128)(2,1)S(1)}, u32[]{:S(2)}, u32[]{:S(2)}) %collective-permute-start.54) | collective-permute-done | bytes 589856 | tf_op jit(solution)/shard_map/ppermute | solution.py:71
  (353 shorter events, 99.3 us)
Async XLA Ops:
  6.2 18.5 %collective-permute-start.5 = (bf16[1,2112]{1,0:T(2,128)(2,1)S(1)}, bf16[1,2112]{1,0:T(2,128)(2,1)S(1)}, u32[]{:S(2)}, u32[]{:S(2)}) collective-permute-start(bf16[1,2112]{1,0:T(2,128)(2,1)S(1)} %broadcast_in_dim.38), channel_id=1, source_target_pairs={{0,2},{1,3},{2,0},{3,1},{4,6},{5,7},{6,4},{7,5},{8,10},{9,11},{10,... | collective-permute-start | bytes 12680 | tf_op jit(solution)/shard_map/ppermute | solution.py:311
  9.2 23.3 %collective-permute-start.14 = (bf16[192,768]{1,0:T(8,128)(2,1)}, bf16[192,768]{1,0:T(8,128)(2,1)}, u32[]{:S(2)}, u32[]{:S(2)}) collective-permute-start(bf16[192,768]{1,0:T(8,128)(2,1)} %own.7), channel_id=1, source_target_pairs={{0,1},{1,0},{2,3},{3,2},{4,5},{5,4},{6,7},{7,6},{8,9},{9,8},{10,11... | collective-permute-start | bytes 884744 | tf_op jit(solution)/shard_map/ppermute | solution.py:291
  10.8 14.9 %collective-permute-start.12 = (bf16[96,768]{1,0:T(8,128)(2,1)}, bf16[96,768]{1,0:T(8,128)(2,1)S(1)}, u32[]{:S(2)}, u32[]{:S(2)}) collective-permute-start(bf16[96,768]{1,0:T(8,128)(2,1)} %constant_dynamic-slice_fusion.7), channel_id=1, source_target_pairs={{0,2},{1,3},{2,0},{3,1},{4,6},{5,7},{6,4},{7,5},{8,10},{9,11},{10,... | collective-permute-start | bytes 442376 | tf_op jit(solution)/shard_map/ppermute | solution.py:290
  10.9 42.8 %collective-permute-start.2 = (bf16[192,1536]{1,0:T(8,128)(2,1)}, bf16[192,1536]{1,0:T(8,128)(2,1)S(1)}, u32[]{:S(2)}, u32[]{:S(2)}) collective-permute-start(bf16[192,1536]{1,0:T(8,128)(2,1)} %own.5), channel_id=1, source_target_pairs={{0,1},{1,0},{2,3},{3,2},{4,5},{5,4},{6,7},{7,6},{8,9},{9,8},{10,11... | collective-permute-start | bytes 1769480 | tf_op jit(solution)/shard_map/ppermute | solution.py:291
  13.0 19.5 %collective-permute-start = (bf16[96,1536]{1,0:T(8,128)(2,1)}, bf16[96,1536]{1,0:T(8,128)(2,1)}, u32[]{:S(2)}, u32[]{:S(2)}) collective-permute-start(bf16[96,1536]{1,0:T(8,128)(2,1)} %constant_dynamic-slice_fusion.9), channel_id=1, source_target_pairs={{0,2},{1,3},{2,0},{3,1},{4,6},{5,7},{6,4},{7,5},{8,10},{9,11},{10,... | collective-permute-start | bytes 884744 | tf_op jit(solution)/shard_map/ppermute | solution.py:290
  27.9 19.3 %collective-permute-start.7 = (bf16[288,768]{1,0:T(8,128)(2,1)S(1)}, bf16[288,768]{1,0:T(8,128)(2,1)}, u32[]{:S(2)}, u32[]{:S(2)}) collective-permute-start(bf16[288,768]{1,0:T(8,128)(2,1)S(1)} %constant_dynamic-slice_fusion.8), channel_id=1, source_target_pairs={{0,2},{1,3},{2,0},{3,1},{4,6},{5,7},{6,4},{7,5},{8,10},{9,11},{10,... | collective-permute-start | bytes 1327112 | tf_op jit(solution)/shard_map/ppermute | solution.py:290
  32.2 21.6 %collective-permute-start.17 = (bf16[384,768]{1,0:T(8,128)(2,1)S(1)}, bf16[384,768]{1,0:T(8,128)(2,1)}, u32[]{:S(2)}, u32[]{:S(2)}) collective-permute-start(bf16[384,768]{1,0:T(8,128)(2,1)S(1)} %constant_dynamic-slice_fusion.6), channel_id=1, source_target_pairs={{0,2},{1,3},{2,0},{3,1},{4,6},{5,7},{6,4},{7,5},{8,10},{9,11},{10,... | collective-permute-start | bytes 1769480 | tf_op jit(solution)/shard_map/ppermute | solution.py:290
  32.6 9.6 %collective-permute-start.1 = (bf16[96,1536]{1,0:T(8,128)(2,1)}, bf16[96,1536]{1,0:T(8,128)(2,1)S(1)}, u32[]{:S(2)}, u32[]{:S(2)}) collective-permute-start(bf16[96,1536]{1,0:T(8,128)(2,1)} %collective-permute-done.near), channel_id=1, source_target_pairs={{0,4},{4,0},{8,12},{12,8},{16,20},{20,16},{24,28},{28,24},{1,5},{5... | collective-permute-start | bytes 884744 | tf_op jit(solution)/shard_map/ppermute | solution.py:292
  34.4 13.4 %collective-permute-start.3 = (bf16[96,1536]{1,0:T(8,128)(2,1)}, bf16[96,1536]{1,0:T(8,128)(2,1)S(1)}, u32[]{:S(2)}, u32[]{:S(2)}) collective-permute-start(bf16[96,1536]{1,0:T(8,128)(2,1)} %collective-permute-done.near), channel_id=1, source_target_pairs={{0,1},{1,0},{2,3},{3,2},{4,5},{5,4},{6,7},{7,6},{8,9},{9,8},{10,11... | collective-permute-start | bytes 884744 | tf_op jit(solution)/shard_map/ppermute | solution.py:293
  42.2 12.5 %collective-permute-start.4 = (bf16[96,1536]{1,0:T(8,128)(2,1)S(1)}, bf16[96,1536]{1,0:T(8,128)(2,1)S(1)}, u32[]{:S(2)}, u32[]{:S(2)}) collective-permute-start(bf16[96,1536]{1,0:T(8,128)(2,1)S(1)} %collective-permute-done.1.far), channel_id=1, source_target_pairs={{0,1},{1,0},{2,3},{3,2},{4,5},{5,4},{6,7},{7,6},{8,9},{9,8},{10,11... | collective-permute-start | bytes 884744 | tf_op jit(solution)/shard_map/ppermute | solution.py:294
  47.2 21.2 %collective-permute-start.9 = (bf16[576,768]{1,0:T(8,128)(2,1)}, bf16[576,768]{1,0:T(8,128)(2,1)}, u32[]{:S(2)}, u32[]{:S(2)}) collective-permute-start(bf16[576,768]{1,0:T(8,128)(2,1)} %own.6), channel_id=1, source_target_pairs={{0,1},{1,0},{2,3},{3,2},{4,5},{5,4},{6,7},{7,6},{8,9},{9,8},{10,11... | collective-permute-start | bytes 2654216 | tf_op jit(solution)/shard_map/ppermute | solution.py:291
  47.8 20.0 %collective-permute-start.22 = (bf16[96,3072]{1,0:T(8,128)(2,1)}, bf16[96,3072]{1,0:T(8,128)(2,1)}, u32[]{:S(2)}, u32[]{:S(2)}) collective-permute-start(bf16[96,3072]{1,0:T(8,128)(2,1)} %constant_dynamic-slice_fusion.5), channel_id=1, source_target_pairs={{0,2},{1,3},{2,0},{3,1},{4,6},{5,7},{6,4},{7,5},{8,10},{9,11},{10,... | collective-permute-start | bytes 1769480 | tf_op jit(solution)/shard_map/ppermute | solution.py:290
  53.8 14.6 %collective-permute-start.10 = (bf16[288,768]{1,0:T(8,128)(2,1)}, bf16[288,768]{1,0:T(8,128)(2,1)}, u32[]{:S(2)}, u32[]{:S(2)}) collective-permute-start(bf16[288,768]{1,0:T(8,128)(2,1)} %collective-permute-done.7.near), channel_id=1, source_target_pairs={{0,1},{1,0},{2,3},{3,2},{4,5},{5,4},{6,7},{7,6},{8,9},{9,8},{10,11... | collective-permute-start | bytes 1327112 | tf_op jit(solution)/shard_map/ppermute | solution.py:293
  53.8 13.4 %collective-permute-start.8 = (bf16[288,768]{1,0:T(8,128)(2,1)}, bf16[288,768]{1,0:T(8,128)(2,1)}, u32[]{:S(2)}, u32[]{:S(2)}) collective-permute-start(bf16[288,768]{1,0:T(8,128)(2,1)} %collective-permute-done.7.near), channel_id=1, source_target_pairs={{0,4},{4,0},{8,12},{12,8},{16,20},{20,16},{24,28},{28,24},{1,5},{5... | collective-permute-start | bytes 1327112 | tf_op jit(solution)/shard_map/ppermute | solution.py:292
  54.7 24.6 %collective-permute-start.18 = (bf16[384,768]{1,0:T(8,128)(2,1)}, bf16[384,768]{1,0:T(8,128)(2,1)}, u32[]{:S(2)}, u32[]{:S(2)}) collective-permute-start(bf16[384,768]{1,0:T(8,128)(2,1)} %collective-permute-done.17.near), channel_id=1, source_target_pairs={{0,4},{4,0},{8,12},{12,8},{16,20},{20,16},{24,28},{28,24},{1,5},{5... | collective-permute-start | bytes 1769480 | tf_op jit(solution)/shard_map/ppermute | solution.py:292
  67.2 13.0 %collective-permute-start.11 = (bf16[288,768]{1,0:T(8,128)(2,1)}, bf16[288,768]{1,0:T(8,128)(2,1)}, u32[]{:S(2)}, u32[]{:S(2)}) collective-permute-start(bf16[288,768]{1,0:T(8,128)(2,1)} %collective-permute-done.8.far), channel_id=1, source_target_pairs={{0,1},{1,0},{2,3},{3,2},{4,5},{5,4},{6,7},{7,6},{8,9},{9,8},{10,11... | collective-permute-start | bytes 1327112 | tf_op jit(solution)/shard_map/ppermute | solution.py:294
  67.8 51.7 %collective-permute-start.19 = (bf16[768,768]{1,0:T(8,128)(2,1)}, bf16[768,768]{1,0:T(8,128)(2,1)}, u32[]{:S(2)}, u32[]{:S(2)}) collective-permute-start(bf16[768,768]{1,0:T(8,128)(2,1)} %own.8), channel_id=1, source_target_pairs={{0,1},{1,0},{2,3},{3,2},{4,5},{5,4},{6,7},{7,6},{8,9},{9,8},{10,11... | collective-permute-start | bytes 3538952 | tf_op jit(solution)/shard_map/ppermute | solution.py:291
  68.3 89.0 %collective-permute-start.24 = (bf16[192,3072]{1,0:T(8,128)(2,1)}, bf16[192,3072]{1,0:T(8,128)(2,1)}, u32[]{:S(2)}, u32[]{:S(2)}) collective-permute-start(bf16[192,3072]{1,0:T(8,128)(2,1)} %own.9), channel_id=1, source_target_pairs={{0,1},{1,0},{2,3},{3,2},{4,5},{5,4},{6,7},{7,6},{8,9},{9,8},{10,11... | collective-permute-start | bytes 3538952 | tf_op jit(solution)/shard_map/ppermute | solution.py:291
  68.4 50.4 %collective-permute-start.20 = (bf16[384,768]{1,0:T(8,128)(2,1)}, bf16[384,768]{1,0:T(8,128)(2,1)}, u32[]{:S(2)}, u32[]{:S(2)}) collective-permute-start(bf16[384,768]{1,0:T(8,128)(2,1)} %collective-permute-done.17.near), channel_id=1, source_target_pairs={{0,1},{1,0},{2,3},{3,2},{4,5},{5,4},{6,7},{7,6},{8,9},{9,8},{10,11... | collective-permute-start | bytes 1769480 | tf_op jit(solution)/shard_map/ppermute | solution.py:293
  79.3 40.1 %collective-permute-start.23 = (bf16[96,3072]{1,0:T(8,128)(2,1)}, bf16[96,3072]{1,0:T(8,128)(2,1)S(1)}, u32[]{:S(2)}, u32[]{:S(2)}) collective-permute-start(bf16[96,3072]{1,0:T(8,128)(2,1)} %collective-permute-done.22.near), channel_id=1, source_target_pairs={{0,4},{4,0},{8,12},{12,8},{16,20},{20,16},{24,28},{28,24},{1,5},{5... | collective-permute-start | bytes 1769480 | tf_op jit(solution)/shard_map/ppermute | solution.py:292
  80.2 39.3 %collective-permute-start.21 = (bf16[384,768]{1,0:T(8,128)(2,1)}, bf16[384,768]{1,0:T(8,128)(2,1)}, u32[]{:S(2)}, u32[]{:S(2)}) collective-permute-start(bf16[384,768]{1,0:T(8,128)(2,1)} %collective-permute-done.18.far), channel_id=1, source_target_pairs={{0,1},{1,0},{2,3},{3,2},{4,5},{5,4},{6,7},{7,6},{8,9},{9,8},{10,11... | collective-permute-start | bytes 1769480 | tf_op jit(solution)/shard_map/ppermute | solution.py:294
  118.8 38.6 %collective-permute-start.25 = (bf16[96,3072]{1,0:T(8,128)(2,1)}, bf16[96,3072]{1,0:T(8,128)(2,1)}, u32[]{:S(2)}, u32[]{:S(2)}) collective-permute-start(bf16[96,3072]{1,0:T(8,128)(2,1)} %collective-permute-done.22.near), channel_id=1, source_target_pairs={{0,1},{1,0},{2,3},{3,2},{4,5},{5,4},{6,7},{7,6},{8,9},{9,8},{10,11... | collective-permute-start | bytes 1769480 | tf_op jit(solution)/shard_map/ppermute | solution.py:293
  119.4 38.0 %collective-permute-start.26 = (bf16[96,3072]{1,0:T(8,128)(2,1)S(1)}, bf16[96,3072]{1,0:T(8,128)(2,1)}, u32[]{:S(2)}, u32[]{:S(2)}) collective-permute-start(bf16[96,3072]{1,0:T(8,128)(2,1)S(1)} %collective-permute-done.23.far), channel_id=1, source_target_pairs={{0,1},{1,0},{2,3},{3,2},{4,5},{5,4},{6,7},{7,6},{8,9},{9,8},{10,11... | collective-permute-start | bytes 1769480 | tf_op jit(solution)/shard_map/ppermute | solution.py:294
  264.7 12.2 %collective-permute-start.41 = (bf16[2,192,768]{2,1,0:T(8,128)(2,1)S(1)}, bf16[2,192,768]{2,1,0:T(8,128)(2,1)}, u32[]{:S(2)}, u32[]{:S(2)}) collective-permute-start(bf16[2,192,768]{2,1,0:T(8,128)(2,1)S(1)} %dynamic-slice_bitcast_fusion.5), channel_id=1, source_target_pairs={{0,1},{1,0},{2,3},{3,2},{4,5},{5,4},{6,7},{7,6},{8,9},{9,8},{10,11... | collective-permute-start | bytes 1769480 | tf_op jit(solution)/shard_map/ppermute | solution.py:56
  278.3 9.1 %collective-permute-start.42 = (bf16[1,192,768]{2,1,0:T(8,128)(2,1)S(1)}, bf16[1,192,768]{2,1,0:T(8,128)(2,1)S(1)}, u32[]{:S(2)}, u32[]{:S(2)}) collective-permute-start(bf16[1,192,768]{2,1,0:T(8,128)(2,1)S(1)} %constant_dynamic-slice_fusion.2), channel_id=1, source_target_pairs={{0,2},{1,3},{2,0},{3,1},{4,6},{5,7},{6,4},{7,5},{8,10},{9,11},{10,... | collective-permute-start | bytes 884744 | tf_op jit(solution)/shard_map/ppermute | solution.py:56
  288.8 15.4 %collective-permute-start.27 = (bf16[2,192,1664]{2,1,0:T(8,128)(2,1)S(1)}, bf16[2,192,1664]{2,1,0:T(8,128)(2,1)S(1)}, u32[]{:S(2)}, u32[]{:S(2)}) collective-permute-start(bf16[2,192,1664]{2,1,0:T(8,128)(2,1)S(1)} %fusion.12), channel_id=1, source_target_pairs={{0,1},{1,0},{2,3},{3,2},{4,5},{5,4},{6,7},{7,6},{8,9},{9,8},{10,11... | collective-permute-start | bytes 3833864 | tf_op jit(solution)/shard_map/ppermute | solution.py:56
  300.4 19.7 %collective-permute-start.34 = (bf16[2,576,768]{2,1,0:T(8,128)(2,1)S(1)}, bf16[2,576,768]{2,1,0:T(8,128)(2,1)S(1)}, u32[]{:S(2)}, u32[]{:S(2)}) collective-permute-start(bf16[2,576,768]{2,1,0:T(8,128)(2,1)S(1)} %dynamic-slice_bitcast_fusion.2), channel_id=1, source_target_pairs={{0,1},{1,0},{2,3},{3,2},{4,5},{5,4},{6,7},{7,6},{8,9},{9,8},{10,11... | collective-permute-start | bytes 5308424 | tf_op jit(solution)/shard_map/ppermute | solution.py:56
  304.6 14.1 %collective-permute-start.28 = (bf16[1,192,1664]{2,1,0:T(8,128)(2,1)S(1)}, bf16[1,192,1664]{2,1,0:T(8,128)(2,1)S(1)}, u32[]{:S(2)}, u32[]{:S(2)}) collective-permute-start(bf16[1,192,1664]{2,1,0:T(8,128)(2,1)S(1)} %constant_dynamic-slice_fusion.4), channel_id=1, source_target_pairs={{0,2},{1,3},{2,0},{3,1},{4,6},{5,7},{6,4},{7,5},{8,10},{9,11},{10,... | collective-permute-start | bytes 1916936 | tf_op jit(solution)/shard_map/ppermute | solution.py:56
  305.4 21.7 %collective-permute-start.55 = (bf16[2,192,3072]{2,1,0:T(8,128)(2,1)S(1)}, bf16[2,192,3072]{2,1,0:T(8,128)(2,1)S(1)}, u32[]{:S(2)}, u32[]{:S(2)}) collective-permute-start(bf16[2,192,3072]{2,1,0:T(8,128)(2,1)S(1)} %dynamic-slice_bitcast_fusion), channel_id=1, source_target_pairs={{0,1},{1,0},{2,3},{3,2},{4,5},{5,4},{6,7},{7,6},{8,9},{9,8},{10,11... | collective-permute-start | bytes 7077896 | tf_op jit(solution)/shard_map/ppermute | solution.py:56
  305.5 41.6 %collective-permute-start.48 = (bf16[2,768,768]{2,1,0:T(8,128)(2,1)S(1)}, bf16[2,768,768]{2,1,0:T(8,128)(2,1)S(1)}, u32[]{:S(2)}, u32[]{:S(2)}) collective-permute-start(bf16[2,768,768]{2,1,0:T(8,128)(2,1)S(1)} %dynamic-slice_bitcast_fusion.1), channel_id=1, source_target_pairs={{0,1},{1,0},{2,3},{3,2},{4,5},{5,4},{6,7},{7,6},{8,9},{9,8},{10,11... | collective-permute-start | bytes 7077896 | tf_op jit(solution)/shard_map/ppermute | solution.py:56
  320.7 22.6 %collective-permute-start.35 = (bf16[1,576,768]{2,1,0:T(8,128)(2,1)S(1)}, bf16[1,576,768]{2,1,0:T(8,128)(2,1)S(1)}, u32[]{:S(2)}, u32[]{:S(2)}) collective-permute-start(bf16[1,576,768]{2,1,0:T(8,128)(2,1)S(1)} %constant_dynamic-slice_fusion.3), channel_id=1, source_target_pairs={{0,2},{1,3},{2,0},{3,1},{4,6},{5,7},{6,4},{7,5},{8,10},{9,11},{10,... | collective-permute-start | bytes 2654216 | tf_op jit(solution)/shard_map/ppermute | solution.py:56
  334.5 34.0 %collective-permute-start.56 = (bf16[1,192,3072]{2,1,0:T(8,128)(2,1)S(1)}, bf16[1,192,3072]{2,1,0:T(8,128)(2,1)S(1)}, u32[]{:S(2)}, u32[]{:S(2)}) collective-permute-start(bf16[1,192,3072]{2,1,0:T(8,128)(2,1)S(1)} %constant_dynamic-slice_fusion), channel_id=1, source_target_pairs={{0,2},{1,3},{2,0},{3,1},{4,6},{5,7},{6,4},{7,5},{8,10},{9,11},{10,... | collective-permute-start | bytes 3538952 | tf_op jit(solution)/shard_map/ppermute | solution.py:56
  343.5 11.9 %collective-permute-start.36 = (bf16[1,288,768]{2,1,0:T(8,128)(2,1)S(1)}, bf16[1,288,768]{2,1,0:T(8,128)(2,1)S(1)}, u32[]{:S(2)}, u32[]{:S(2)}) collective-permute-start(bf16[1,288,768]{2,1,0:T(8,128)(2,1)S(1)} %dynamic-slice_bitcast_fusion.6), channel_id=1, source_target_pairs={{0,4},{4,0},{8,12},{12,8},{16,20},{20,16},{24,28},{28,24},{1,5},{5... | collective-permute-start | bytes 1327112 | tf_op jit(solution)/shard_map/ppermute | solution.py:56
  345.8 9.5 %collective-permute-start.33 = (bf16[96,1664]{1,0:T(8,128)(2,1)S(1)}, bf16[96,1664]{1,0:T(8,128)(2,1)S(1)}, u32[]{:S(2)}, u32[]{:S(2)}) collective-permute-start(bf16[96,1664]{1,0:T(8,128)(2,1)S(1)} %maximum_select_fusion.7), channel_id=1, source_target_pairs={{0,4},{4,0},{8,12},{12,8},{16,20},{20,16},{24,28},{28,24},{1,5},{5... | collective-permute-start | bytes 958472 | tf_op jit(solution)/shard_map/ppermute | solution.py:71
  347.7 41.7 %collective-permute-start.49 = (bf16[1,768,768]{2,1,0:T(8,128)(2,1)S(1)}, bf16[1,768,768]{2,1,0:T(8,128)(2,1)S(1)}, u32[]{:S(2)}, u32[]{:S(2)}) collective-permute-start(bf16[1,768,768]{2,1,0:T(8,128)(2,1)S(1)} %constant_dynamic-slice_fusion.1), channel_id=1, source_target_pairs={{0,2},{1,3},{2,0},{3,1},{4,6},{5,7},{6,4},{7,5},{8,10},{9,11},{10,... | collective-permute-start | bytes 3538952 | tf_op jit(solution)/shard_map/ppermute | solution.py:56
  355.6 14.3 %collective-permute-start.37 = (bf16[1,144,768]{2,1,0:T(8,128)(2,1)S(1)}, bf16[1,144,768]{2,1,0:T(8,128)(2,1)S(1)}, u32[]{:S(2)}, u32[]{:S(2)}) collective-permute-start(bf16[1,144,768]{2,1,0:T(8,128)(2,1)S(1)} %dynamic-slice_bitcast_fusion.10), channel_id=1, source_target_pairs={{0,8},{4,12},{8,0},{12,4},{16,24},{20,28},{24,16},{28,20},{1,9},{5... | collective-permute-start | bytes 663560 | tf_op jit(solution)/shard_map/ppermute | solution.py:56
  369.0 21.7 %collective-permute-start.57 = (bf16[1,96,3072]{2,1,0:T(8,128)(2,1)S(1)}, bf16[1,96,3072]{2,1,0:T(8,128)(2,1)S(1)}, u32[]{:S(2)}, u32[]{:S(2)}) collective-permute-start(bf16[1,96,3072]{2,1,0:T(8,128)(2,1)S(1)} %dynamic-slice_bitcast_fusion.3), channel_id=1, source_target_pairs={{0,4},{4,0},{8,12},{12,8},{16,20},{20,16},{24,28},{28,24},{1,5},{5... | collective-permute-start | bytes 1769480 | tf_op jit(solution)/shard_map/ppermute | solution.py:56
  370.0 32.9 %collective-permute-start.38 = (bf16[144,768]{1,0:T(8,128)(2,1)S(1)}, bf16[144,768]{1,0:T(8,128)(2,1)S(1)}, u32[]{:S(2)}, u32[]{:S(2)}) collective-permute-start(bf16[144,768]{1,0:T(8,128)(2,1)S(1)} %fusion.38), channel_id=1, source_target_pairs={{0,16},{4,20},{8,24},{12,28},{16,0},{20,4},{24,8},{28,12},{1,17},{... | collective-permute-start | bytes 663560 | tf_op jit(solution)/shard_map/ppermute | solution.py:69
  389.8 11.0 %collective-permute-start.50 = (bf16[1,384,768]{2,1,0:T(8,128)(2,1)S(1)}, bf16[1,384,768]{2,1,0:T(8,128)(2,1)S(1)}, u32[]{:S(2)}, u32[]{:S(2)}) collective-permute-start(bf16[1,384,768]{2,1,0:T(8,128)(2,1)S(1)} %dynamic-slice_bitcast_fusion.4), channel_id=1, source_target_pairs={{0,4},{4,0},{8,12},{12,8},{16,20},{20,16},{24,28},{28,24},{1,5},{5... | collective-permute-start | bytes 1769480 | tf_op jit(solution)/shard_map/ppermute | solution.py:56
  390.9 11.8 %collective-permute-start.58 = (bf16[1,48,3072]{2,1,0:T(8,128)(2,1)S(1)}, bf16[1,48,3072]{2,1,0:T(8,128)(2,1)S(1)}, u32[]{:S(2)}, u32[]{:S(2)}) collective-permute-start(bf16[1,48,3072]{2,1,0:T(8,128)(2,1)S(1)} %dynamic-slice_bitcast_fusion.8), channel_id=1, source_target_pairs={{0,8},{4,12},{8,0},{12,4},{16,24},{20,28},{24,16},{28,20},{1,9},{5... | collective-permute-start | bytes 884744 | tf_op jit(solution)/shard_map/ppermute | solution.py:56
  401.0 14.6 %collective-permute-start.51 = (bf16[1,192,768]{2,1,0:T(8,128)(2,1)S(1)}, bf16[1,192,768]{2,1,0:T(8,128)(2,1)S(1)}, u32[]{:S(2)}, u32[]{:S(2)}) collective-permute-start(bf16[1,192,768]{2,1,0:T(8,128)(2,1)S(1)} %dynamic-slice_bitcast_fusion.9), channel_id=1, source_target_pairs={{0,8},{4,12},{8,0},{12,4},{16,24},{20,28},{24,16},{28,20},{1,9},{5... | collective-permute-start | bytes 884744 | tf_op jit(solution)/shard_map/ppermute | solution.py:56
  402.8 17.3 %collective-permute-start.59 = (bf16[48,3072]{1,0:T(8,128)(2,1)S(1)}, bf16[48,3072]{1,0:T(8,128)(2,1)S(1)}, u32[]{:S(2)}, u32[]{:S(2)}) collective-permute-start(bf16[48,3072]{1,0:T(8,128)(2,1)S(1)} %fusion.36), channel_id=1, source_target_pairs={{0,16},{4,20},{8,24},{12,28},{16,0},{20,4},{24,8},{28,12},{1,17},{... | collective-permute-start | bytes 884744 | tf_op jit(solution)/shard_map/ppermute | solution.py:69
  403.0 23.7 %collective-permute-start.39 = (bf16[144,768]{1,0:T(8,128)(2,1)S(1)}, bf16[144,768]{1,0:T(8,128)(2,1)S(1)}, u32[]{:S(2)}, u32[]{:S(2)}) collective-permute-start(bf16[144,768]{1,0:T(8,128)(2,1)S(1)} %add_convert_fusion.12), channel_id=1, source_target_pairs={{0,8},{4,12},{8,0},{12,4},{16,24},{20,28},{24,16},{28,20},{1,9},{5... | collective-permute-start | bytes 663560 | tf_op jit(solution)/shard_map/ppermute | solution.py:71
  415.7 11.9 %collective-permute-start.52 = (bf16[192,768]{1,0:T(8,128)(2,1)S(1)}, bf16[192,768]{1,0:T(8,128)(2,1)S(1)}, u32[]{:S(2)}, u32[]{:S(2)}) collective-permute-start(bf16[192,768]{1,0:T(8,128)(2,1)S(1)} %fusion.35), channel_id=1, source_target_pairs={{0,16},{4,20},{8,24},{12,28},{16,0},{20,4},{24,8},{28,12},{1,17},{... | collective-permute-start | bytes 884744 | tf_op jit(solution)/shard_map/ppermute | solution.py:69
  420.1 11.9 %collective-permute-start.60 = (bf16[48,3072]{1,0:T(8,128)(2,1)S(1)}, bf16[48,3072]{1,0:T(8,128)(2,1)S(1)}, u32[]{:S(2)}, u32[]{:S(2)}) collective-permute-start(bf16[48,3072]{1,0:T(8,128)(2,1)S(1)} %add_convert_fusion.9), channel_id=1, source_target_pairs={{0,8},{4,12},{8,0},{12,4},{16,24},{20,28},{24,16},{28,20},{1,9},{5... | collective-permute-start | bytes 884744 | tf_op jit(solution)/shard_map/ppermute | solution.py:71
  426.7 12.6 %collective-permute-start.40 = (bf16[288,768]{1,0:T(8,128)(2,1)S(1)}, bf16[288,768]{1,0:T(8,128)(2,1)S(1)}, u32[]{:S(2)}, u32[]{:S(2)}) collective-permute-start(bf16[288,768]{1,0:T(8,128)(2,1)S(1)} %maximum_select_fusion.6), channel_id=1, source_target_pairs={{0,4},{4,0},{8,12},{12,8},{16,20},{20,16},{24,28},{28,24},{1,5},{5... | collective-permute-start | bytes 1327112 | tf_op jit(solution)/shard_map/ppermute | solution.py:71
  432.1 16.9 %collective-permute-start.61 = (bf16[96,3072]{1,0:T(8,128)(2,1)S(1)}, bf16[96,3072]{1,0:T(8,128)(2,1)S(1)}, u32[]{:S(2)}, u32[]{:S(2)}) collective-permute-start(bf16[96,3072]{1,0:T(8,128)(2,1)S(1)} %maximum_select_fusion.5), channel_id=1, source_target_pairs={{0,4},{4,0},{8,12},{12,8},{16,20},{20,16},{24,28},{28,24},{1,5},{5... | collective-permute-start | bytes 1769480 | tf_op jit(solution)/shard_map/ppermute | solution.py:71
  435.3 20.0 %collective-permute-start.54 = (bf16[384,768]{1,0:T(8,128)(2,1)S(1)}, bf16[384,768]{1,0:T(8,128)(2,1)S(1)}, u32[]{:S(2)}, u32[]{:S(2)}) collective-permute-start(bf16[384,768]{1,0:T(8,128)(2,1)S(1)} %maximum_select_fusion.4), channel_id=1, source_target_pairs={{0,4},{4,0},{8,12},{12,8},{16,20},{20,16},{24,28},{28,24},{1,5},{5... | collective-permute-start | bytes 1769480 | tf_op jit(solution)/shard_map/ppermute | solution.py:71
  (74 other events, 719.1 us)

commit v3 on v2

--- a/solution.py
+++ b/solution.py
@@ -49,31 +49,69 @@
     return (first.astype(jnp.float32) + second.astype(jnp.float32)).astype(jnp.bfloat16)
 
 
-def half_swap(stack, axis_name, bit):
-    mine = (lax.axis_index(axis_name) >> bit) & 1
-    keep = lax.dynamic_index_in_dim(stack, mine, 1, keepdims=False)
-    send = lax.dynamic_index_in_dim(stack, 1 - mine, 1, keepdims=False)
-    return add_low(keep, lax.ppermute(send, axis_name, bit_pairs(lax.axis_size(axis_name), bit)))
-
-
-def reduce_shard(grad):
-    n_group, n_data = lax.axis_size("fsdp"), lax.axis_size("dp")
-    rows, columns = grad.shape[0] // n_group, grad.shape[1]
-    part = grad.reshape(n_group, rows, columns)
-    for bit in range(n_group.bit_length() - 1):
-        part = half_swap(part.reshape(-1, 2, rows, columns), "fsdp", bit)
-    part = part.reshape(rows, columns)
-    bits = n_data.bit_length() - 1
-    for bit in range(bits - 1):
-        part = half_swap(part.reshape(1, 2, -1, columns), "dp", bit)[0]
-    part = add_low(part, lax.ppermute(part, "dp", bit_pairs(n_data, bits - 1)))
-    for bit in reversed(range(bits - 1)):
-        other = lax.ppermute(part, "dp", bit_pairs(n_data, bit))
-        low = ((lax.axis_index("dp") >> bit) & 1) == 0
-        part = jnp.where(
-            low, jnp.concatenate([part, other], 0), jnp.concatenate([other, part], 0)
-        )
-    return part.astype(jnp.float32) / (n_group * n_data)
+def after(value, *gates):
+    return lax.optimization_barrier((value,) + gates)[0]
+
+
+class Reducer:
+    def __init__(self, name, *grads):
+        self.name = name
+        self.n_group, self.n_data = lax.axis_size("fsdp"), lax.axis_size("dp")
+        columns = grads[0].shape[1]
+        self.parts = [grad.reshape(self.n_group, -1, columns) for grad in grads]
+        bits = self.n_data.bit_length() - 1
+        self.plan = [("fsdp", bit, "halve") for bit in range(self.n_group.bit_length() - 1)]
+        self.plan += [("dp", bit, "halve") for bit in range(bits - 1)]
+        self.plan += [("dp", bits - 1, "swap")]
+        self.plan += [("dp", bit, "join") for bit in reversed(range(bits - 1))]
+        self.flight = None
+        self.at = 0
+
+    def take(self, gates):
+        if self.flight is None:
+            return
+        got = after(self.flight, *gates)
+        axis, bit, kind = self.plan[self.at - 1]
+        if kind == "join":
+            low = ((lax.axis_index(axis) >> bit) & 1) == 0
+            part = self.parts[0]
+            part = jnp.where(
+                low, jnp.concatenate([part, got], 1), jnp.concatenate([got, part], 1)
+            )
+        else:
+            part = add_low(self.keep, got)
+        self.parts = [part]
+
+    def step(self, *gates):
+        if self.at == len(self.plan):
+            return self.parts[0]
+        self.take(gates)
+        axis, bit, kind = self.plan[self.at]
+        self.at += 1
+        if kind == "halve":
+            mine = (lax.axis_index(axis) >> bit) & 1
+            keeps, sends = [], []
+            for part in self.parts:
+                columns = part.shape[-1]
+                if axis == "fsdp":
+                    stack = part.reshape(part.shape[0] // 2, 2, -1, columns)
+                else:
+                    stack = part.reshape(1, 2, -1, columns)
+                keeps.append(lax.dynamic_index_in_dim(stack, mine, 1, keepdims=False))
+                sends.append(lax.dynamic_index_in_dim(stack, 1 - mine, 1, keepdims=False))
+            self.keep = keeps[0] if len(keeps) == 1 else jnp.concatenate(keeps, 1)
+            send = sends[0] if len(sends) == 1 else jnp.concatenate(sends, 1)
+        else:
+            send = self.keep = self.parts[0]
+        with jax.named_scope(f"{self.name}_{self.at}"):
+            self.flight = lax.ppermute(send, axis, bit_pairs(lax.axis_size(axis), bit))
+        return send
+
+    def finish(self, *gates):
+        while self.at < len(self.plan):
+            self.step(*gates)
+        self.take(gates)
+        return self.parts[0][0].astype(jnp.float32) / (self.n_group * self.n_data)
 
 
 LANES = 128
@@ -174,7 +212,10 @@
     )(packed, packed, packed, qmark, kmark)
 
 
-def attention_backward_kernel(scale, rows, chunk, q_ref, k_ref, v_ref, go_ref, out_ref, qaug_ref, kmark_ref, dq_ref, dk_ref, dv_ref, qa, da, ka, va, kt, dqt):
+def attention_backward_kernel(scale, rows, chunk, first, q_ref, k_ref, v_ref, go_ref, out_ref, qaug_ref, kmark_ref, *rest):
+    grad_ref, qa, da, ka, va, kt, dqt, found, sems = rest[-9:]
+    step = pl.program_id(0)
+    dq_ref, dk_ref, dv_ref = found.at[step, 0], found.at[step, 1], found.at[step, 2]
     queries = qa.shape[1]
     total = ka.shape[0]
     head = q_ref.shape[1] // 2
@@ -219,23 +260,40 @@
         dv_ref[start : start + size, :] = dv.astype(bf16)[:size]
     dq_ref[...] = (dqt[...].T * scale).astype(bf16)[:rows]
 
-
-def attention_backward(packed, grad_attended, attended, qaug, kmark, chunk=912):
+    def copy_of(at, which):
+        column = LANES * first + LANES * at + which * (grad_ref.shape[1] // 3)
+        spot = pl.ds(pl.multiple_of(column, LANES), LANES)
+        return pltpu.make_async_copy(
+            found.at[at, which], grad_ref.at[:, spot], sems.at[at, which]
+        )
+
+    for which in range(3):
+        copy_of(step, which).start()
+
+    @pl.when(step == pl.num_programs(0) - 1)
+    def _():
+        for at in range(found.shape[0]):
+            for which in range(3):
+                copy_of(at, which).wait()
+
+
+def attention_backward(packed, grad_attended, attended, qaug, kmark, first, count, before=None, chunk=912):
     rows, width = packed.shape[0], packed.shape[1] // 3
     pairs = width // LANES
     queries = padded(rows, 256)
     total = padded(rows, 16)
     if total % chunk:
         chunk = total
-    kernel = functools.partial(attention_backward_kernel, (width // H) ** (-0.5), rows, chunk)
-    block = lambda offset: pl.BlockSpec((rows, LANES), lambda g: (0, g + offset))
+    kernel = functools.partial(attention_backward_kernel, (width // H) ** (-0.5), rows, chunk, first)
+    block = lambda offset: pl.BlockSpec((rows, LANES), lambda g: (0, g + offset + first))
+    anywhere = pl.BlockSpec(memory_space=pl.ANY)
     fixed = pl.BlockSpec((rows, LANES), lambda g: (0, 0))
     return pl.pallas_call(
         kernel,
-        grid=(pairs,),
-        in_specs=[block(0), block(pairs), block(2 * pairs), block(0), block(0), pl.BlockSpec((rows, 2 * LANES), lambda g: (0, g)), fixed],
-        out_specs=[block(0)] * 3,
-        out_shape=[jax.ShapeDtypeStruct((rows, width), bf16)] * 3,
+        grid=(count,),
+        in_specs=[block(0), block(pairs), block(2 * pairs), block(0), block(0), pl.BlockSpec((rows, 2 * LANES), lambda g: (0, g + first)), fixed] + ([] if before is None else [anywhere]),
+        out_specs=anywhere,
+        out_shape=jax.ShapeDtypeStruct((rows, 3 * width), bf16),
         scratch_shapes=[
             pltpu.VMEM((2, queries, 2 * LANES), bf16),
             pltpu.VMEM((2, queries, 2 * LANES), bf16),
@@ -243,9 +301,12 @@
             pltpu.VMEM((total, 2 * LANES), bf16),
             pltpu.VMEM((LANES, total), bf16),
             pltpu.VMEM((LANES, queries), f32),
+            pltpu.VMEM((count, 3, rows, LANES), bf16),
+            pltpu.SemaphoreType.DMA((count, 3)),
         ],
+        input_output_aliases={} if before is None else {7: 0},
         name="attention_backward",
-    )(packed, packed, packed, grad_attended, attended, qaug, kmark)
+    )(packed, packed, packed, grad_attended, attended, qaug, kmark, *([] if before is None else [before]))
 
 
 def marks(row_item, row_live):
@@ -281,20 +342,27 @@
         copy.wait()
 
 
-def gather_rows(shard, name):
+def gather_rows(shard, name, *gates):
     rows, columns = shard.shape
     half = rows // 2
     n_group, n_data = lax.axis_size("fsdp"), lax.axis_size("dp")
     low = lax.axis_index("dp") & 1
+    if gates:
+        shard = after(shard, *gates)
     send = lax.dynamic_slice_in_dim(shard, half * low, half, 0)
-    near = lax.ppermute(send, "fsdp", bit_pairs(n_group, 1))
-    own_c = lax.ppermute(shard, "fsdp", bit_pairs(n_group, 0))
-    far = lax.ppermute(near, "dp", bit_pairs(n_data, 0))
-    near_c = lax.ppermute(near, "fsdp", bit_pairs(n_group, 0))
-    far_c = lax.ppermute(far, "fsdp", bit_pairs(n_group, 0))
+    with jax.named_scope(name + "_near"):
+        near = lax.ppermute(send, "fsdp", bit_pairs(n_group, 1))
+    with jax.named_scope(name + "_own_c"):
+        own_c = lax.ppermute(shard, "fsdp", bit_pairs(n_group, 0))
+    with jax.named_scope(name + "_far"):
+        far = lax.ppermute(near, "dp", bit_pairs(n_data, 0))
+    with jax.named_scope(name + "_near_c"):
+        near_c = lax.ppermute(near, "fsdp", bit_pairs(n_group, 0))
+    with jax.named_scope(name + "_far_c"):
+        far_c = lax.ppermute(far, "fsdp", bit_pairs(n_group, 0))
     place = jnp.stack([lax.axis_index("fsdp"), low]).astype(jnp.int32)
     anywhere = pl.BlockSpec(memory_space=pl.ANY)
-    return pl.pallas_call(
+    full = pl.pallas_call(
         functools.partial(place_kernel, half),
         in_specs=[pl.BlockSpec(memory_space=pltpu.SMEM)] + [anywhere] * 6,
         out_specs=pl.BlockSpec(memory_space=pltpu.VMEM),
@@ -302,31 +370,37 @@
         scratch_shapes=[pltpu.SemaphoreType.DMA((6,))],
         name=name,
     )(place, shard, near, far, own_c, near_c, far_c)
-
-
-def gather_vectors(members):
+    return full, near
+
+
+def gather_vectors(members, *gates):
     n_group = lax.axis_size("fsdp")
     f = lax.axis_index("fsdp")
-    joined = jnp.concatenate(members)[None, :]
-    pair = lax.ppermute(joined, "fsdp", bit_pairs(n_group, 1))
-    both = jnp.concatenate([joined, pair], 0)
+    size = members[0].shape[0]
+    rows = [row for member in members for row in member.reshape(-1, size)]
+    spot = lax.broadcasted_iota(jnp.int32, (padded(len(rows), 16), size), 0)
+    packed = jnp.zeros(spot.shape, bf16)
+    for at, row in enumerate(rows):
+        packed = jnp.where(spot == at, row[None, :], packed)
+    packed = after(packed, *gates)[None]
+    pair = lax.ppermute(packed, "fsdp", bit_pairs(n_group, 1))
+    both = jnp.concatenate([packed, pair], 0)
     core = lax.ppermute(both, "fsdp", bit_pairs(n_group, 0))
-    every = jnp.concatenate([both, core], 0)
-    found = [every[0:1], every[2:3], every[1:2], every[3:4]]
-    ordered = jnp.concatenate(
+    found = [both[0], core[0], both[1], core[1]]
+    ordered = jnp.stack(
         [
             sum(
-                jnp.where((f ^ at) == away, found[away], jnp.zeros_like(joined))
+                jnp.where((f ^ at) == away, found[away], jnp.zeros_like(found[away]))
                 for away in range(n_group)
             )
             for at in range(n_group)
-        ],
-        0,
-    ).astype(jnp.float32)
+        ]
+    ).astype(f32)
     outs, start = [], 0
     for member in members:
-        outs.append(ordered[:, start : start + member.shape[0]].reshape(-1))
-        start += member.shape[0]
+        count = member.shape[0] // size
+        outs.append(ordered[:, start : start + count].reshape(-1))
+        start += count
     return outs
 
 
@@ -351,7 +425,7 @@
     output_bias,
 ):
     model_width = inputs.shape[1]
-    skip_full = gather_rows(skip_weight, "place_skip")
+    skip_full, skip_near = gather_rows(skip_weight, "place_skip")
     (
         skip_vec,
         gain_first,
@@ -371,12 +445,12 @@
             mlp_shift,
             hidden_bias,
             output_bias,
-        ]
+        ],
     )
-    qkv_full = gather_rows(qkv_weight, "place_qkv")
-    proj_full = gather_rows(proj_weight, "place_proj")
-    hidden_full = gather_rows(hidden_weight, "place_hidden")
-    output_full = gather_rows(output_weight, "place_output")
+    qkv_full, qkv_near = gather_rows(qkv_weight, "place_qkv", skip_near)
+    proj_full, _ = gather_rows(proj_weight, "place_proj", qkv_near)
+    hidden_full, _ = gather_rows(hidden_weight, "place_hidden", qkv_near)
+    output_full, _ = gather_rows(output_weight, "place_output", qkv_near)
     joined = jnp.concatenate([inputs, skip_input], axis=1)
     stream_a = times_t(joined, skip_full) + skip_vec
     normed_a = layer_norm(stream_a, gain_first, shift_first).astype(jnp.bfloat16)
@@ -387,44 +461,56 @@
     normed_b = layer_norm(stream_b, gain_second, shift_second).astype(jnp.bfloat16)
     pre_act = times_t(normed_b, hidden_full) + hidden_vec
     activation = jax.nn.gelu(pre_act, approximate=False).astype(jnp.bfloat16)
-    output = (stream_b + times_t(activation, output_full) + output_vec).astype(jnp.bfloat16)
-    hidden_back, output_back = (hidden_full, output_full)
     grad_out = cotangent * row_live[:, None].astype(jnp.bfloat16)
-    grad_output_weight = rows_outer(grad_out, activation)
-    grad_output_bias = column_sums(grad_out)
-    grad_act = times_n(grad_out, output_back)
+    grad_output_weight = rows_outer(grad_out, activation).astype(bf16)
+    reduce_out = Reducer("out", grad_output_weight)
+    sent = reduce_out.step()
+    grad_act = times_n(after(grad_out, sent), output_full)
     gelu_value, gelu_back = jax.vjp(lambda value: jax.nn.gelu(value, approximate=False), pre_act)
     grad_pre = gelu_back(grad_act)[0].astype(jnp.bfloat16)
-    grad_hidden_weight = rows_outer(grad_pre, normed_b)
+    sent = reduce_out.step(grad_pre)
+    grad_hidden_weight = rows_outer(after(grad_pre, sent), normed_b).astype(bf16)
     grad_hidden_bias = column_sums(grad_pre)
-    grad_normed_b = times_n(grad_pre, hidden_back)
+    grad_normed_b = times_n(after(grad_pre, grad_hidden_weight), hidden_full)
     norm_value, norm_back = jax.vjp(layer_norm, stream_b, gain_second, shift_second)
     grad_part_b, grad_mlp_gain, grad_mlp_shift = norm_back(grad_normed_b)
     grad_stream_b = grad_out.astype(jnp.float32) + grad_part_b
-    vec_grads = [grad_hidden_bias, grad_output_bias, grad_mlp_gain, grad_mlp_shift]
-    final_hidden = reduce_shard(grad_hidden_weight.astype(jnp.bfloat16))
-    final_output = reduce_shard(grad_output_weight.astype(jnp.bfloat16))
-    skip_back, qkv_back, proj_back = (skip_full, qkv_full, proj_full)
     grad_branch = grad_stream_b.astype(jnp.bfloat16)
-    grad_proj_weight = rows_outer(grad_branch, attended)
+    grad_proj_weight = rows_outer(grad_branch, attended).astype(bf16)
     grad_proj_bias = column_sums(grad_branch)
-    grad_attended = times_n(grad_branch, proj_back).astype(jnp.bfloat16)
-
-    grad_qkv = jnp.concatenate(
-        attention_backward(packed, grad_attended, attended, qaug, kmark), axis=1
-    )
-    grad_qkv_weight = rows_outer(grad_qkv, normed_a)
-    grad_normed_a = times_n(grad_qkv, qkv_back)
+    grad_attended = times_n(grad_branch, proj_full).astype(jnp.bfloat16)
+    reduce_mlp = Reducer("mlp", grad_hidden_weight, grad_proj_weight)
+    sent = [reduce_mlp.step(), reduce_out.step(grad_attended)]
+    pairs = model_width // LANES
+    cuts = [pairs * third // 3 for third in range(4)]
+    grad_qkv = None
+    for third in range(3):
+        with jax.named_scope(f"bwd_a{third}"):
+            grad_qkv = attention_backward(
+                packed, after(grad_attended, *sent), attended, qaug, kmark,
+                cuts[third], cuts[third + 1] - cuts[third], grad_qkv,
+            )
+        sent = [reduce_out.step(grad_qkv)]
+        if third != 1:
+            sent.append(reduce_mlp.step(grad_qkv))
+    grad_qkv_weight = rows_outer(after(grad_qkv, sent), normed_a).astype(bf16)
+    reduce_qkv = Reducer("qkv", grad_qkv_weight)
+    sent = [
+        reduce_qkv.step(),
+        reduce_out.step(grad_qkv_weight),
+    ]
+    grad_normed_a = times_n(after(grad_qkv, *sent), qkv_full)
+    sent = [
+        reduce_qkv.step(grad_normed_a),
+        reduce_mlp.step(grad_normed_a),
+    ]
     first_value, first_back = jax.vjp(layer_norm, stream_a, gain_first, shift_first)
-    grad_part_a, grad_attn_gain, grad_attn_shift = first_back(grad_normed_a)
+    grad_part_a, grad_attn_gain, grad_attn_shift = first_back(after(grad_normed_a, *sent))
     grad_rounded = (grad_stream_b + grad_part_a).astype(jnp.bfloat16)
-    grad_skip_weight = rows_outer(grad_rounded, joined)
+    sent = reduce_mlp.step(grad_rounded)
+    grad_skip_weight = rows_outer(after(grad_rounded, sent), joined)
     grad_skip_bias = column_sums(grad_rounded)
-    grad_joined = times_n(grad_rounded, skip_back)
-    grad_input = grad_joined[:, :model_width].astype(jnp.bfloat16)
-    grad_skip = grad_joined[:, model_width:].astype(jnp.bfloat16)
-    final_proj = reduce_shard(grad_proj_weight.astype(jnp.bfloat16))
-    final_qkv = reduce_shard(grad_qkv_weight.astype(jnp.bfloat16))
+    grad_output_bias = column_sums(grad_out)
     n_group = lax.axis_size("fsdp")
     rows = model_width // n_group
     vectors = jnp.stack(
@@ -442,9 +528,30 @@
     wide_count = wide.shape[1]
     wide = jnp.swapaxes(wide, 0, 1).reshape(wide_count, model_width)
     vectors = jnp.concatenate([vectors, wide], 0)
-    vectors = jnp.pad(vectors, ((0, 128 - vectors.shape[0]), (0, 0))).T
+    vectors = jnp.pad(vectors, ((0, LANES - vectors.shape[0]), (0, 0))).T
     last = jnp.concatenate([grad_skip_weight, vectors], 1).astype(jnp.bfloat16)
-    last = reduce_shard(last)
+    reduce_last = Reducer("last", last)
+    sent = [reduce_last.step(), reduce_mlp.step(last)]
+    grad_joined = times_n(after(grad_rounded, *sent), skip_full)
+    grad_input = grad_joined[:, :model_width].astype(jnp.bfloat16)
+    grad_skip = grad_joined[:, model_width:].astype(jnp.bfloat16)
+    sent = [
+        reduce_last.step(grad_input, grad_skip),
+        reduce_mlp.step(grad_input),
+        reduce_qkv.step(grad_input),
+    ]
+    output = (
+        stream_b + times_t(after(activation, *sent), output_full) + output_vec
+    ).astype(jnp.bfloat16)
+    gate = output
+    for turn in range(len(reduce_last.plan)):
+        gate = after(reduce_qkv.step(gate), reduce_last.step(gate))
+    final_output = reduce_out.finish(output)
+    both_final = reduce_mlp.finish(output)
+    final_hidden = both_final[: hidden_weight.shape[0]]
+    final_proj = both_final[hidden_weight.shape[0] :]
+    final_qkv = reduce_qkv.finish()
+    last = reduce_last.finish()
     final_skip = last[:, : 2 * model_width]
     final_vec = last[:, 2 * model_width :].T
     final_wide = final_vec[7 : 7 + wide_count].reshape(-1)

time: 463 us -> 408 us (0.88)
  waiting for transfers between devices: 159 us -> 93.9 us
  other arithmetic: 24.9 us -> 36.7 us
  matrix products: 116 us -> 106 us
  Pallas kernels: 76.6 us -> 82.7 us
  local copies, waits for them, and re-layouts: 32.2 us -> 37.4 us
    ppermute x36 -> x29, waiting for transfers between devices: 131 us -> 64.6 us  [the longest x28 64.6 us: step(): self.flight = lax.ppermute(send, axis, bit_pairs(lax.axis_size(axis), bit))]
    ppermute x5, waiting for transfers between devices: 24.2 us -> 8.62 us  [gather_rows(): far = lax.ppermute(near, 'dp', bit_pairs(n_data, 0))]
    ppermute x5, waiting for transfers between devices: 4.36 us -> 19 us  [gather_rows(): near = lax.ppermute(send, 'fsdp', bit_pairs(n_group, 1))]
    convert_element_type x20, other arithmetic: 5.45 us -> 14.9 us  [add_low(): (first.astype(jnp.float32) + second.astype(jnp.float32)).astype(jnp.bfloa...]
    unnamed x123 -> x127, local copies, waits for them, and re-layouts: 8.1 us -> 15.1 us
    pallas_call x1 -> x3, Pallas kernels: 33.8 us -> 40 us  [attention_backward(): pl.pallas_call(kernel, grid=(count,), in_specs=[block(0), block(pairs), b...]
    dot_general x5, matrix products: 29.4 us -> 23.5 us  [rows_outer(): lax.dot_general(grad_rows, left, (((0,), (0,)), ((), ())), preferred_elem...]
    concatenate x11 -> x0, local copies, waits for them, and re-layouts: 5.77 us -> none  [the longest x10 5.68 us: gather_vectors(): joined = jnp.concatenate(members)[None, :]]
  transfers between devices with their start and end apart: 62 -> 55, of which waited for: 28 -> 21; matrix products, arithmetic and copies ran while one was open for 21% -> 40% of each run, Pallas kernels for 8% -> 21%
where the time goes in v3:
time: 408 us; the launch traced here: 403 us
  matrix products  106 us (26%)
  waiting for transfers between devices  93.9 us (23%)
  Pallas kernels  82.7 us (20%)
  starting transfers between devices  43.9 us (11%)
  local copies, waits for them, and re-layouts  37.4 us (9%)
  other arithmetic  36.7 us (9%)
    ppermute x28, waiting for transfers between devices, step(): self.flight = lax.ppermute(send, axis, bit_pairs(lax.axis_size(axis), bit))  64.6 us
    dot_general x5, matrix products, times_t(): lax.dot_general(left, weight, (((1,), (1,)), ((), ())), preferred_element...  54.6 us
    pallas_call x3, Pallas kernels, attention_backward(): pl.pallas_call(kernel, grid=(count,), in_specs=[block(0), block(pairs), b...  40 us
    dot_general x5, matrix products, times_n(): return jnp.dot(left, weight, preferred_element_type=jnp.float32)  27.5 us
    ppermute x28, starting transfers between devices, step(): self.flight = lax.ppermute(send, axis, bit_pairs(lax.axis_size(axis), bit))  24.7 us
    dot_general x5, matrix products, rows_outer(): lax.dot_general(grad_rows, left, (((0,), (0,)), ((), ())), preferred_elem...  23.5 us
    pallas_call x5, Pallas kernels, gather_rows(): pl.pallas_call(functools.partial(place_kernel, half), in_specs=[pl.BlockS...  21.5 us
    pallas_call x1, Pallas kernels, attention_forward(): pl.pallas_call(kernel, grid=(pairs,), in_specs=[block(0), block(pairs), b...  21.2 us
  transfers between devices with their start and end apart: 55, of which 21 were waited for; matrix products, arithmetic and copies ran while one was open for 40% of the time, Pallas kernels for 21%

profile of v3, /device:TPU:0, one launch (start us, length us, event | category | flops | bytes accessed | tf_op | source)
XLA Modules:
  0.0 402.5 jit_solution(12370436154306510653)
XLA Ops:
  2.5 3.0 collective-permute-start.5
  8.1 2.6 constant_dynamic-update-slice_fusion.1
  24.6 5.1 %collective-permute-done.1.far = bf16[96,1536]{1,0:T(8,128)(2,1)} collective-permute-done((bf16[96,1536]{1,0:T(8,128)(2,1)S(1)}, bf16[96,1536]{1,0:T(8,128)(2,1)}, u32[]{:S(2)}, u32[]{:S(2)}) %collective-permute-start.1) | collective-permute-done | bytes 294944 | tf_op jit(solution)/shard_map/place_skip_far/ppermute | solution.py:358
  38.6 3.7 place_skip.1
  42.4 5.1 %add_reduce_fusion = (f32[904]{0:T(1024)S(1)}, f32[904,768]{1,0:T(8,128)S(1)}) fusion(f32[768]{0:T(1024)S(1)} %add.287, bf16[904,1536]{1,0:T(8,128)(2,1)} %constant_dynamic-update-slice_fusion, bf16[768,1536]{1,0:T(8,128)(2,1)} %place_skip.1), kind=kOutput, calls=%fused_computation.50 | convolution fusion | flops 2134191232 | bytes 7920160 | tf_op jit(solution)/shard_map/dot_general | solution.py:25
  47.4 3.5 collective-permute-done.13.far
  55.6 3.0 place_proj.1
  59.2 8.2 %collective-permute-done.17.near = bf16[384,768]{1,0:T(8,128)(2,1)} collective-permute-done((bf16[384,768]{1,0:T(8,128)(2,1)}, bf16[384,768]{1,0:T(8,128)(2,1)}, u32[]{:S(2)}, u32[]{:S(2)}) %collective-permute-start.17) | collective-permute-done | bytes 589856 | tf_op jit(solution)/shard_map/place_hidden_near/ppermute | solution.py:354
  68.9 9.1 %collective-permute-done.22.near = bf16[96,3072]{1,0:T(8,128)(2,1)} collective-permute-done((bf16[96,3072]{1,0:T(8,128)(2,1)}, bf16[96,3072]{1,0:T(8,128)(2,1)}, u32[]{:S(2)}, u32[]{:S(2)}) %collective-permute-start.22) | collective-permute-done | bytes 589856 | tf_op jit(solution)/shard_map/place_output_near/ppermute | solution.py:354
  79.6 4.4 %place_qkv.1 = bf16[2304,768]{1,0:T(8,128)(2,1)} custom-call(s32[2]{0:T(128)} %pad_add_fusion.place_ref, bf16[576,768]{1,0:T(8,128)(2,1)} %own.2, bf16[288,768]{1,0:T(8,128)(2,1)} %copy-done.32, bf16[288,768]{1,0:T(8,128)(2,1)} %collective-permute-done.8.far, bf16[576,768]{1,0:T(8,128)(2,1)} %collective-permute-done.9.own_c, ...), custom_call_target="tpu_custom_call" | custom-call | tf_op jit(solution)/shard_map/place_qkv/pallas_call | solution.py:365
  84.1 8.0 %convolution_convert_fusion.q_ref.k_ref.v_ref = bf16[904,2304]{1,0:T(8,128)(2,1)} fusion(bf16[2304,768]{1,0:T(8,128)(2,1)} %place_qkv.1, f32[904,768]{1,0:T(8,128)S(1)} %get-tuple-element.155, f32[768]{0:T(1024)S(1)} %add.291, f32[768]{0:T(1024)S(1)} %mul.169, f32[904]{0:T(1024)S(1)} %fusion.32, f32[904]{0:T(1024)S(1)} %broadcast_multiply_fusion.2, ...), kind=kOutput, calls=%fused_computation.18 | convolution fusion | flops 3205453824 | bytes 10498112 | tf_op jit(solution)/shard_map/dot_general | solution.py:25
  92.1 21.2 %attention_forward.1 = (bf16[904,768]{1,0:T(8,128)(2,1)}, bf16[904,1536]{1,0:T(8,128)(2,1)}) custom-call(bf16[904,2304]{1,0:T(8,128)(2,1)} %convolution_convert_fusion.q_ref.k_ref.v_ref, bf16[904,2304]{1,0:T(8,128)(2,1)} %convolution_convert_fusion.q_ref.k_ref.v_ref, bf16[904,2304]{1,0:T(8,128)(2,1)} %convolution_convert_fusion.q_ref.k_ref.v_ref, ...), custom_call_target="tpu_custom_call" | custom-call | tf_op jit(solution)/shard_map/attention_forward/pallas_call | solution.py:197
  113.3 3.1 fusion.45
  119.9 5.3 %place_hidden.1 = bf16[3072,768]{1,0:T(8,128)(2,1)} custom-call(s32[2]{0:T(128)} %pad_add_fusion.place_ref, bf16[768,768]{1,0:T(8,128)(2,1)} %own.4, bf16[384,768]{1,0:T(8,128)(2,1)} %collective-permute-done.17.near, bf16[384,768]{1,0:T(8,128)(2,1)} %collective-permute-done.18.far, bf16[768,768]{1,0:T(8,128)(2,1)} %collective-permute-done.19.own_c, ...), custom_call_target="tpu_custom_call" | custom-call | tf_op jit(solution)/shard_map/place_hidden/pallas_call | solution.py:365
  125.2 32.7 %multiply_convert_fusion = (bf16[904,3072]{1,0:T(8,128)(2,1)S(1)}, f32[904,3072]{1,0:T(8,128)}, f32[904,3072]{1,0:T(8,128)}) fusion(f32[3072]{0:T(1024)S(1)} %add.304, bf16[3072,768]{1,0:T(8,128)(2,1)} %place_hidden.1, f32[904,768]{1,0:T(8,128)} %copy-done.9, f32[768]{0:T(1024)S(1)} %add.300, f32[768]{0:T(1024)S(1)} %mul.175, f32[904]{0:T(1024)S(1)} %fusion.33, ...), kind=kOutput, calls=%fused_computation.3 | convolution fusion | flops 4452366336 | bytes 35292224 | tf_op jit(solution)/shard_map/dot_general | solution.py:25
  157.9 5.4 %convolution_convert_fusion.2 = bf16[768,3072]{1,0:T(8,128)(2,1)S(1)} fusion(bf16[904,768]{1,0:T(8,128)(2,1)S(1)} %copy-done.6, bf16[904,3072]{1,0:T(8,128)(2,1)S(1)} %get-tuple-element.92), kind=kOutput, calls=%fused_computation.20 | convolution fusion | flops 4267966464 | bytes 11661312 | tf_op jit(solution)/shard_map/dot_general | solution.py:35
  163.3 2.1 copy-done.14
  168.8 5.1 %place_output.1 = bf16[768,3072]{1,0:T(8,128)(2,1)} custom-call(s32[2]{0:T(128)} %pad_add_fusion.place_ref, bf16[192,3072]{1,0:T(8,128)(2,1)} %own.5, bf16[96,3072]{1,0:T(8,128)(2,1)} %collective-permute-done.22.near, bf16[96,3072]{1,0:T(8,128)(2,1)} %copy-done.28, bf16[192,3072]{1,0:T(8,128)(2,1)} %collective-permute-done.24.own_c, ...), custom_call_target="tpu_custom_call" | custom-call | tf_op jit(solution)/shard_map/place_output/pallas_call | solution.py:365
  174.0 13.7 %fusion.35 = (bf16[3072]{0:T(1024)(128)(2,1)S(1)}, bf16[904,3072]{1,0:T(8,128)(2,1)S(1)}) fusion(f32[904,3072]{1,0:T(8,128)} %get-tuple-element.139, f32[904,3072]{1,0:T(8,128)} %get-tuple-element.158, f32[3072]{0:T(1024)S(1)} %add.304, bf16[904,768]{1,0:T(8,128)(2,1)S(1)} %copy-done.6, bf16[768,3072]{1,0:T(8,128)(2,1)} %place_output.1), kind=kOutput, calls=%fused_computation.195 | convolution fusion | flops 4310037504 | bytes 33896448 | tf_op jit(solution)/shard_map/dot_general | solution.py:31
  187.8 2.7 fusion.6
  191.2 6.8 %convolution_convert_fusion.1 = bf16[3072,768]{1,0:T(8,128)(2,1)S(1)} fusion(bf16[904,3072]{1,0:T(8,128)(2,1)S(1)} %get-tuple-element.69, f32[904,768]{1,0:T(8,128)S(1)} %copy-done.10, f32[768]{0:T(1024)S(1)} %copy-done.52, f32[768]{0:T(1024)S(1)} %mul.175, f32[904]{0:T(1024)S(1)} %fusion.33, f32[904]{0:T(1024)S(1)} %broadcast_multiply_fusion.1), kind=kOutput, calls=%fused_computation.19 | convolution fusion | flops 4271437824 | bytes 13063232 | tf_op jit(solution)/shard_map/dot_general | solution.py:35
  198.0 5.6 %multiply_reduce_fusion = (bf16[768]{0:T(1024)(128)(2,1)}, f32[904]{0:T(1024)S(1)}, bf16[768]{0:T(1024)(128)(2,1)}, f32[904,768]{1,0:T(8,128)S(1)}) fusion(f32[904,768]{1,0:T(8,128)S(1)} %copy-done.10, f32[904]{0:T(1024)S(1)} %fusion.33, f32[904]{0:T(1024)S(1)} %broadcast_multiply_fusion.1, f32[768]{0:T(1024)S(1)} %mul.175, ...), kind=kOutput, calls=%fused_computation.36 | convolution fusion | flops 4271158784 | bytes 15843936 | tf_op jit(solution)/shard_map/dot_general | solution.py:31
  211.5 2.4 convolution_convert_fusion.6.go_ref
  213.9 5.0 %collective-permute-done.28 = bf16[1,192,3072]{2,1,0:T(8,128)(2,1)S(1)} collective-permute-done((bf16[1,192,3072]{2,1,0:T(8,128)(2,1)S(1)}, bf16[1,192,3072]{2,1,0:T(8,128)(2,1)S(1)}, u32[]{:S(2)}, u32[]{:S(2)}) %collective-permute-start.28) | collective-permute-done | bytes 1179680 | tf_op jit(solution)/shard_map/out_2/ppermute | solution.py:107
  220.7 13.6 %attention_backward.3.rest_0_ = bf16[904,2304]{1,0:T(8,128)(2,1)} custom-call(bf16[904,2304]{1,0:T(8,128)(2,1)} %convolution_convert_fusion.q_ref.k_ref.v_ref, bf16[904,2304]{1,0:T(8,128)(2,1)} %convolution_convert_fusion.q_ref.k_ref.v_ref, bf16[904,2304]{1,0:T(8,128)(2,1)} %convolution_convert_fusion.q_ref.k_ref.v_ref, ...), custom_call_target="tpu_custom_call" | custom-call | tf_op jit(solution)/shard_map/bwd_a0/attention_backward/pallas_call | solution.py:291
  238.1 2.6 add_convert_fusion.1
  244.1 13.1 %attention_backward.4.rest_0_ = bf16[904,2304]{1,0:T(8,128)(2,1)} custom-call(bf16[904,2304]{1,0:T(8,128)(2,1)} %convolution_convert_fusion.q_ref.k_ref.v_ref, bf16[904,2304]{1,0:T(8,128)(2,1)} %convolution_convert_fusion.q_ref.k_ref.v_ref, bf16[904,2304]{1,0:T(8,128)(2,1)} %convolution_convert_fusion.q_ref.k_ref.v_ref, ...), custom_call_target="tpu_custom_call", output_to_operand_aliasing={{}: (7, {})} | custom-call | tf_op jit(solution)/shard_map/bwd_a1/attention_backward/pallas_call | solution.py:291
  257.3 2.7 collective-permute-start.32
  260.3 13.4 %attention_backward.5 = bf16[904,2304]{1,0:T(8,128)(2,1)} custom-call(bf16[904,2304]{1,0:T(8,128)(2,1)} %convolution_convert_fusion.q_ref.k_ref.v_ref, bf16[904,2304]{1,0:T(8,128)(2,1)} %convolution_convert_fusion.q_ref.k_ref.v_ref, bf16[904,2304]{1,0:T(8,128)(2,1)} %convolution_convert_fusion.q_ref.k_ref.v_ref, ...), custom_call_target="tpu_custom_call", output_to_operand_aliasing={{}: (7, {})} | custom-call | tf_op jit(solution)/shard_map/bwd_a2/attention_backward/pallas_call | solution.py:291
  276.4 2.2 add_convert_fusion.2
  280.0 5.2 %convolution_convert_fusion.3 = bf16[2304,768]{1,0:T(8,128)(2,1)S(1)} fusion(bf16[904,2304]{1,0:T(8,128)(2,1)S(1)} %copy-done, f32[904,768]{1,0:T(8,128)S(1)} %copy-done.2, f32[768]{0:T(1024)S(1)} %copy-done.50, f32[768]{0:T(1024)S(1)} %copy-done.43, f32[904]{0:T(1024)S(1)} %copy-done.45, f32[904]{0:T(1024)S(1)} %copy-done.39, f32[768]{0:T(1024)S(1)} %copy-done.37), kind=kOutput, calls=%fused_computation.21 | convolution fusion | flops 3205140480 | bytes 10498112 | tf_op jit(solution)/shard_map/dot_general | solution.py:35
  287.4 3.5 fusion.46
  290.8 7.3 %collective-permute-done.36 = bf16[1,480,768]{2,1,0:T(8,128)(2,1)S(1)} collective-permute-done((bf16[1,480,768]{2,1,0:T(8,128)(2,1)S(1)}, bf16[1,480,768]{2,1,0:T(8,128)(2,1)S(1)}, u32[]{:S(2)}, u32[]{:S(2)}) %collective-permute-start.36) | collective-permute-done | bytes 737312 | tf_op jit(solution)/shard_map/mlp_3/ppermute | solution.py:107
  308.5 4.7 %collective-permute-start.39 = (bf16[1,240,768]{2,1,0:T(8,128)(2,1)}, bf16[1,240,768]{2,1,0:T(8,128)(2,1)}, u32[]{:S(2)}, u32[]{:S(2)}) collective-permute-start(bf16[1,240,768]{2,1,0:T(8,128)(2,1)} %fusion.17), channel_id=1, source_target_pairs={{0,16},{4,20},{8,24},{12,28},{16,0},{20,4},{24,8},{28,12},{1,17},{... | collective-permute-start | bytes 1105928 | tf_op jit(solution)/shard_map/mlp_5/ppermute | solution.py:107
  313.8 4.7 %convolution_convert_fusion.5 = bf16[768,1536]{1,0:T(8,128)(2,1)S(1)} fusion(bf16[904,768]{1,0:T(8,128)(2,1)S(1)} %get-tuple-element.88, bf16[904,1536]{1,0:T(8,128)(2,1)} %constant_dynamic-update-slice_fusion), kind=kOutput, calls=%fused_computation.31 | convolution fusion | flops 2133983232 | bytes 6524928 | tf_op jit(solution)/shard_map/dot_general | solution.py:35
  319.3 2.6 collective-permute-done.39
  323.9 2.3 convolution_convert_fusion.4
  328.0 3.6 collective-permute-done.40
  333.7 2.1 collective-permute-start.44
  337.7 5.7 %add_convert_fusion.3 = bf16[904,768]{1,0:T(8,128)(2,1)} fusion(f32[904,768]{1,0:T(8,128)S(1)} %copy-done.11, bf16[904,3072]{1,0:T(8,128)(2,1)S(1)} %bitcast.226, bf16[768,3072]{1,0:T(8,128)(2,1)S(1)} %bitcast.188, f32[768]{0:T(1024)S(1)} %add.331), kind=kOutput, calls=%fused_computation.35 | convolution fusion | flops 4267689984 | bytes 14441472 | tf_op jit(solution)/shard_map/dot_general | solution.py:25
  343.4 13.5 %collective-permute-done.44 = bf16[1,288,768]{2,1,0:T(8,128)(2,1)S(1)} collective-permute-done((bf16[1,288,768]{2,1,0:T(8,128)(2,1)S(1)}, bf16[1,288,768]{2,1,0:T(8,128)(2,1)S(1)}, u32[]{:S(2)}, u32[]{:S(2)}) %collective-permute-start.44) | collective-permute-done | bytes 442400 | tf_op jit(solution)/shard_map/qkv_3/ppermute | solution.py:107
  357.5 3.0 convert_multiply_fusion.1
  360.5 6.5 %collective-permute-done.46 = bf16[1,144,768]{2,1,0:T(8,128)(2,1)S(1)} collective-permute-done((bf16[1,144,768]{2,1,0:T(8,128)(2,1)S(1)}, bf16[1,144,768]{2,1,0:T(8,128)(2,1)S(1)}, u32[]{:S(2)}, u32[]{:S(2)}) %collective-permute-start.46) | collective-permute-done | bytes 221216 | tf_op jit(solution)/shard_map/qkv_4/ppermute | solution.py:107
  369.2 9.1 %collective-permute-done.48 = bf16[1,144,768]{2,1,0:T(8,128)(2,1)S(1)} collective-permute-done((bf16[1,144,768]{2,1,0:T(8,128)(2,1)S(1)}, bf16[1,144,768]{2,1,0:T(8,128)(2,1)S(1)}, u32[]{:S(2)}, u32[]{:S(2)}) %collective-permute-start.48) | collective-permute-done | bytes 221216 | tf_op jit(solution)/shard_map/qkv_5/ppermute | solution.py:107
  383.0 3.0 collective-permute-done.51
  387.8 4.1 %collective-permute-done.49 = bf16[1,48,1664]{2,1,0:T(8,128)(2,1)S(1)} collective-permute-done((bf16[1,48,1664]{2,1,0:T(8,128)(2,1)S(1)}, bf16[1,48,1664]{2,1,0:T(8,128)(2,1)S(1)}, u32[]{:S(2)}, u32[]{:S(2)}) %collective-permute-start.49) | collective-permute-done | bytes 159776 | tf_op jit(solution)/shard_map/last_6/ppermute | solution.py:107
  392.6 2.8 collective-permute-done.52
  396.9 2.1 collective-permute-done.50
  (339 shorter events, 100.2 us)
Async XLA Ops:
  2.5 14.0 %collective-permute-start.5 = (bf16[1,16,192]{2,1,0:T(8,128)(2,1)S(1)}, bf16[1,16,192]{2,1,0:T(8,128)(2,1)S(1)}, u32[]{:S(2)}, u32[]{:S(2)}) collective-permute-start(bf16[1,16,192]{2,1,0:T(8,128)(2,1)S(1)} %bitcast.222), channel_id=1, source_target_pairs={{0,2},{1,3},{2,0},{3,1},{4,6},{5,7},{6,4},{7,5},{8,10},{9,11},{10,... | collective-permute-start | bytes 18440 | tf_op jit(solution)/shard_map/ppermute | solution.py:386
  5.5 30.2 %collective-permute-start.2 = (bf16[192,1536]{1,0:T(8,128)(2,1)}, bf16[192,1536]{1,0:T(8,128)(2,1)}, u32[]{:S(2)}, u32[]{:S(2)}) collective-permute-start(bf16[192,1536]{1,0:T(8,128)(2,1)} %own.1), channel_id=1, source_target_pairs={{0,1},{1,0},{2,3},{3,2},{4,5},{5,4},{6,7},{7,6},{8,9},{9,8},{10,11... | collective-permute-start | bytes 1769480 | tf_op jit(solution)/shard_map/place_skip_own_c/ppermute | solution.py:356
  6.5 10.5 %collective-permute-start = (bf16[96,1536]{1,0:T(8,128)(2,1)S(1)}, bf16[96,1536]{1,0:T(8,128)(2,1)S(1)}, u32[]{:S(2)}, u32[]{:S(2)}) collective-permute-start(bf16[96,1536]{1,0:T(8,128)(2,1)S(1)} %constant_dynamic-slice_fusion.8), channel_id=1, source_target_pairs={{0,2},{1,3},{2,0},{3,1},{4,6},{5,7},{6,4},{7,5},{8,10},{9,11},{10,... | collective-permute-start | bytes 884744 | tf_op jit(solution)/shard_map/place_skip_near/ppermute | solution.py:354
  18.9 12.5 %collective-permute-start.7 = (bf16[288,768]{1,0:T(8,128)(2,1)}, bf16[288,768]{1,0:T(8,128)(2,1)S(1)}, u32[]{:S(2)}, u32[]{:S(2)}) collective-permute-start(bf16[288,768]{1,0:T(8,128)(2,1)} %constant_dynamic-slice_fusion.7), channel_id=1, source_target_pairs={{0,2},{1,3},{2,0},{3,1},{4,6},{5,7},{6,4},{7,5},{8,10},{9,11},{10,... | collective-permute-start | bytes 1327112 | tf_op jit(solution)/shard_map/place_qkv_near/ppermute | solution.py:354
  20.7 9.1 %collective-permute-start.1 = (bf16[96,1536]{1,0:T(8,128)(2,1)S(1)}, bf16[96,1536]{1,0:T(8,128)(2,1)}, u32[]{:S(2)}, u32[]{:S(2)}) collective-permute-start(bf16[96,1536]{1,0:T(8,128)(2,1)S(1)} %collective-permute-done.near), channel_id=1, source_target_pairs={{0,4},{4,0},{8,12},{12,8},{16,20},{20,16},{24,28},{28,24},{1,5},{5... | collective-permute-start | bytes 884744 | tf_op jit(solution)/shard_map/place_skip_far/ppermute | solution.py:358
  24.1 34.7 %collective-permute-start.9 = (bf16[576,768]{1,0:T(8,128)(2,1)}, bf16[576,768]{1,0:T(8,128)(2,1)}, u32[]{:S(2)}, u32[]{:S(2)}) collective-permute-start(bf16[576,768]{1,0:T(8,128)(2,1)} %own.2), channel_id=1, source_target_pairs={{0,1},{1,0},{2,3},{3,2},{4,5},{5,4},{6,7},{7,6},{8,9},{9,8},{10,11... | collective-permute-start | bytes 2654216 | tf_op jit(solution)/shard_map/place_qkv_own_c/ppermute | solution.py:356
  24.1 10.9 %collective-permute-start.3 = (bf16[96,1536]{1,0:T(8,128)(2,1)S(1)}, bf16[96,1536]{1,0:T(8,128)(2,1)S(1)}, u32[]{:S(2)}, u32[]{:S(2)}) collective-permute-start(bf16[96,1536]{1,0:T(8,128)(2,1)S(1)} %collective-permute-done.near), channel_id=1, source_target_pairs={{0,1},{1,0},{2,3},{3,2},{4,5},{5,4},{6,7},{7,6},{8,9},{9,8},{10,11... | collective-permute-start | bytes 884744 | tf_op jit(solution)/shard_map/place_skip_near_c/ppermute | solution.py:360
  29.8 8.9 %collective-permute-start.4 = (bf16[96,1536]{1,0:T(8,128)(2,1)}, bf16[96,1536]{1,0:T(8,128)(2,1)}, u32[]{:S(2)}, u32[]{:S(2)}) collective-permute-start(bf16[96,1536]{1,0:T(8,128)(2,1)} %collective-permute-done.1.far), channel_id=1, source_target_pairs={{0,1},{1,0},{2,3},{3,2},{4,5},{5,4},{6,7},{7,6},{8,9},{9,8},{10,11... | collective-permute-start | bytes 884744 | tf_op jit(solution)/shard_map/place_skip_far_c/ppermute | solution.py:362
  35.0 17.9 %collective-permute-start.14 = (bf16[192,768]{1,0:T(8,128)(2,1)S(1)}, bf16[192,768]{1,0:T(8,128)(2,1)}, u32[]{:S(2)}, u32[]{:S(2)}) collective-permute-start(bf16[192,768]{1,0:T(8,128)(2,1)S(1)} %copy-done.27), channel_id=1, source_target_pairs={{0,1},{1,0},{2,3},{3,2},{4,5},{5,4},{6,7},{7,6},{8,9},{9,8},{10,11... | collective-permute-start | bytes 884744 | tf_op jit(solution)/shard_map/place_proj_own_c/ppermute | solution.py:356
  35.7 18.9 %collective-permute-start.8 = (bf16[288,768]{1,0:T(8,128)(2,1)S(1)}, bf16[288,768]{1,0:T(8,128)(2,1)}, u32[]{:S(2)}, u32[]{:S(2)}) collective-permute-start(bf16[288,768]{1,0:T(8,128)(2,1)S(1)} %collective-permute-done.7.near), channel_id=1, source_target_pairs={{0,4},{4,0},{8,12},{12,8},{16,20},{20,16},{24,28},{28,24},{1,5},{5... | collective-permute-start | bytes 1327112 | tf_op jit(solution)/shard_map/place_qkv_far/ppermute | solution.py:358
  37.3 13.6 %collective-permute-start.13 = (bf16[96,768]{1,0:T(8,128)(2,1)}, bf16[96,768]{1,0:T(8,128)(2,1)}, u32[]{:S(2)}, u32[]{:S(2)}) collective-permute-start(bf16[96,768]{1,0:T(8,128)(2,1)} %collective-permute-done.12.near), channel_id=1, source_target_pairs={{0,4},{4,0},{8,12},{12,8},{16,20},{20,16},{24,28},{28,24},{1,5},{5... | collective-permute-start | bytes 442376 | tf_op jit(solution)/shard_map/place_proj_far/ppermute | solution.py:358
  38.6 12.6 %collective-permute-start.15 = (bf16[96,768]{1,0:T(8,128)(2,1)}, bf16[96,768]{1,0:T(8,128)(2,1)}, u32[]{:S(2)}, u32[]{:S(2)}) collective-permute-start(bf16[96,768]{1,0:T(8,128)(2,1)} %collective-permute-done.12.near), channel_id=1, source_target_pairs={{0,1},{1,0},{2,3},{3,2},{4,5},{5,4},{6,7},{7,6},{8,9},{9,8},{10,11... | collective-permute-start | bytes 442376 | tf_op jit(solution)/shard_map/place_proj_near_c/ppermute | solution.py:360
  50.9 16.5 %collective-permute-start.17 = (bf16[384,768]{1,0:T(8,128)(2,1)}, bf16[384,768]{1,0:T(8,128)(2,1)}, u32[]{:S(2)}, u32[]{:S(2)}) collective-permute-start(bf16[384,768]{1,0:T(8,128)(2,1)} %constant_dynamic-slice_fusion.5), channel_id=1, source_target_pairs={{0,2},{1,3},{2,0},{3,1},{4,6},{5,7},{6,4},{7,5},{8,10},{9,11},{10,... | collective-permute-start | bytes 1769480 | tf_op jit(solution)/shard_map/place_hidden_near/ppermute | solution.py:354
  51.2 26.8 %collective-permute-start.22 = (bf16[96,3072]{1,0:T(8,128)(2,1)}, bf16[96,3072]{1,0:T(8,128)(2,1)}, u32[]{:S(2)}, u32[]{:S(2)}) collective-permute-start(bf16[96,3072]{1,0:T(8,128)(2,1)} %constant_dynamic-slice_fusion.4), channel_id=1, source_target_pairs={{0,2},{1,3},{2,0},{3,1},{4,6},{5,7},{6,4},{7,5},{8,10},{9,11},{10,... | collective-permute-start | bytes 1769480 | tf_op jit(solution)/shard_map/place_output_near/ppermute | solution.py:354
  54.7 23.4 %collective-permute-start.11 = (bf16[288,768]{1,0:T(8,128)(2,1)}, bf16[288,768]{1,0:T(8,128)(2,1)}, u32[]{:S(2)}, u32[]{:S(2)}) collective-permute-start(bf16[288,768]{1,0:T(8,128)(2,1)} %collective-permute-done.8.far), channel_id=1, source_target_pairs={{0,1},{1,0},{2,3},{3,2},{4,5},{5,4},{6,7},{7,6},{8,9},{9,8},{10,11... | collective-permute-start | bytes 1327112 | tf_op jit(solution)/shard_map/place_qkv_far_c/ppermute | solution.py:362
  58.6 60.4 %collective-permute-start.19 = (bf16[768,768]{1,0:T(8,128)(2,1)}, bf16[768,768]{1,0:T(8,128)(2,1)}, u32[]{:S(2)}, u32[]{:S(2)}) collective-permute-start(bf16[768,768]{1,0:T(8,128)(2,1)} %own.4), channel_id=1, source_target_pairs={{0,1},{1,0},{2,3},{3,2},{4,5},{5,4},{6,7},{7,6},{8,9},{9,8},{10,11... | collective-permute-start | bytes 3538952 | tf_op jit(solution)/shard_map/place_hidden_own_c/ppermute | solution.py:356
  58.8 108.4 %collective-permute-start.24 = (bf16[192,3072]{1,0:T(8,128)(2,1)}, bf16[192,3072]{1,0:T(8,128)(2,1)}, u32[]{:S(2)}, u32[]{:S(2)}) collective-permute-start(bf16[192,3072]{1,0:T(8,128)(2,1)} %own.5), channel_id=1, source_target_pairs={{0,1},{1,0},{2,3},{3,2},{4,5},{5,4},{6,7},{7,6},{8,9},{9,8},{10,11... | collective-permute-start | bytes 3538952 | tf_op jit(solution)/shard_map/place_output_own_c/ppermute | solution.py:356
  67.4 49.1 %collective-permute-start.18 = (bf16[384,768]{1,0:T(8,128)(2,1)}, bf16[384,768]{1,0:T(8,128)(2,1)}, u32[]{:S(2)}, u32[]{:S(2)}) collective-permute-start(bf16[384,768]{1,0:T(8,128)(2,1)} %collective-permute-done.17.near), channel_id=1, source_target_pairs={{0,4},{4,0},{8,12},{12,8},{16,20},{20,16},{24,28},{28,24},{1,5},{5... | collective-permute-start | bytes 1769480 | tf_op jit(solution)/shard_map/place_hidden_far/ppermute | solution.py:358
  78.0 40.4 %collective-permute-start.20 = (bf16[384,768]{1,0:T(8,128)(2,1)}, bf16[384,768]{1,0:T(8,128)(2,1)}, u32[]{:S(2)}, u32[]{:S(2)}) collective-permute-start(bf16[384,768]{1,0:T(8,128)(2,1)} %collective-permute-done.17.near), channel_id=1, source_target_pairs={{0,1},{1,0},{2,3},{3,2},{4,5},{5,4},{6,7},{7,6},{8,9},{9,8},{10,11... | collective-permute-start | bytes 1769480 | tf_op jit(solution)/shard_map/place_hidden_near_c/ppermute | solution.py:360
  78.0 40.7 %collective-permute-start.23 = (bf16[96,3072]{1,0:T(8,128)(2,1)}, bf16[96,3072]{1,0:T(8,128)(2,1)S(1)}, u32[]{:S(2)}, u32[]{:S(2)}) collective-permute-start(bf16[96,3072]{1,0:T(8,128)(2,1)} %collective-permute-done.22.near), channel_id=1, source_target_pairs={{0,4},{4,0},{8,12},{12,8},{16,20},{20,16},{24,28},{28,24},{1,5},{5... | collective-permute-start | bytes 1769480 | tf_op jit(solution)/shard_map/place_output_far/ppermute | solution.py:358
  118.5 48.8 %collective-permute-start.25 = (bf16[96,3072]{1,0:T(8,128)(2,1)}, bf16[96,3072]{1,0:T(8,128)(2,1)S(1)}, u32[]{:S(2)}, u32[]{:S(2)}) collective-permute-start(bf16[96,3072]{1,0:T(8,128)(2,1)} %collective-permute-done.22.near), channel_id=1, source_target_pairs={{0,1},{1,0},{2,3},{3,2},{4,5},{5,4},{6,7},{7,6},{8,9},{9,8},{10,11... | collective-permute-start | bytes 1769480 | tf_op jit(solution)/shard_map/place_output_near_c/ppermute | solution.py:360
  118.7 48.5 %collective-permute-start.26 = (bf16[96,3072]{1,0:T(8,128)(2,1)S(1)}, bf16[96,3072]{1,0:T(8,128)(2,1)S(1)}, u32[]{:S(2)}, u32[]{:S(2)}) collective-permute-start(bf16[96,3072]{1,0:T(8,128)(2,1)S(1)} %collective-permute-done.23.far), channel_id=1, source_target_pairs={{0,1},{1,0},{2,3},{3,2},{4,5},{5,4},{6,7},{7,6},{8,9},{9,8},{10,11... | collective-permute-start | bytes 1769480 | tf_op jit(solution)/shard_map/place_output_far_c/ppermute | solution.py:362
  167.0 20.7 %collective-permute-start.27 = (bf16[2,192,3072]{2,1,0:T(8,128)(2,1)}, bf16[2,192,3072]{2,1,0:T(8,128)(2,1)}, u32[]{:S(2)}, u32[]{:S(2)}) collective-permute-start(bf16[2,192,3072]{2,1,0:T(8,128)(2,1)} %dynamic-slice_bitcast_fusion.2), channel_id=1, source_target_pairs={{0,1},{1,0},{2,3},{3,2},{4,5},{5,4},{6,7},{7,6},{8,9},{9,8},{10,11... | collective-permute-start | bytes 7077896 | tf_op jit(solution)/shard_map/out_1/ppermute | solution.py:107
  190.6 28.3 %collective-permute-start.28 = (bf16[1,192,3072]{2,1,0:T(8,128)(2,1)S(1)}, bf16[1,192,3072]{2,1,0:T(8,128)(2,1)S(1)}, u32[]{:S(2)}, u32[]{:S(2)}) collective-permute-start(bf16[1,192,3072]{2,1,0:T(8,128)(2,1)S(1)} %constant_dynamic-slice_fusion.3), channel_id=1, source_target_pairs={{0,2},{1,3},{2,0},{3,1},{4,6},{5,7},{6,4},{7,5},{8,10},{9,11},{10,... | collective-permute-start | bytes 3538952 | tf_op jit(solution)/shard_map/out_2/ppermute | solution.py:107
  211.5 26.6 %collective-permute-start.31 = (bf16[2,960,768]{2,1,0:T(8,128)(2,1)}, bf16[2,960,768]{2,1,0:T(8,128)(2,1)}, u32[]{:S(2)}, u32[]{:S(2)}) collective-permute-start(bf16[2,960,768]{2,1,0:T(8,128)(2,1)} %pad_maximum_fusion), channel_id=1, source_target_pairs={{0,1},{1,0},{2,3},{3,2},{4,5},{5,4},{6,7},{7,6},{8,9},{9,8},{10,11... | collective-permute-start | bytes 8847368 | tf_op jit(solution)/shard_map/mlp_1/ppermute | solution.py:107
  220.2 15.0 %collective-permute-start.29 = (bf16[1,96,3072]{2,1,0:T(8,128)(2,1)}, bf16[1,96,3072]{2,1,0:T(8,128)(2,1)}, u32[]{:S(2)}, u32[]{:S(2)}) collective-permute-start(bf16[1,96,3072]{2,1,0:T(8,128)(2,1)} %dynamic-slice_bitcast_fusion.7), channel_id=1, source_target_pairs={{0,4},{4,0},{8,12},{12,8},{16,20},{20,16},{24,28},{28,24},{1,5},{5... | collective-permute-start | bytes 1769480 | tf_op jit(solution)/shard_map/out_3/ppermute | solution.py:107
  236.4 20.8 %collective-permute-start.30 = (bf16[1,48,3072]{2,1,0:T(8,128)(2,1)S(1)}, bf16[1,48,3072]{2,1,0:T(8,128)(2,1)S(1)}, u32[]{:S(2)}, u32[]{:S(2)}) collective-permute-start(bf16[1,48,3072]{2,1,0:T(8,128)(2,1)S(1)} %dynamic-slice_bitcast_fusion.11), channel_id=1, source_target_pairs={{0,8},{4,12},{8,0},{12,4},{16,24},{20,28},{24,16},{28,20},{1,9},{5... | collective-permute-start | bytes 884744 | tf_op jit(solution)/shard_map/out_4/ppermute | solution.py:107
  243.5 32.9 %collective-permute-start.33 = (bf16[1,960,768]{2,1,0:T(8,128)(2,1)}, bf16[1,960,768]{2,1,0:T(8,128)(2,1)}, u32[]{:S(2)}, u32[]{:S(2)}) collective-permute-start(bf16[1,960,768]{2,1,0:T(8,128)(2,1)} %constant_dynamic-slice_fusion.2), channel_id=1, source_target_pairs={{0,2},{1,3},{2,0},{3,1},{4,6},{5,7},{6,4},{7,5},{8,10},{9,11},{10,... | collective-permute-start | bytes 4423688 | tf_op jit(solution)/shard_map/mlp_2/ppermute | solution.py:107
  257.3 16.4 %collective-permute-start.32 = (bf16[1,48,3072]{2,1,0:T(8,128)(2,1)S(1)}, bf16[1,48,3072]{2,1,0:T(8,128)(2,1)S(1)}, u32[]{:S(2)}, u32[]{:S(2)}) collective-permute-start(bf16[1,48,3072]{2,1,0:T(8,128)(2,1)S(1)} %fusion.19), channel_id=1, source_target_pairs={{0,16},{4,20},{8,24},{12,28},{16,0},{20,4},{24,8},{28,12},{1,17},{... | collective-permute-start | bytes 884744 | tf_op jit(solution)/shard_map/out_5/ppermute | solution.py:107
  273.9 11.3 %collective-permute-start.34 = (bf16[1,48,3072]{2,1,0:T(8,128)(2,1)S(1)}, bf16[1,48,3072]{2,1,0:T(8,128)(2,1)S(1)}, u32[]{:S(2)}, u32[]{:S(2)}) collective-permute-start(bf16[1,48,3072]{2,1,0:T(8,128)(2,1)S(1)} %add_convert_fusion.11), channel_id=1, source_target_pairs={{0,8},{4,12},{8,0},{12,4},{16,24},{20,28},{24,16},{28,20},{1,9},{5... | collective-permute-start | bytes 884744 | tf_op jit(solution)/shard_map/out_6/ppermute | solution.py:107
  278.7 19.4 %collective-permute-start.36 = (bf16[1,480,768]{2,1,0:T(8,128)(2,1)S(1)}, bf16[1,480,768]{2,1,0:T(8,128)(2,1)S(1)}, u32[]{:S(2)}, u32[]{:S(2)}) collective-permute-start(bf16[1,480,768]{2,1,0:T(8,128)(2,1)S(1)} %dynamic-slice_bitcast_fusion.4), channel_id=1, source_target_pairs={{0,4},{4,0},{8,12},{12,8},{16,20},{20,16},{24,28},{28,24},{1,5},{5... | collective-permute-start | bytes 2211848 | tf_op jit(solution)/shard_map/mlp_3/ppermute | solution.py:107
  285.3 14.1 %collective-permute-start.35 = (bf16[2,576,768]{2,1,0:T(8,128)(2,1)S(1)}, bf16[2,576,768]{2,1,0:T(8,128)(2,1)S(1)}, u32[]{:S(2)}, u32[]{:S(2)}) collective-permute-start(bf16[2,576,768]{2,1,0:T(8,128)(2,1)S(1)} %dynamic-slice_bitcast_fusion.3), channel_id=1, source_target_pairs={{0,1},{1,0},{2,3},{3,2},{4,5},{5,4},{6,7},{7,6},{8,9},{9,8},{10,11... | collective-permute-start | bytes 5308424 | tf_op jit(solution)/shard_map/qkv_1/ppermute | solution.py:107
  286.3 57.1 %collective-permute-start.54 = (bf16[1,96,3072]{2,1,0:T(8,128)(2,1)}, bf16[1,96,3072]{2,1,0:T(8,128)(2,1)}, u32[]{:S(2)}, u32[]{:S(2)}) collective-permute-start(bf16[1,96,3072]{2,1,0:T(8,128)(2,1)} %maximum_select_fusion.6), channel_id=1, source_target_pairs={{0,4},{4,0},{8,12},{12,8},{16,20},{20,16},{24,28},{28,24},{1,5},{5... | collective-permute-start | bytes 1769480 | tf_op jit(solution)/shard_map/out_7/ppermute | solution.py:107
  298.3 9.4 %collective-permute-start.37 = (bf16[1,240,768]{2,1,0:T(8,128)(2,1)S(1)}, bf16[1,240,768]{2,1,0:T(8,128)(2,1)S(1)}, u32[]{:S(2)}, u32[]{:S(2)}) collective-permute-start(bf16[1,240,768]{2,1,0:T(8,128)(2,1)S(1)} %dynamic-slice_bitcast_fusion.9), channel_id=1, source_target_pairs={{0,8},{4,12},{8,0},{12,4},{16,24},{20,28},{24,16},{28,20},{1,9},{5... | collective-permute-start | bytes 1105928 | tf_op jit(solution)/shard_map/mlp_4/ppermute | solution.py:107
  308.5 13.4 %collective-permute-start.39 = (bf16[1,240,768]{2,1,0:T(8,128)(2,1)}, bf16[1,240,768]{2,1,0:T(8,128)(2,1)}, u32[]{:S(2)}, u32[]{:S(2)}) collective-permute-start(bf16[1,240,768]{2,1,0:T(8,128)(2,1)} %fusion.17), channel_id=1, source_target_pairs={{0,16},{4,20},{8,24},{12,28},{16,0},{20,4},{24,8},{28,12},{1,17},{... | collective-permute-start | bytes 1105928 | tf_op jit(solution)/shard_map/mlp_5/ppermute | solution.py:107
  313.2 19.0 %collective-permute-start.41 = (bf16[1,576,768]{2,1,0:T(8,128)(2,1)}, bf16[1,576,768]{2,1,0:T(8,128)(2,1)}, u32[]{:S(2)}, u32[]{:S(2)}) collective-permute-start(bf16[1,576,768]{2,1,0:T(8,128)(2,1)} %constant_dynamic-slice_fusion.1), channel_id=1, source_target_pairs={{0,2},{1,3},{2,0},{3,1},{4,6},{5,7},{6,4},{7,5},{8,10},{9,11},{10,... | collective-permute-start | bytes 2654216 | tf_op jit(solution)/shard_map/qkv_2/ppermute | solution.py:107
  319.2 16.5 %collective-permute-start.38 = (bf16[2,192,1664]{2,1,0:T(8,128)(2,1)S(1)}, bf16[2,192,1664]{2,1,0:T(8,128)(2,1)S(1)}, u32[]{:S(2)}, u32[]{:S(2)}) collective-permute-start(bf16[2,192,1664]{2,1,0:T(8,128)(2,1)S(1)} %fusion.12), channel_id=1, source_target_pairs={{0,1},{1,0},{2,3},{3,2},{4,5},{5,4},{6,7},{7,6},{8,9},{9,8},{10,11... | collective-permute-start | bytes 3833864 | tf_op jit(solution)/shard_map/last_1/ppermute | solution.py:107
  323.8 7.8 %collective-permute-start.40 = (bf16[1,240,768]{2,1,0:T(8,128)(2,1)S(1)}, bf16[1,240,768]{2,1,0:T(8,128)(2,1)S(1)}, u32[]{:S(2)}, u32[]{:S(2)}) collective-permute-start(bf16[1,240,768]{2,1,0:T(8,128)(2,1)S(1)} %add_convert_fusion.10), channel_id=1, source_target_pairs={{0,8},{4,12},{8,0},{12,4},{16,24},{20,28},{24,16},{28,20},{1,9},{5... | collective-permute-start | bytes 1105928 | tf_op jit(solution)/shard_map/mlp_6/ppermute | solution.py:107
  331.9 28.7 %collective-permute-start.53 = (bf16[1,480,768]{2,1,0:T(8,128)(2,1)S(1)}, bf16[1,480,768]{2,1,0:T(8,128)(2,1)S(1)}, u32[]{:S(2)}, u32[]{:S(2)}) collective-permute-start(bf16[1,480,768]{2,1,0:T(8,128)(2,1)S(1)} %maximum_select_fusion.3), channel_id=1, source_target_pairs={{0,4},{4,0},{8,12},{12,8},{16,20},{20,16},{24,28},{28,24},{1,5},{5... | collective-permute-start | bytes 2211848 | tf_op jit(solution)/shard_map/mlp_7/ppermute | solution.py:107
  333.7 23.3 %collective-permute-start.44 = (bf16[1,288,768]{2,1,0:T(8,128)(2,1)S(1)}, bf16[1,288,768]{2,1,0:T(8,128)(2,1)S(1)}, u32[]{:S(2)}, u32[]{:S(2)}) collective-permute-start(bf16[1,288,768]{2,1,0:T(8,128)(2,1)S(1)} %dynamic-slice_bitcast_fusion.8), channel_id=1, source_target_pairs={{0,4},{4,0},{8,12},{12,8},{16,20},{20,16},{24,28},{28,24},{1,5},{5... | collective-permute-start | bytes 1327112 | tf_op jit(solution)/shard_map/qkv_3/ppermute | solution.py:107
  336.1 21.1 %collective-permute-start.42 = (bf16[1,192,1664]{2,1,0:T(8,128)(2,1)S(1)}, bf16[1,192,1664]{2,1,0:T(8,128)(2,1)S(1)}, u32[]{:S(2)}, u32[]{:S(2)}) collective-permute-start(bf16[1,192,1664]{2,1,0:T(8,128)(2,1)S(1)} %constant_dynamic-slice_fusion), channel_id=1, source_target_pairs={{0,2},{1,3},{2,0},{3,1},{4,6},{5,7},{6,4},{7,5},{8,10},{9,11},{10,... | collective-permute-start | bytes 1916936 | tf_op jit(solution)/shard_map/last_2/ppermute | solution.py:107
  357.1 9.9 %collective-permute-start.46 = (bf16[1,144,768]{2,1,0:T(8,128)(2,1)S(1)}, bf16[1,144,768]{2,1,0:T(8,128)(2,1)S(1)}, u32[]{:S(2)}, u32[]{:S(2)}) collective-permute-start(bf16[1,144,768]{2,1,0:T(8,128)(2,1)S(1)} %dynamic-slice_bitcast_fusion.12), channel_id=1, source_target_pairs={{0,8},{4,12},{8,0},{12,4},{16,24},{20,28},{24,16},{28,20},{1,9},{5... | collective-permute-start | bytes 663560 | tf_op jit(solution)/shard_map/qkv_4/ppermute | solution.py:107
  357.4 9.7 %collective-permute-start.43 = (bf16[1,96,1664]{2,1,0:T(8,128)(2,1)S(1)}, bf16[1,96,1664]{2,1,0:T(8,128)(2,1)S(1)}, u32[]{:S(2)}, u32[]{:S(2)}) collective-permute-start(bf16[1,96,1664]{2,1,0:T(8,128)(2,1)S(1)} %dynamic-slice_bitcast_fusion.10), channel_id=1, source_target_pairs={{0,4},{4,0},{8,12},{12,8},{16,20},{20,16},{24,28},{28,24},{1,5},{5... | collective-permute-start | bytes 958472 | tf_op jit(solution)/shard_map/last_3/ppermute | solution.py:107
  367.1 11.2 %collective-permute-start.48 = (bf16[1,144,768]{2,1,0:T(8,128)(2,1)S(1)}, bf16[1,144,768]{2,1,0:T(8,128)(2,1)S(1)}, u32[]{:S(2)}, u32[]{:S(2)}) collective-permute-start(bf16[1,144,768]{2,1,0:T(8,128)(2,1)S(1)} %fusion.24), channel_id=1, source_target_pairs={{0,16},{4,20},{8,24},{12,28},{16,0},{20,4},{24,8},{28,12},{1,17},{... | collective-permute-start | bytes 663560 | tf_op jit(solution)/shard_map/qkv_5/ppermute | solution.py:107
  367.3 11.1 %collective-permute-start.45 = (bf16[1,48,1664]{2,1,0:T(8,128)(2,1)S(1)}, bf16[1,48,1664]{2,1,0:T(8,128)(2,1)S(1)}, u32[]{:S(2)}, u32[]{:S(2)}) collective-permute-start(bf16[1,48,1664]{2,1,0:T(8,128)(2,1)S(1)} %dynamic-slice_bitcast_fusion.13), channel_id=1, source_target_pairs={{0,8},{4,12},{8,0},{12,4},{16,24},{20,28},{24,16},{28,20},{1,9},{5... | collective-permute-start | bytes 479240 | tf_op jit(solution)/shard_map/last_4/ppermute | solution.py:107
  378.4 7.6 %collective-permute-start.51 = (bf16[1,144,768]{2,1,0:T(8,128)(2,1)S(1)}, bf16[1,144,768]{2,1,0:T(8,128)(2,1)S(1)}, u32[]{:S(2)}, u32[]{:S(2)}) collective-permute-start(bf16[1,144,768]{2,1,0:T(8,128)(2,1)S(1)} %add_convert_fusion.12), channel_id=1, source_target_pairs={{0,8},{4,12},{8,0},{12,4},{16,24},{20,28},{24,16},{28,20},{1,9},{5... | collective-permute-start | bytes 663560 | tf_op jit(solution)/shard_map/qkv_6/ppermute | solution.py:107
  378.5 8.0 %collective-permute-start.47 = (bf16[1,48,1664]{2,1,0:T(8,128)(2,1)S(1)}, bf16[1,48,1664]{2,1,0:T(8,128)(2,1)S(1)}, u32[]{:S(2)}, u32[]{:S(2)}) collective-permute-start(bf16[1,48,1664]{2,1,0:T(8,128)(2,1)S(1)} %fusion.25), channel_id=1, source_target_pairs={{0,16},{4,20},{8,24},{12,28},{16,0},{20,4},{24,8},{28,12},{1,17},{... | collective-permute-start | bytes 479240 | tf_op jit(solution)/shard_map/last_5/ppermute | solution.py:107
  387.1 8.4 %collective-permute-start.52 = (bf16[1,288,768]{2,1,0:T(8,128)(2,1)S(1)}, bf16[1,288,768]{2,1,0:T(8,128)(2,1)S(1)}, u32[]{:S(2)}, u32[]{:S(2)}) collective-permute-start(bf16[1,288,768]{2,1,0:T(8,128)(2,1)S(1)} %maximum_select_fusion.9), channel_id=1, source_target_pairs={{0,4},{4,0},{8,12},{12,8},{16,20},{20,16},{24,28},{28,24},{1,5},{5... | collective-permute-start | bytes 1327112 | tf_op jit(solution)/shard_map/qkv_7/ppermute | solution.py:107
  (70 other events, 974.4 us)

commit v4 on v3

--- a/solution.py
+++ b/solution.py
@@ -54,8 +54,7 @@
 
 
 class Reducer:
-    def __init__(self, name, *grads):
-        self.name = name
+    def __init__(self, *grads):
         self.n_group, self.n_data = lax.axis_size("fsdp"), lax.axis_size("dp")
         columns = grads[0].shape[1]
         self.parts = [grad.reshape(self.n_group, -1, columns) for grad in grads]
@@ -103,8 +102,7 @@
             send = sends[0] if len(sends) == 1 else jnp.concatenate(sends, 1)
         else:
             send = self.keep = self.parts[0]
-        with jax.named_scope(f"{self.name}_{self.at}"):
-            self.flight = lax.ppermute(send, axis, bit_pairs(lax.axis_size(axis), bit))
+        self.flight = lax.ppermute(send, axis, bit_pairs(lax.axis_size(axis), bit))
         return send
 
     def finish(self, *gates):
@@ -309,6 +307,36 @@
     )(packed, packed, packed, grad_attended, attended, qaug, kmark, *([] if before is None else [before]))
 
 
+def hidden_kernel(normed_ref, weight_ref, bias_ref, act_ref, slope_ref):
+    pre_act = dot_nt(normed_ref[...], weight_ref[...]) + bias_ref[...]
+    t = 1.0 / (1.0 + 0.23164189 * jnp.abs(pre_act))
+    bell = jnp.exp(-0.5 * pre_act * pre_act)
+    tail = 0.5307027145 * t - 0.7265760135
+    tail = (tail * t + 0.7107068705) * t - 0.142248368
+    tail = (tail * t + 0.127414796) * t * bell
+    normal = jnp.where(pre_act >= 0, 1.0 - tail, tail)
+    act_ref[...] = (pre_act * normal).astype(bf16)
+    slope_ref[...] = (normal + 0.3989422804 * pre_act * bell).astype(bf16)
+
+
+def hidden_forward(normed, weight, bias, step=256):
+    rows, width = normed.shape
+    hidden = weight.shape[0]
+    block = pl.BlockSpec((rows, step), lambda g: (0, g))
+    return pl.pallas_call(
+        hidden_kernel,
+        grid=(hidden // step,),
+        in_specs=[
+            pl.BlockSpec((rows, width), lambda g: (0, 0)),
+            pl.BlockSpec((step, width), lambda g: (g, 0)),
+            pl.BlockSpec((1, step), lambda g: (0, g)),
+        ],
+        out_specs=[block, block],
+        out_shape=[jax.ShapeDtypeStruct((rows, hidden), bf16)] * 2,
+        name="hidden_forward",
+    )(normed, weight, bias[None, :])
+
+
 def marks(row_item, row_live):
     rows = row_item.shape[0]
     lane = lane_index(rows)
@@ -342,24 +370,30 @@
         copy.wait()
 
 
-def gather_rows(shard, name, *gates):
-    rows, columns = shard.shape
+def gather_start(shard, *gates):
+    rows, _ = shard.shape
     half = rows // 2
-    n_group, n_data = lax.axis_size("fsdp"), lax.axis_size("dp")
+    n_group = lax.axis_size("fsdp")
     low = lax.axis_index("dp") & 1
     if gates:
         shard = after(shard, *gates)
     send = lax.dynamic_slice_in_dim(shard, half * low, half, 0)
-    with jax.named_scope(name + "_near"):
-        near = lax.ppermute(send, "fsdp", bit_pairs(n_group, 1))
-    with jax.named_scope(name + "_own_c"):
-        own_c = lax.ppermute(shard, "fsdp", bit_pairs(n_group, 0))
-    with jax.named_scope(name + "_far"):
-        far = lax.ppermute(near, "dp", bit_pairs(n_data, 0))
-    with jax.named_scope(name + "_near_c"):
-        near_c = lax.ppermute(near, "fsdp", bit_pairs(n_group, 0))
-    with jax.named_scope(name + "_far_c"):
-        far_c = lax.ppermute(far, "fsdp", bit_pairs(n_group, 0))
+    near = lax.ppermute(send, "fsdp", bit_pairs(n_group, 1))
+    own_c = lax.ppermute(shard, "fsdp", bit_pairs(n_group, 0))
+    return shard, near, own_c
+
+
+def gather_finish(started, *gates):
+    shard, near, own_c = started
+    half, columns = shard.shape[0] // 2, shard.shape[1]
+    rows = 2 * half
+    n_group, n_data = lax.axis_size("fsdp"), lax.axis_size("dp")
+    low = lax.axis_index("dp") & 1
+    if gates:
+        near = after(near, *gates)
+    far = lax.ppermute(near, "dp", bit_pairs(n_data, 0))
+    near_c = lax.ppermute(near, "fsdp", bit_pairs(n_group, 0))
+    far_c = lax.ppermute(far, "fsdp", bit_pairs(n_group, 0))
     place = jnp.stack([lax.axis_index("fsdp"), low]).astype(jnp.int32)
     anywhere = pl.BlockSpec(memory_space=pl.ANY)
     full = pl.pallas_call(
@@ -368,9 +402,8 @@
         out_specs=pl.BlockSpec(memory_space=pltpu.VMEM),
         out_shape=jax.ShapeDtypeStruct((n_group * rows, columns), shard.dtype),
         scratch_shapes=[pltpu.SemaphoreType.DMA((6,))],
-        name=name,
     )(place, shard, near, far, own_c, near_c, far_c)
-    return full, near
+    return full
 
 
 def gather_vectors(members, *gates):
@@ -425,7 +458,8 @@
     output_bias,
 ):
     model_width = inputs.shape[1]
-    skip_full, skip_near = gather_rows(skip_weight, "place_skip")
+    skip_start = gather_start(skip_weight)
+    skip_full = gather_finish(skip_start)
     (
         skip_vec,
         gain_first,
@@ -447,64 +481,69 @@
             output_bias,
         ],
     )
-    qkv_full, qkv_near = gather_rows(qkv_weight, "place_qkv", skip_near)
-    proj_full, _ = gather_rows(proj_weight, "place_proj", qkv_near)
-    hidden_full, _ = gather_rows(hidden_weight, "place_hidden", qkv_near)
-    output_full, _ = gather_rows(output_weight, "place_output", qkv_near)
+    qkv_start = gather_start(qkv_weight, skip_start[1])
+    qkv_full = gather_finish(qkv_start)
+    proj_start = gather_start(proj_weight, qkv_start[1])
+    hidden_start = gather_start(hidden_weight, qkv_start[1])
+    output_start = gather_start(output_weight, qkv_start[1])
     joined = jnp.concatenate([inputs, skip_input], axis=1)
     stream_a = times_t(joined, skip_full) + skip_vec
     normed_a = layer_norm(stream_a, gain_first, shift_first).astype(jnp.bfloat16)
     packed = times_t(normed_a, qkv_full).astype(jnp.bfloat16)
+    proj_full = gather_finish(proj_start, packed)
+    hidden_full = gather_finish(hidden_start, packed)
+    output_full = gather_finish(output_start, packed)
     qmark, kmark = marks(row_item, row_live)
     attended, qaug = attention_forward(packed, qmark, kmark)
     stream_b = stream_a + times_t(attended, proj_full) + proj_vec
     normed_b = layer_norm(stream_b, gain_second, shift_second).astype(jnp.bfloat16)
-    pre_act = times_t(normed_b, hidden_full) + hidden_vec
-    activation = jax.nn.gelu(pre_act, approximate=False).astype(jnp.bfloat16)
+    activation, gelu_slope = hidden_forward(normed_b, hidden_full, hidden_vec)
     grad_out = cotangent * row_live[:, None].astype(jnp.bfloat16)
     grad_output_weight = rows_outer(grad_out, activation).astype(bf16)
-    reduce_out = Reducer("out", grad_output_weight)
+    reduce_out = Reducer(grad_output_weight)
     sent = reduce_out.step()
     grad_act = times_n(after(grad_out, sent), output_full)
-    gelu_value, gelu_back = jax.vjp(lambda value: jax.nn.gelu(value, approximate=False), pre_act)
-    grad_pre = gelu_back(grad_act)[0].astype(jnp.bfloat16)
+    grad_pre = (grad_act * gelu_slope.astype(f32)).astype(bf16)
     sent = reduce_out.step(grad_pre)
     grad_hidden_weight = rows_outer(after(grad_pre, sent), normed_b).astype(bf16)
     grad_hidden_bias = column_sums(grad_pre)
     grad_normed_b = times_n(after(grad_pre, grad_hidden_weight), hidden_full)
-    norm_value, norm_back = jax.vjp(layer_norm, stream_b, gain_second, shift_second)
+    _, norm_back = jax.vjp(layer_norm, stream_b, gain_second, shift_second)
     grad_part_b, grad_mlp_gain, grad_mlp_shift = norm_back(grad_normed_b)
     grad_stream_b = grad_out.astype(jnp.float32) + grad_part_b
     grad_branch = grad_stream_b.astype(jnp.bfloat16)
     grad_proj_weight = rows_outer(grad_branch, attended).astype(bf16)
     grad_proj_bias = column_sums(grad_branch)
     grad_attended = times_n(grad_branch, proj_full).astype(jnp.bfloat16)
-    reduce_mlp = Reducer("mlp", grad_hidden_weight, grad_proj_weight)
-    sent = [reduce_mlp.step(), reduce_out.step(grad_attended)]
+    reduce_mlp = Reducer(grad_hidden_weight, grad_proj_weight)
+    sent = [
+        reduce_mlp.step(),
+        reduce_out.step(grad_attended),
+        reduce_mlp.step(grad_attended),
+    ]
     pairs = model_width // LANES
     cuts = [pairs * third // 3 for third in range(4)]
     grad_qkv = None
     for third in range(3):
-        with jax.named_scope(f"bwd_a{third}"):
-            grad_qkv = attention_backward(
-                packed, after(grad_attended, *sent), attended, qaug, kmark,
-                cuts[third], cuts[third + 1] - cuts[third], grad_qkv,
-            )
+        grad_qkv = attention_backward(
+            packed, after(grad_attended, *sent), attended, qaug, kmark,
+            cuts[third], cuts[third + 1] - cuts[third], grad_qkv,
+        )
         sent = [reduce_out.step(grad_qkv)]
-        if third != 1:
+        if third > 0:
             sent.append(reduce_mlp.step(grad_qkv))
     grad_qkv_weight = rows_outer(after(grad_qkv, sent), normed_a).astype(bf16)
-    reduce_qkv = Reducer("qkv", grad_qkv_weight)
+    reduce_qkv = Reducer(grad_qkv_weight)
     sent = [
         reduce_qkv.step(),
+        reduce_mlp.step(grad_qkv_weight),
         reduce_out.step(grad_qkv_weight),
     ]
     grad_normed_a = times_n(after(grad_qkv, *sent), qkv_full)
     sent = [
         reduce_qkv.step(grad_normed_a),
-        reduce_mlp.step(grad_normed_a),
     ]
-    first_value, first_back = jax.vjp(layer_norm, stream_a, gain_first, shift_first)
+    _, first_back = jax.vjp(layer_norm, stream_a, gain_first, shift_first)
     grad_part_a, grad_attn_gain, grad_attn_shift = first_back(after(grad_normed_a, *sent))
     grad_rounded = (grad_stream_b + grad_part_a).astype(jnp.bfloat16)
     sent = reduce_mlp.step(grad_rounded)
@@ -530,7 +569,7 @@
     vectors = jnp.concatenate([vectors, wide], 0)
     vectors = jnp.pad(vectors, ((0, LANES - vectors.shape[0]), (0, 0))).T
     last = jnp.concatenate([grad_skip_weight, vectors], 1).astype(jnp.bfloat16)
-    reduce_last = Reducer("last", last)
+    reduce_last = Reducer(last)
     sent = [reduce_last.step(), reduce_mlp.step(last)]
     grad_joined = times_n(after(grad_rounded, *sent), skip_full)
     grad_input = grad_joined[:, :model_width].astype(jnp.bfloat16)
@@ -544,7 +583,7 @@
         stream_b + times_t(after(activation, *sent), output_full) + output_vec
     ).astype(jnp.bfloat16)
     gate = output
-    for turn in range(len(reduce_last.plan)):
+    for _ in range(len(reduce_last.plan)):
         gate = after(reduce_qkv.step(gate), reduce_last.step(gate))
     final_output = reduce_out.finish(output)
     both_final = reduce_mlp.finish(output)
@@ -614,4 +653,5 @@
         P("fsdp", None),
         P("fsdp"),
     )
+
     return jax.shard_map(shards, mesh=mesh, in_specs=in_specs, out_specs=out_specs, check_vma=False)

time: 408 us -> 420 us (1.029)
  matrix products: 106 us -> 76.5 us
  Pallas kernels: 82.7 us -> 99.7 us
  other arithmetic: 36.7 us -> 48.6 us
  local copies, waits for them, and re-layouts: 37.4 us -> 45.5 us
    dot_general x5 -> x4, matrix products: 54.6 us -> 22.5 us  [times_t(): lax.dot_general(left, weight, (((1,), (1,)), ((), ())), preferred_element...]
    pallas_call x5 -> x6, Pallas kernels: 21.5 us -> 38.9 us  [the longest x5 21.5 us: gather_finish(): pl.pallas_call(functools.partial(place_kernel, half), in_specs=[pl.BlockS...]
    ppermute x28, waiting for transfers between devices: 64.6 us -> 72.6 us  [step(): self.flight = lax.ppermute(send, axis, bit_pairs(lax.axis_size(axis), bit))]
    dot_general x5, matrix products: 23.5 us -> 28 us  [rows_outer(): lax.dot_general(grad_rows, left, (((0,), (0,)), ((), ())), preferred_elem...]
    ppermute x25, waiting for transfers between devices: 29.2 us -> 24.8 us  [the longest x5 15.2 us: gather_finish(): far = lax.ppermute(near, 'dp', bit_pairs(n_data, 0))]
    unnamed x127 -> x139, local copies, waits for them, and re-layouts: 15.1 us -> 13 us
  transfers between devices with their start and end apart: 55 -> 55, of which waited for: 21 -> 21; matrix products, arithmetic and copies ran while one was open for 40% -> 32% of each run, Pallas kernels for 21% -> 24%
where the time goes in v4:
time: 420 us; the launch traced here: 415 us
  Pallas kernels  99.7 us (24%)
  waiting for transfers between devices  97.4 us (23%)
  matrix products  76.5 us (18%)
  other arithmetic  48.6 us (12%)
  local copies, waits for them, and re-layouts  45.5 us (11%)
  starting transfers between devices  44.6 us (11%)
    ppermute x28, waiting for transfers between devices, step(): self.flight = lax.ppermute(send, axis, bit_pairs(lax.axis_size(axis), bit))  72.6 us
    pallas_call x3, Pallas kernels, attention_backward(): pl.pallas_call(kernel, grid=(count,), in_specs=[block(0), block(pairs), b...  39.6 us
    dot_general x5, matrix products, rows_outer(): lax.dot_general(grad_rows, left, (((0,), (0,)), ((), ())), preferred_elem...  28 us
    ppermute x28, starting transfers between devices, step(): self.flight = lax.ppermute(send, axis, bit_pairs(lax.axis_size(axis), bit))  27.2 us
    dot_general x5, matrix products, times_n(): return jnp.dot(left, weight, preferred_element_type=jnp.float32)  26 us
    dot_general x4, matrix products, times_t(): lax.dot_general(left, weight, (((1,), (1,)), ((), ())), preferred_element...  22.5 us
    pallas_call x5, Pallas kernels, gather_finish(): pl.pallas_call(functools.partial(place_kernel, half), in_specs=[pl.BlockS...  21.5 us
    pallas_call x1, Pallas kernels, attention_forward(): pl.pallas_call(kernel, grid=(pairs,), in_specs=[block(0), block(pairs), b...  21.1 us
  transfers between devices with their start and end apart: 55, of which 21 were waited for; matrix products, arithmetic and copies ran while one was open for 32% of the time, Pallas kernels for 24%

profile of v4, /device:TPU:0, one launch (start us, length us, event | category | flops | bytes accessed | tf_op | source)
XLA Modules:
  0.0 414.5 jit_solution(2671815465640718459)
XLA Ops:
  2.5 3.0 collective-permute-start.5
  11.3 2.1 fusion.28
  22.1 5.5 %collective-permute-done.1.far = bf16[96,1536]{1,0:T(8,128)(2,1)} collective-permute-done((bf16[96,1536]{1,0:T(8,128)(2,1)S(1)}, bf16[96,1536]{1,0:T(8,128)(2,1)}, u32[]{:S(2)}, u32[]{:S(2)}) %collective-permute-start.1) | collective-permute-done | bytes 294944 | tf_op jit(solution)/shard_map/ppermute | solution.py:394
  27.6 2.2 collective-permute-done.7.near
  36.6 3.7 shard_map.297
  40.3 5.1 %add_reduce_fusion = (f32[904]{0:T(1024)S(1)}, f32[904,768]{1,0:T(8,128)S(1)}) fusion(f32[768]{0:T(1024)S(1)} %add.277, bf16[904,1536]{1,0:T(8,128)(2,1)} %copy-done.28, bf16[768,1536]{1,0:T(8,128)(2,1)} %shard_map.297), kind=kOutput, calls=%fused_computation.34 | convolution fusion | flops 2134191232 | bytes 7920160 | tf_op jit(solution)/shard_map/dot_general | solution.py:25
  48.5 4.4 %shard_map.298 = bf16[2304,768]{1,0:T(8,128)(2,1)} custom-call(s32[2]{0:T(128)} %pad_add_fusion.place_ref, bf16[576,768]{1,0:T(8,128)(2,1)} %own.2, bf16[288,768]{1,0:T(8,128)(2,1)} %copy-done.32, bf16[288,768]{1,0:T(8,128)(2,1)} %collective-permute-done.8.far, bf16[576,768]{1,0:T(8,128)(2,1)} %collective-permute-done.9.own_c, ...), custom_call_target="tpu_custom_call" | custom-call | tf_op jit(solution)/shard_map/pallas_call | solution.py:399
  53.1 7.8 %convolution_convert_fusion.q_ref.k_ref.v_ref = bf16[904,2304]{1,0:T(8,128)(2,1)} fusion(bf16[2304,768]{1,0:T(8,128)(2,1)} %shard_map.298, f32[904,768]{1,0:T(8,128)S(1)} %get-tuple-element.161, f32[768]{0:T(1024)S(1)} %copy-done.57, f32[768]{0:T(1024)S(1)} %copy-done.44, f32[904]{0:T(1024)S(1)} %copy-done.46, f32[904]{0:T(1024)S(1)} %broadcast_multiply_fusion.2, ...), kind=kOutput, calls=%fused_computation.2 | convolution fusion | flops 3205453824 | bytes 10498112 | tf_op jit(solution)/shard_map/dot_general | solution.py:25
  64.1 2.5 collective-permute-done.13.far
  71.4 21.1 %attention_forward.1 = (bf16[904,768]{1,0:T(8,128)(2,1)}, bf16[904,1536]{1,0:T(8,128)(2,1)}) custom-call(bf16[904,2304]{1,0:T(8,128)(2,1)} %convolution_convert_fusion.q_ref.k_ref.v_ref, bf16[904,2304]{1,0:T(8,128)(2,1)} %convolution_convert_fusion.q_ref.k_ref.v_ref, bf16[904,2304]{1,0:T(8,128)(2,1)} %convolution_convert_fusion.q_ref.k_ref.v_ref, ...), custom_call_target="tpu_custom_call" | custom-call | tf_op jit(solution)/shard_map/attention_forward/pallas_call | solution.py:195
  94.8 3.0 shard_map.299
  97.9 4.0 fusion.36
  101.9 7.3 %collective-permute-done.18.far = bf16[384,768]{1,0:T(8,128)(2,1)} collective-permute-done((bf16[384,768]{1,0:T(8,128)(2,1)}, bf16[384,768]{1,0:T(8,128)(2,1)}, u32[]{:S(2)}, u32[]{:S(2)}) %collective-permute-start.18) | collective-permute-done | bytes 589856 | tf_op jit(solution)/shard_map/ppermute | solution.py:394
  111.5 5.2 %shard_map.300.weight_ref = bf16[3072,768]{1,0:T(8,128)(2,1)} custom-call(s32[2]{0:T(128)} %pad_add_fusion.place_ref, bf16[768,768]{1,0:T(8,128)(2,1)} %own.4, bf16[384,768]{1,0:T(8,128)(2,1)} %collective-permute-done.17.near, bf16[384,768]{1,0:T(8,128)(2,1)} %collective-permute-done.18.far, bf16[768,768]{1,0:T(8,128)(2,1)} %collective-permute-done.19.own_c, ...), custom_call_target="tpu_custom_call" | custom-call | tf_op jit(solution)/shard_map/pallas_call | solution.py:399
  116.7 17.4 %hidden_forward.1 = (bf16[904,3072]{1,0:T(8,128)(2,1)}, bf16[904,3072]{1,0:T(8,128)(2,1)}) custom-call(bf16[904,768]{1,0:T(8,128)(2,1)} %add_convert_fusion.4.normed_ref, bf16[3072,768]{1,0:T(8,128)(2,1)} %shard_map.300.weight_ref, f32[1,3072]{1,0:T(1,128)} %broadcast_in_dim_reshape.2.bias_ref), custom_call_target="tpu_custom_call" | custom-call | tf_op jit(solution)/shard_map/hidden_forward/pallas_call | solution.py:326
  134.1 8.4 %convolution_convert_fusion.2 = bf16[768,3072]{1,0:T(8,128)(2,1)S(1)} fusion(bf16[904,768]{1,0:T(8,128)(2,1)} %get-tuple-element.73, bf16[904,3072]{1,0:T(8,128)(2,1)} %get-tuple-element.102), kind=kOutput, calls=%fused_computation.4 | convolution fusion | flops 4267966464 | bytes 11661312 | tf_op jit(solution)/shard_map/dot_general | solution.py:35
  142.5 2.2 copy-done.16
  147.0 5.0 %collective-permute-done.25.near_c = bf16[96,3072]{1,0:T(8,128)(2,1)} collective-permute-done((bf16[96,3072]{1,0:T(8,128)(2,1)}, bf16[96,3072]{1,0:T(8,128)(2,1)}, u32[]{:S(2)}, u32[]{:S(2)}) %collective-permute-start.25) | collective-permute-done | bytes 589856 | tf_op jit(solution)/shard_map/ppermute | solution.py:395
  152.8 5.2 %shard_map.301 = bf16[768,3072]{1,0:T(8,128)(2,1)} custom-call(s32[2]{0:T(128)} %pad_add_fusion.place_ref, bf16[192,3072]{1,0:T(8,128)(2,1)} %own.5, bf16[96,3072]{1,0:T(8,128)(2,1)} %collective-permute-done.22.near, bf16[96,3072]{1,0:T(8,128)(2,1)} %copy-done.31, bf16[192,3072]{1,0:T(8,128)(2,1)} %collective-permute-done.24.own_c, ...), custom_call_target="tpu_custom_call" | custom-call | tf_op jit(solution)/shard_map/pallas_call | solution.py:399
  158.0 9.0 %fusion.37 = (bf16[3072]{0:T(1024)(128)(2,1)S(1)}, bf16[904,3072]{1,0:T(8,128)(2,1)S(1)}) fusion(bf16[904,3072]{1,0:T(8,128)(2,1)} %get-tuple-element.76, bf16[904,768]{1,0:T(8,128)(2,1)} %get-tuple-element.73, bf16[768,3072]{1,0:T(8,128)(2,1)} %shard_map.301), kind=kOutput, calls=%fused_computation.186 | convolution fusion | flops 4276712448 | bytes 17221632 | tf_op jit(solution)/shard_map/dot_general | solution.py:31
  167.1 2.6 fusion
  172.3 6.1 %convolution_convert_fusion.1 = bf16[3072,768]{1,0:T(8,128)(2,1)S(1)} fusion(bf16[904,3072]{1,0:T(8,128)(2,1)S(1)} %get-tuple-element.79, bf16[904,768]{1,0:T(8,128)(2,1)S(1)} %copy-done.15), kind=kOutput, calls=%fused_computation.3 | convolution fusion | flops 4267966464 | bytes 11661312 | tf_op jit(solution)/shard_map/dot_general | solution.py:35
  178.5 5.5 %multiply_reduce_fusion = (bf16[768]{0:T(1024)(128)(2,1)}, f32[904]{0:T(1024)S(1)}, bf16[768]{0:T(1024)(128)(2,1)}, f32[904,768]{1,0:T(8,128)S(1)}) fusion(f32[904,768]{1,0:T(8,128)S(1)} %get-tuple-element.163, f32[904]{0:T(1024)S(1)} %fusion.27, f32[904]{0:T(1024)S(1)} %broadcast_multiply_fusion.1, f32[768]{0:T(1024)S(1)} %copy-done.41, ...), kind=kOutput, calls=%fused_computation.20 | convolution fusion | flops 4271158784 | bytes 15843936 | tf_op jit(solution)/shard_map/dot_general | solution.py:31
  194.0 4.2 %convolution_convert_fusion.6.go_ref = bf16[904,768]{1,0:T(8,128)(2,1)} fusion(bf16[904,768]{1,0:T(8,128)(2,1)} %copy-done.25, bf16[768,768]{1,0:T(8,128)(2,1)} %shard_map.299), kind=kOutput, calls=%fused_computation.46 | convolution fusion | flops 1067096064 | bytes 3956736 | tf_op jit(solution)/shard_map/dot_general | solution.py:31
  198.3 22.9 %collective-permute-done.28 = bf16[1,192,3072]{2,1,0:T(8,128)(2,1)} collective-permute-done((bf16[1,192,3072]{2,1,0:T(8,128)(2,1)}, bf16[1,192,3072]{2,1,0:T(8,128)(2,1)}, u32[]{:S(2)}, u32[]{:S(2)}) %collective-permute-start.28) | collective-permute-done | bytes 1179680 | tf_op jit(solution)/shard_map/ppermute | solution.py:105
  225.9 3.3 add_convert_fusion
  233.7 13.3 %attention_backward.3.rest_0_ = bf16[904,2304]{1,0:T(8,128)(2,1)} custom-call(bf16[904,2304]{1,0:T(8,128)(2,1)} %convolution_convert_fusion.q_ref.k_ref.v_ref, bf16[904,2304]{1,0:T(8,128)(2,1)} %convolution_convert_fusion.q_ref.k_ref.v_ref, bf16[904,2304]{1,0:T(8,128)(2,1)} %convolution_convert_fusion.q_ref.k_ref.v_ref, ...), custom_call_target="tpu_custom_call" | custom-call | tf_op jit(solution)/shard_map/attention_backward/pallas_call | solution.py:289
  250.7 13.1 %attention_backward.4.rest_0_ = bf16[904,2304]{1,0:T(8,128)(2,1)} custom-call(bf16[904,2304]{1,0:T(8,128)(2,1)} %convolution_convert_fusion.q_ref.k_ref.v_ref, bf16[904,2304]{1,0:T(8,128)(2,1)} %convolution_convert_fusion.q_ref.k_ref.v_ref, bf16[904,2304]{1,0:T(8,128)(2,1)} %convolution_convert_fusion.q_ref.k_ref.v_ref, ...), custom_call_target="tpu_custom_call", output_to_operand_aliasing={{}: (7, {})} | custom-call | tf_op jit(solution)/shard_map/attention_backward/pallas_call | solution.py:289
  265.5 2.6 collective-permute-start.33
  268.1 2.2 add_convert_fusion.1
  277.4 13.3 %attention_backward.5 = bf16[904,2304]{1,0:T(8,128)(2,1)} custom-call(bf16[904,2304]{1,0:T(8,128)(2,1)} %convolution_convert_fusion.q_ref.k_ref.v_ref, bf16[904,2304]{1,0:T(8,128)(2,1)} %convolution_convert_fusion.q_ref.k_ref.v_ref, bf16[904,2304]{1,0:T(8,128)(2,1)} %convolution_convert_fusion.q_ref.k_ref.v_ref, ...), custom_call_target="tpu_custom_call", output_to_operand_aliasing={{}: (7, {})} | custom-call | tf_op jit(solution)/shard_map/attention_backward/pallas_call | solution.py:289
  295.5 8.0 %convolution_convert_fusion.3 = bf16[2304,768]{1,0:T(8,128)(2,1)S(1)} fusion(bf16[904,2304]{1,0:T(8,128)(2,1)} %attention_backward.5, f32[904,768]{1,0:T(8,128)S(1)} %copy-done.2, f32[768]{0:T(1024)S(1)} %copy-done.58, f32[768]{0:T(1024)S(1)} %copy-done.45, f32[904]{0:T(1024)S(1)} %copy-done.47, f32[904]{0:T(1024)S(1)} %broadcast_multiply_fusion.2, ...), kind=kOutput, calls=%fused_computation.5 | convolution fusion | flops 3205140480 | bytes 10498112 | tf_op jit(solution)/shard_map/dot_general | solution.py:35
  307.7 3.5 fusion.38
  316.9 9.8 %collective-permute-done.38 = bf16[1,240,768]{2,1,0:T(8,128)(2,1)S(1)} collective-permute-done((bf16[1,240,768]{2,1,0:T(8,128)(2,1)S(1)}, bf16[1,240,768]{2,1,0:T(8,128)(2,1)S(1)}, u32[]{:S(2)}, u32[]{:S(2)}) %collective-permute-start.38) | collective-permute-done | bytes 368672 | tf_op jit(solution)/shard_map/ppermute | solution.py:105
  327.4 4.0 convolution_convert_fusion.5
  333.6 3.9 collective-permute-done.40
  340.7 3.8 convolution_convert_fusion.4
  346.3 2.6 collective-permute-done.41
  352.1 5.6 %add_convert_fusion.2 = bf16[904,768]{1,0:T(8,128)(2,1)} fusion(f32[904,768]{1,0:T(8,128)S(1)} %get-tuple-element.163, bf16[904,3072]{1,0:T(8,128)(2,1)S(1)} %bitcast.225, bf16[768,3072]{1,0:T(8,128)(2,1)S(1)} %bitcast.190, f32[768]{0:T(1024)S(1)} %copy-done.59), kind=kOutput, calls=%fused_computation.19 | convolution fusion | flops 4267689984 | bytes 14441472 | tf_op jit(solution)/shard_map/dot_general | solution.py:25
  357.7 8.2 %collective-permute-done.44 = bf16[1,288,768]{2,1,0:T(8,128)(2,1)S(1)} collective-permute-done((bf16[1,288,768]{2,1,0:T(8,128)(2,1)S(1)}, bf16[1,288,768]{2,1,0:T(8,128)(2,1)S(1)}, u32[]{:S(2)}, u32[]{:S(2)}) %collective-permute-start.44) | collective-permute-done | bytes 442400 | tf_op jit(solution)/shard_map/ppermute | solution.py:105
  368.4 3.0 convert_multiply_fusion.1
  376.1 6.3 %collective-permute-done.48 = bf16[1,144,768]{2,1,0:T(8,128)(2,1)S(1)} collective-permute-done((bf16[1,144,768]{2,1,0:T(8,128)(2,1)S(1)}, bf16[1,144,768]{2,1,0:T(8,128)(2,1)S(1)}, u32[]{:S(2)}, u32[]{:S(2)}) %collective-permute-start.48) | collective-permute-done | bytes 221216 | tf_op jit(solution)/shard_map/ppermute | solution.py:105
  382.7 2.5 collective-permute-start.47
  388.0 4.0 collective-permute-done.51
  392.9 2.1 collective-permute-start.52
  395.0 2.3 collective-permute-done.49
  398.7 7.2 %collective-permute-done.52 = bf16[1,288,768]{2,1,0:T(8,128)(2,1)S(1)} collective-permute-done((bf16[1,288,768]{2,1,0:T(8,128)(2,1)S(1)}, bf16[1,288,768]{2,1,0:T(8,128)(2,1)S(1)}, u32[]{:S(2)}, u32[]{:S(2)}) %collective-permute-start.52) | collective-permute-done | bytes 442400 | tf_op jit(solution)/shard_map/ppermute | solution.py:105
  407.4 3.4 collective-permute-done.50
  (352 shorter events, 119.0 us)
Async XLA Ops:
  2.5 12.0 %collective-permute-start.5 = (bf16[1,16,192]{2,1,0:T(8,128)(2,1)S(1)}, bf16[1,16,192]{2,1,0:T(8,128)(2,1)S(1)}, u32[]{:S(2)}, u32[]{:S(2)}) collective-permute-start(bf16[1,16,192]{2,1,0:T(8,128)(2,1)S(1)} %bitcast.221), channel_id=1, source_target_pairs={{0,2},{1,3},{2,0},{3,1},{4,6},{5,7},{6,4},{7,5},{8,10},{9,11},{10,... | collective-permute-start | bytes 18440 | tf_op jit(solution)/shard_map/ppermute | solution.py:419
  5.5 28.8 %collective-permute-start.2 = (bf16[192,1536]{1,0:T(8,128)(2,1)}, bf16[192,1536]{1,0:T(8,128)(2,1)}, u32[]{:S(2)}, u32[]{:S(2)}) collective-permute-start(bf16[192,1536]{1,0:T(8,128)(2,1)} %own.1), channel_id=1, source_target_pairs={{0,1},{1,0},{2,3},{3,2},{4,5},{5,4},{6,7},{7,6},{8,9},{9,8},{10,11... | collective-permute-start | bytes 1769480 | tf_op jit(solution)/shard_map/ppermute | solution.py:382
  6.5 9.5 %collective-permute-start = (bf16[96,1536]{1,0:T(8,128)(2,1)S(1)}, bf16[96,1536]{1,0:T(8,128)(2,1)S(1)}, u32[]{:S(2)}, u32[]{:S(2)}) collective-permute-start(bf16[96,1536]{1,0:T(8,128)(2,1)S(1)} %constant_dynamic-slice_fusion.8), channel_id=1, source_target_pairs={{0,2},{1,3},{2,0},{3,1},{4,6},{5,7},{6,4},{7,5},{8,10},{9,11},{10,... | collective-permute-start | bytes 884744 | tf_op jit(solution)/shard_map/ppermute | solution.py:381
  17.9 11.9 %collective-permute-start.7 = (bf16[288,768]{1,0:T(8,128)(2,1)}, bf16[288,768]{1,0:T(8,128)(2,1)S(1)}, u32[]{:S(2)}, u32[]{:S(2)}) collective-permute-start(bf16[288,768]{1,0:T(8,128)(2,1)} %constant_dynamic-slice_fusion.7), channel_id=1, source_target_pairs={{0,2},{1,3},{2,0},{3,1},{4,6},{5,7},{6,4},{7,5},{8,10},{9,11},{10,... | collective-permute-start | bytes 1327112 | tf_op jit(solution)/shard_map/ppermute | solution.py:381
  18.6 9.0 %collective-permute-start.1 = (bf16[96,1536]{1,0:T(8,128)(2,1)S(1)}, bf16[96,1536]{1,0:T(8,128)(2,1)}, u32[]{:S(2)}, u32[]{:S(2)}) collective-permute-start(bf16[96,1536]{1,0:T(8,128)(2,1)S(1)} %collective-permute-done.near), channel_id=1, source_target_pairs={{0,4},{4,0},{8,12},{12,8},{16,20},{20,16},{24,28},{28,24},{1,5},{5... | collective-permute-start | bytes 884744 | tf_op jit(solution)/shard_map/ppermute | solution.py:394
  21.6 26.9 %collective-permute-start.9 = (bf16[576,768]{1,0:T(8,128)(2,1)}, bf16[576,768]{1,0:T(8,128)(2,1)}, u32[]{:S(2)}, u32[]{:S(2)}) collective-permute-start(bf16[576,768]{1,0:T(8,128)(2,1)} %own.2), channel_id=1, source_target_pairs={{0,1},{1,0},{2,3},{3,2},{4,5},{5,4},{6,7},{7,6},{8,9},{9,8},{10,11... | collective-permute-start | bytes 2654216 | tf_op jit(solution)/shard_map/ppermute | solution.py:382
  21.6 12.0 %collective-permute-start.3 = (bf16[96,1536]{1,0:T(8,128)(2,1)S(1)}, bf16[96,1536]{1,0:T(8,128)(2,1)S(1)}, u32[]{:S(2)}, u32[]{:S(2)}) collective-permute-start(bf16[96,1536]{1,0:T(8,128)(2,1)S(1)} %collective-permute-done.near), channel_id=1, source_target_pairs={{0,1},{1,0},{2,3},{3,2},{4,5},{5,4},{6,7},{7,6},{8,9},{9,8},{10,11... | collective-permute-start | bytes 884744 | tf_op jit(solution)/shard_map/ppermute | solution.py:395
  27.6 8.2 %collective-permute-start.4 = (bf16[96,1536]{1,0:T(8,128)(2,1)}, bf16[96,1536]{1,0:T(8,128)(2,1)S(1)}, u32[]{:S(2)}, u32[]{:S(2)}) collective-permute-start(bf16[96,1536]{1,0:T(8,128)(2,1)} %collective-permute-done.1.far), channel_id=1, source_target_pairs={{0,1},{1,0},{2,3},{3,2},{4,5},{5,4},{6,7},{7,6},{8,9},{9,8},{10,11... | collective-permute-start | bytes 884744 | tf_op jit(solution)/shard_map/ppermute | solution.py:396
  30.8 40.0 %collective-permute-start.22 = (bf16[96,3072]{1,0:T(8,128)(2,1)}, bf16[96,3072]{1,0:T(8,128)(2,1)}, u32[]{:S(2)}, u32[]{:S(2)}) collective-permute-start(bf16[96,3072]{1,0:T(8,128)(2,1)} %constant_dynamic-slice_fusion.4), channel_id=1, source_target_pairs={{0,2},{1,3},{2,0},{3,1},{4,6},{5,7},{6,4},{7,5},{8,10},{9,11},{10,... | collective-permute-start | bytes 1769480 | tf_op jit(solution)/shard_map/ppermute | solution.py:381
  33.7 37.7 %collective-permute-start.17 = (bf16[384,768]{1,0:T(8,128)(2,1)}, bf16[384,768]{1,0:T(8,128)(2,1)}, u32[]{:S(2)}, u32[]{:S(2)}) collective-permute-start(bf16[384,768]{1,0:T(8,128)(2,1)} %constant_dynamic-slice_fusion.5), channel_id=1, source_target_pairs={{0,2},{1,3},{2,0},{3,1},{4,6},{5,7},{6,4},{7,5},{8,10},{9,11},{10,... | collective-permute-start | bytes 1769480 | tf_op jit(solution)/shard_map/ppermute | solution.py:381
  34.3 11.1 %collective-permute-start.8 = (bf16[288,768]{1,0:T(8,128)(2,1)S(1)}, bf16[288,768]{1,0:T(8,128)(2,1)}, u32[]{:S(2)}, u32[]{:S(2)}) collective-permute-start(bf16[288,768]{1,0:T(8,128)(2,1)S(1)} %collective-permute-done.7.near), channel_id=1, source_target_pairs={{0,4},{4,0},{8,12},{12,8},{16,20},{20,16},{24,28},{28,24},{1,5},{5... | collective-permute-start | bytes 1327112 | tf_op jit(solution)/shard_map/ppermute | solution.py:394
  36.6 10.5 %collective-permute-start.10 = (bf16[288,768]{1,0:T(8,128)(2,1)S(1)}, bf16[288,768]{1,0:T(8,128)(2,1)}, u32[]{:S(2)}, u32[]{:S(2)}) collective-permute-start(bf16[288,768]{1,0:T(8,128)(2,1)S(1)} %collective-permute-done.7.near), channel_id=1, source_target_pairs={{0,1},{1,0},{2,3},{3,2},{4,5},{5,4},{6,7},{7,6},{8,9},{9,8},{10,11... | collective-permute-start | bytes 1327112 | tf_op jit(solution)/shard_map/ppermute | solution.py:395
  47.1 13.9 %collective-permute-start.12 = (bf16[96,768]{1,0:T(8,128)(2,1)}, bf16[96,768]{1,0:T(8,128)(2,1)S(1)}, u32[]{:S(2)}, u32[]{:S(2)}) collective-permute-start(bf16[96,768]{1,0:T(8,128)(2,1)} %constant_dynamic-slice_fusion.6), channel_id=1, source_target_pairs={{0,2},{1,3},{2,0},{3,1},{4,6},{5,7},{6,4},{7,5},{8,10},{9,11},{10,... | collective-permute-start | bytes 442376 | tf_op jit(solution)/shard_map/ppermute | solution.py:381
  63.6 29.0 %collective-permute-start.14 = (bf16[192,768]{1,0:T(8,128)(2,1)S(1)}, bf16[192,768]{1,0:T(8,128)(2,1)S(1)}, u32[]{:S(2)}, u32[]{:S(2)}) collective-permute-start(bf16[192,768]{1,0:T(8,128)(2,1)S(1)} %copy-done.30), channel_id=1, source_target_pairs={{0,1},{1,0},{2,3},{3,2},{4,5},{5,4},{6,7},{7,6},{8,9},{9,8},{10,11... | collective-permute-start | bytes 884744 | tf_op jit(solution)/shard_map/ppermute | solution.py:382
  63.6 30.2 %collective-permute-start.15 = (bf16[96,768]{1,0:T(8,128)(2,1)S(1)}, bf16[96,768]{1,0:T(8,128)(2,1)S(1)}, u32[]{:S(2)}, u32[]{:S(2)}) collective-permute-start(bf16[96,768]{1,0:T(8,128)(2,1)S(1)} %collective-permute-done.12.near), channel_id=1, source_target_pairs={{0,1},{1,0},{2,3},{3,2},{4,5},{5,4},{6,7},{7,6},{8,9},{9,8},{10,11... | collective-permute-start | bytes 442376 | tf_op jit(solution)/shard_map/ppermute | solution.py:395
  66.6 27.4 %collective-permute-start.16 = (bf16[96,768]{1,0:T(8,128)(2,1)S(1)}, bf16[96,768]{1,0:T(8,128)(2,1)S(1)}, u32[]{:S(2)}, u32[]{:S(2)}) collective-permute-start(bf16[96,768]{1,0:T(8,128)(2,1)S(1)} %collective-permute-done.13.far), channel_id=1, source_target_pairs={{0,1},{1,0},{2,3},{3,2},{4,5},{5,4},{6,7},{7,6},{8,9},{9,8},{10,11... | collective-permute-start | bytes 442376 | tf_op jit(solution)/shard_map/ppermute | solution.py:396
  70.8 76.2 %collective-permute-start.24 = (bf16[192,3072]{1,0:T(8,128)(2,1)}, bf16[192,3072]{1,0:T(8,128)(2,1)}, u32[]{:S(2)}, u32[]{:S(2)}) collective-permute-start(bf16[192,3072]{1,0:T(8,128)(2,1)} %own.5), channel_id=1, source_target_pairs={{0,1},{1,0},{2,3},{3,2},{4,5},{5,4},{6,7},{7,6},{8,9},{9,8},{10,11... | collective-permute-start | bytes 3538952 | tf_op jit(solution)/shard_map/ppermute | solution.py:382
  71.3 39.9 %collective-permute-start.19 = (bf16[768,768]{1,0:T(8,128)(2,1)}, bf16[768,768]{1,0:T(8,128)(2,1)}, u32[]{:S(2)}, u32[]{:S(2)}) collective-permute-start(bf16[768,768]{1,0:T(8,128)(2,1)} %own.4), channel_id=1, source_target_pairs={{0,1},{1,0},{2,3},{3,2},{4,5},{5,4},{6,7},{7,6},{8,9},{9,8},{10,11... | collective-permute-start | bytes 3538952 | tf_op jit(solution)/shard_map/ppermute | solution.py:382
  92.6 16.6 %collective-permute-start.18 = (bf16[384,768]{1,0:T(8,128)(2,1)}, bf16[384,768]{1,0:T(8,128)(2,1)}, u32[]{:S(2)}, u32[]{:S(2)}) collective-permute-start(bf16[384,768]{1,0:T(8,128)(2,1)} %collective-permute-done.17.near), channel_id=1, source_target_pairs={{0,4},{4,0},{8,12},{12,8},{16,20},{20,16},{24,28},{28,24},{1,5},{5... | collective-permute-start | bytes 1769480 | tf_op jit(solution)/shard_map/ppermute | solution.py:394
  93.8 17.4 %collective-permute-start.20 = (bf16[384,768]{1,0:T(8,128)(2,1)}, bf16[384,768]{1,0:T(8,128)(2,1)}, u32[]{:S(2)}, u32[]{:S(2)}) collective-permute-start(bf16[384,768]{1,0:T(8,128)(2,1)} %collective-permute-done.17.near), channel_id=1, source_target_pairs={{0,1},{1,0},{2,3},{3,2},{4,5},{5,4},{6,7},{7,6},{8,9},{9,8},{10,11... | collective-permute-start | bytes 1769480 | tf_op jit(solution)/shard_map/ppermute | solution.py:395
  94.0 52.8 %collective-permute-start.23 = (bf16[96,3072]{1,0:T(8,128)(2,1)}, bf16[96,3072]{1,0:T(8,128)(2,1)S(1)}, u32[]{:S(2)}, u32[]{:S(2)}) collective-permute-start(bf16[96,3072]{1,0:T(8,128)(2,1)} %collective-permute-done.22.near), channel_id=1, source_target_pairs={{0,4},{4,0},{8,12},{12,8},{16,20},{20,16},{24,28},{28,24},{1,5},{5... | collective-permute-start | bytes 1769480 | tf_op jit(solution)/shard_map/ppermute | solution.py:394
  146.2 20.9 %collective-permute-start.27 = (bf16[2,192,3072]{2,1,0:T(8,128)(2,1)}, bf16[2,192,3072]{2,1,0:T(8,128)(2,1)}, u32[]{:S(2)}, u32[]{:S(2)}) collective-permute-start(bf16[2,192,3072]{2,1,0:T(8,128)(2,1)} %dynamic-slice_bitcast_fusion.2), channel_id=1, source_target_pairs={{0,1},{1,0},{2,3},{3,2},{4,5},{5,4},{6,7},{7,6},{8,9},{9,8},{10,11... | collective-permute-start | bytes 7077896 | tf_op jit(solution)/shard_map/ppermute | solution.py:105
  146.8 6.0 %collective-permute-start.26 = (bf16[96,3072]{1,0:T(8,128)(2,1)S(1)}, bf16[96,3072]{1,0:T(8,128)(2,1)}, u32[]{:S(2)}, u32[]{:S(2)}) collective-permute-start(bf16[96,3072]{1,0:T(8,128)(2,1)S(1)} %collective-permute-done.23.far), channel_id=1, source_target_pairs={{0,1},{1,0},{2,3},{3,2},{4,5},{5,4},{6,7},{7,6},{8,9},{9,8},{10,11... | collective-permute-start | bytes 1769480 | tf_op jit(solution)/shard_map/ppermute | solution.py:396
  192.5 33.4 %collective-permute-start.30 = (bf16[2,960,768]{2,1,0:T(8,128)(2,1)}, bf16[2,960,768]{2,1,0:T(8,128)(2,1)}, u32[]{:S(2)}, u32[]{:S(2)}) collective-permute-start(bf16[2,960,768]{2,1,0:T(8,128)(2,1)} %pad_maximum_fusion), channel_id=1, source_target_pairs={{0,1},{1,0},{2,3},{3,2},{4,5},{5,4},{6,7},{7,6},{8,9},{9,8},{10,11... | collective-permute-start | bytes 8847368 | tf_op jit(solution)/shard_map/ppermute | solution.py:105
  192.7 28.5 %collective-permute-start.28 = (bf16[1,192,3072]{2,1,0:T(8,128)(2,1)}, bf16[1,192,3072]{2,1,0:T(8,128)(2,1)}, u32[]{:S(2)}, u32[]{:S(2)}) collective-permute-start(bf16[1,192,3072]{2,1,0:T(8,128)(2,1)} %constant_dynamic-slice_fusion.3), channel_id=1, source_target_pairs={{0,2},{1,3},{2,0},{3,1},{4,6},{5,7},{6,4},{7,5},{8,10},{9,11},{10,... | collective-permute-start | bytes 3538952 | tf_op jit(solution)/shard_map/ppermute | solution.py:105
  224.7 22.2 %collective-permute-start.29 = (bf16[1,96,3072]{2,1,0:T(8,128)(2,1)}, bf16[1,96,3072]{2,1,0:T(8,128)(2,1)}, u32[]{:S(2)}, u32[]{:S(2)}) collective-permute-start(bf16[1,96,3072]{2,1,0:T(8,128)(2,1)} %dynamic-slice_bitcast_fusion.7), channel_id=1, source_target_pairs={{0,4},{4,0},{8,12},{12,8},{16,20},{20,16},{24,28},{28,24},{1,5},{5... | collective-permute-start | bytes 1769480 | tf_op jit(solution)/shard_map/ppermute | solution.py:105
  232.0 36.1 %collective-permute-start.32 = (bf16[1,960,768]{2,1,0:T(8,128)(2,1)}, bf16[1,960,768]{2,1,0:T(8,128)(2,1)}, u32[]{:S(2)}, u32[]{:S(2)}) collective-permute-start(bf16[1,960,768]{2,1,0:T(8,128)(2,1)} %constant_dynamic-slice_fusion.2), channel_id=1, source_target_pairs={{0,2},{1,3},{2,0},{3,1},{4,6},{5,7},{6,4},{7,5},{8,10},{9,11},{10,... | collective-permute-start | bytes 4423688 | tf_op jit(solution)/shard_map/ppermute | solution.py:105
  249.1 14.7 %collective-permute-start.31 = (bf16[1,48,3072]{2,1,0:T(8,128)(2,1)}, bf16[1,48,3072]{2,1,0:T(8,128)(2,1)}, u32[]{:S(2)}, u32[]{:S(2)}) collective-permute-start(bf16[1,48,3072]{2,1,0:T(8,128)(2,1)} %dynamic-slice_bitcast_fusion.11), channel_id=1, source_target_pairs={{0,8},{4,12},{8,0},{12,4},{16,24},{20,28},{24,16},{28,20},{1,9},{5... | collective-permute-start | bytes 884744 | tf_op jit(solution)/shard_map/ppermute | solution.py:105
  265.5 25.2 %collective-permute-start.33 = (bf16[1,48,3072]{2,1,0:T(8,128)(2,1)}, bf16[1,48,3072]{2,1,0:T(8,128)(2,1)}, u32[]{:S(2)}, u32[]{:S(2)}) collective-permute-start(bf16[1,48,3072]{2,1,0:T(8,128)(2,1)} %fusion.13), channel_id=1, source_target_pairs={{0,16},{4,20},{8,24},{12,28},{16,0},{20,4},{24,8},{28,12},{1,17},{... | collective-permute-start | bytes 884744 | tf_op jit(solution)/shard_map/ppermute | solution.py:105
  272.3 20.2 %collective-permute-start.34 = (bf16[1,480,768]{2,1,0:T(8,128)(2,1)}, bf16[1,480,768]{2,1,0:T(8,128)(2,1)S(1)}, u32[]{:S(2)}, u32[]{:S(2)}) collective-permute-start(bf16[1,480,768]{2,1,0:T(8,128)(2,1)} %dynamic-slice_bitcast_fusion.4), channel_id=1, source_target_pairs={{0,4},{4,0},{8,12},{12,8},{16,20},{20,16},{24,28},{28,24},{1,5},{5... | collective-permute-start | bytes 2211848 | tf_op jit(solution)/shard_map/ppermute | solution.py:105
  292.0 11.6 %collective-permute-start.36 = (bf16[1,48,3072]{2,1,0:T(8,128)(2,1)S(1)}, bf16[1,48,3072]{2,1,0:T(8,128)(2,1)S(1)}, u32[]{:S(2)}, u32[]{:S(2)}) collective-permute-start(bf16[1,48,3072]{2,1,0:T(8,128)(2,1)S(1)} %add_convert_fusion.10), channel_id=1, source_target_pairs={{0,8},{4,12},{8,0},{12,4},{16,24},{20,28},{24,16},{28,20},{1,9},{5... | collective-permute-start | bytes 884744 | tf_op jit(solution)/shard_map/ppermute | solution.py:105
  293.8 13.3 %collective-permute-start.35 = (bf16[1,240,768]{2,1,0:T(8,128)(2,1)S(1)}, bf16[1,240,768]{2,1,0:T(8,128)(2,1)S(1)}, u32[]{:S(2)}, u32[]{:S(2)}) collective-permute-start(bf16[1,240,768]{2,1,0:T(8,128)(2,1)S(1)} %dynamic-slice_bitcast_fusion.9), channel_id=1, source_target_pairs={{0,8},{4,12},{8,0},{12,4},{16,24},{20,28},{24,16},{28,20},{1,9},{5... | collective-permute-start | bytes 1105928 | tf_op jit(solution)/shard_map/ppermute | solution.py:105
  303.7 7.5 %collective-permute-start.37 = (bf16[2,576,768]{2,1,0:T(8,128)(2,1)S(1)}, bf16[2,576,768]{2,1,0:T(8,128)(2,1)S(1)}, u32[]{:S(2)}, u32[]{:S(2)}) collective-permute-start(bf16[2,576,768]{2,1,0:T(8,128)(2,1)S(1)} %dynamic-slice_bitcast_fusion.3), channel_id=1, source_target_pairs={{0,1},{1,0},{2,3},{3,2},{4,5},{5,4},{6,7},{7,6},{8,9},{9,8},{10,11... | collective-permute-start | bytes 5308424 | tf_op jit(solution)/shard_map/ppermute | solution.py:105
  304.7 53.0 %collective-permute-start.54 = (bf16[1,96,3072]{2,1,0:T(8,128)(2,1)}, bf16[1,96,3072]{2,1,0:T(8,128)(2,1)}, u32[]{:S(2)}, u32[]{:S(2)}) collective-permute-start(bf16[1,96,3072]{2,1,0:T(8,128)(2,1)} %maximum_select_fusion.6), channel_id=1, source_target_pairs={{0,4},{4,0},{8,12},{12,8},{16,20},{20,16},{24,28},{28,24},{1,5},{5... | collective-permute-start | bytes 1769480 | tf_op jit(solution)/shard_map/ppermute | solution.py:105
  307.3 19.4 %collective-permute-start.38 = (bf16[1,240,768]{2,1,0:T(8,128)(2,1)S(1)}, bf16[1,240,768]{2,1,0:T(8,128)(2,1)S(1)}, u32[]{:S(2)}, u32[]{:S(2)}) collective-permute-start(bf16[1,240,768]{2,1,0:T(8,128)(2,1)S(1)} %fusion.11), channel_id=1, source_target_pairs={{0,16},{4,20},{8,24},{12,28},{16,0},{20,4},{24,8},{28,12},{1,17},{... | collective-permute-start | bytes 1105928 | tf_op jit(solution)/shard_map/ppermute | solution.py:105
  326.8 10.7 %collective-permute-start.40 = (bf16[1,240,768]{2,1,0:T(8,128)(2,1)S(1)}, bf16[1,240,768]{2,1,0:T(8,128)(2,1)}, u32[]{:S(2)}, u32[]{:S(2)}) collective-permute-start(bf16[1,240,768]{2,1,0:T(8,128)(2,1)S(1)} %add_convert_fusion.9), channel_id=1, source_target_pairs={{0,8},{4,12},{8,0},{12,4},{16,24},{20,28},{24,16},{28,20},{1,9},{5... | collective-permute-start | bytes 1105928 | tf_op jit(solution)/shard_map/ppermute | solution.py:105
  326.9 22.0 %collective-permute-start.41 = (bf16[1,576,768]{2,1,0:T(8,128)(2,1)}, bf16[1,576,768]{2,1,0:T(8,128)(2,1)}, u32[]{:S(2)}, u32[]{:S(2)}) collective-permute-start(bf16[1,576,768]{2,1,0:T(8,128)(2,1)} %constant_dynamic-slice_fusion.1), channel_id=1, source_target_pairs={{0,2},{1,3},{2,0},{3,1},{4,6},{5,7},{6,4},{7,5},{8,10},{9,11},{10,... | collective-permute-start | bytes 2654216 | tf_op jit(solution)/shard_map/ppermute | solution.py:105
  333.6 17.3 %collective-permute-start.39 = (bf16[2,192,1664]{2,1,0:T(8,128)(2,1)S(1)}, bf16[2,192,1664]{2,1,0:T(8,128)(2,1)S(1)}, u32[]{:S(2)}, u32[]{:S(2)}) collective-permute-start(bf16[2,192,1664]{2,1,0:T(8,128)(2,1)S(1)} %fusion.6), channel_id=1, source_target_pairs={{0,1},{1,0},{2,3},{3,2},{4,5},{5,4},{6,7},{7,6},{8,9},{9,8},{10,11... | collective-permute-start | bytes 3833864 | tf_op jit(solution)/shard_map/ppermute | solution.py:105
  338.8 32.5 %collective-permute-start.53 = (bf16[1,480,768]{2,1,0:T(8,128)(2,1)S(1)}, bf16[1,480,768]{2,1,0:T(8,128)(2,1)S(1)}, u32[]{:S(2)}, u32[]{:S(2)}) collective-permute-start(bf16[1,480,768]{2,1,0:T(8,128)(2,1)S(1)} %maximum_select_fusion.3), channel_id=1, source_target_pairs={{0,4},{4,0},{8,12},{12,8},{16,20},{20,16},{24,28},{28,24},{1,5},{5... | collective-permute-start | bytes 2211848 | tf_op jit(solution)/shard_map/ppermute | solution.py:105
  350.3 15.6 %collective-permute-start.44 = (bf16[1,288,768]{2,1,0:T(8,128)(2,1)S(1)}, bf16[1,288,768]{2,1,0:T(8,128)(2,1)S(1)}, u32[]{:S(2)}, u32[]{:S(2)}) collective-permute-start(bf16[1,288,768]{2,1,0:T(8,128)(2,1)S(1)} %dynamic-slice_bitcast_fusion.8), channel_id=1, source_target_pairs={{0,4},{4,0},{8,12},{12,8},{16,20},{20,16},{24,28},{28,24},{1,5},{5... | collective-permute-start | bytes 1327112 | tf_op jit(solution)/shard_map/ppermute | solution.py:105
  351.3 15.4 %collective-permute-start.42 = (bf16[1,192,1664]{2,1,0:T(8,128)(2,1)S(1)}, bf16[1,192,1664]{2,1,0:T(8,128)(2,1)S(1)}, u32[]{:S(2)}, u32[]{:S(2)}) collective-permute-start(bf16[1,192,1664]{2,1,0:T(8,128)(2,1)S(1)} %constant_dynamic-slice_fusion), channel_id=1, source_target_pairs={{0,2},{1,3},{2,0},{3,1},{4,6},{5,7},{6,4},{7,5},{8,10},{9,11},{10,... | collective-permute-start | bytes 1916936 | tf_op jit(solution)/shard_map/ppermute | solution.py:105
  367.0 7.8 %collective-permute-start.43 = (bf16[1,96,1664]{2,1,0:T(8,128)(2,1)S(1)}, bf16[1,96,1664]{2,1,0:T(8,128)(2,1)S(1)}, u32[]{:S(2)}, u32[]{:S(2)}) collective-permute-start(bf16[1,96,1664]{2,1,0:T(8,128)(2,1)S(1)} %dynamic-slice_bitcast_fusion.10), channel_id=1, source_target_pairs={{0,4},{4,0},{8,12},{12,8},{16,20},{20,16},{24,28},{28,24},{1,5},{5... | collective-permute-start | bytes 958472 | tf_op jit(solution)/shard_map/ppermute | solution.py:105
  372.2 10.3 %collective-permute-start.48 = (bf16[1,144,768]{2,1,0:T(8,128)(2,1)S(1)}, bf16[1,144,768]{2,1,0:T(8,128)(2,1)S(1)}, u32[]{:S(2)}, u32[]{:S(2)}) collective-permute-start(bf16[1,144,768]{2,1,0:T(8,128)(2,1)S(1)} %fusion.18), channel_id=1, source_target_pairs={{0,16},{4,20},{8,24},{12,28},{16,0},{20,4},{24,8},{28,12},{1,17},{... | collective-permute-start | bytes 663560 | tf_op jit(solution)/shard_map/ppermute | solution.py:105
  374.9 7.7 %collective-permute-start.45 = (bf16[1,48,1664]{2,1,0:T(8,128)(2,1)S(1)}, bf16[1,48,1664]{2,1,0:T(8,128)(2,1)S(1)}, u32[]{:S(2)}, u32[]{:S(2)}) collective-permute-start(bf16[1,48,1664]{2,1,0:T(8,128)(2,1)S(1)} %dynamic-slice_bitcast_fusion.13), channel_id=1, source_target_pairs={{0,8},{4,12},{8,0},{12,4},{16,24},{20,28},{24,16},{28,20},{1,9},{5... | collective-permute-start | bytes 479240 | tf_op jit(solution)/shard_map/ppermute | solution.py:105
  382.5 9.4 %collective-permute-start.51 = (bf16[1,144,768]{2,1,0:T(8,128)(2,1)S(1)}, bf16[1,144,768]{2,1,0:T(8,128)(2,1)S(1)}, u32[]{:S(2)}, u32[]{:S(2)}) collective-permute-start(bf16[1,144,768]{2,1,0:T(8,128)(2,1)S(1)} %add_convert_fusion.11), channel_id=1, source_target_pairs={{0,8},{4,12},{8,0},{12,4},{16,24},{20,28},{24,16},{28,20},{1,9},{5... | collective-permute-start | bytes 663560 | tf_op jit(solution)/shard_map/ppermute | solution.py:105
  382.7 9.3 %collective-permute-start.47 = (bf16[1,48,1664]{2,1,0:T(8,128)(2,1)S(1)}, bf16[1,48,1664]{2,1,0:T(8,128)(2,1)S(1)}, u32[]{:S(2)}, u32[]{:S(2)}) collective-permute-start(bf16[1,48,1664]{2,1,0:T(8,128)(2,1)S(1)} %fusion.19), channel_id=1, source_target_pairs={{0,16},{4,20},{8,24},{12,28},{16,0},{20,4},{24,8},{28,12},{1,17},{... | collective-permute-start | bytes 479240 | tf_op jit(solution)/shard_map/ppermute | solution.py:105
  392.9 13.1 %collective-permute-start.52 = (bf16[1,288,768]{2,1,0:T(8,128)(2,1)S(1)}, bf16[1,288,768]{2,1,0:T(8,128)(2,1)S(1)}, u32[]{:S(2)}, u32[]{:S(2)}) collective-permute-start(bf16[1,288,768]{2,1,0:T(8,128)(2,1)S(1)} %maximum_select_fusion.9), channel_id=1, source_target_pairs={{0,4},{4,0},{8,12},{12,8},{16,20},{20,16},{24,28},{28,24},{1,5},{5... | collective-permute-start | bytes 1327112 | tf_op jit(solution)/shard_map/ppermute | solution.py:105
  397.4 13.4 %collective-permute-start.50 = (bf16[1,96,1664]{2,1,0:T(8,128)(2,1)S(1)}, bf16[1,96,1664]{2,1,0:T(8,128)(2,1)S(1)}, u32[]{:S(2)}, u32[]{:S(2)}) collective-permute-start(bf16[1,96,1664]{2,1,0:T(8,128)(2,1)S(1)} %maximum_select_fusion.11), channel_id=1, source_target_pairs={{0,4},{4,0},{8,12},{12,8},{16,20},{20,16},{24,28},{28,24},{1,5},{5... | collective-permute-start | bytes 958472 | tf_op jit(solution)/shard_map/ppermute | solution.py:105
  (76 other events, 566.4 us)
